TPU v7x, 32 devices: a whole 2x2x4 slice. The times are simulated.
32 devices in a mesh: wave: 4 (over z), tile: 8 (over y, x, core).
Axes of the slice: x: 2, y: 2, z: 4, core: 2. Of those that a mesh axis runs over, the one named last changes fastest.
Arguments:
- warm_start: float32 [4, 2, 256, 1024], P('wave', None, 'tile'), may hold values from -30 to 30
- class_map: int32 [256, 1024], P('tile'), may hold values from 0 to 7
- conductivities: float32 [8], replicated, may hold values from 0.1 to 10
- wavenumbers: float32 [4], P('wave'), may hold values from 0.05 to 2
- weights: float32 [4], P('wave'), may hold values from 0.1 to 1
- source_row: int32 [2], replicated, may hold values from 0 to 255
- source_col: int32 [2], replicated, may hold values from 0 to 1023
- electrode_row: int32 [64], replicated, may hold values from 0 to 255
Outputs:
- potentials: float32 [2, 256, 1024], P(None, 'tile', 'wave')
- readings: float32 [2, 64], replicated
All inputs are finite; a program needn't handle non-finite values.
Results may differ from a plain program's by a relative error of at most 0.0003.
Values sent between devices are 32-bit elements; how exact they have to be, the bound alone decides.
No kernel may reach another device: no remote copies, remote signals or barrier semaphores. Data moves between devices by JAX's collectives and lax.ppermute only.
A program may use at most 64 MiB of HBM per device.

v0:
```python
import jax
import jax.numpy as jnp
from jax import lax
from jax.sharding import PartitionSpec as P

ITERS = 3


source_strength = 50.0


def extended(shard, sides, width):
    for axis, dim in sides:
        size, length = (lax.axis_size(axis), shard.shape[dim])
        up = [(i, (i + 1) % size) for i in range(size - 1)]
        down = [(j, i) for i, j in up]
        last = lax.slice_in_dim(shard, length - width, length, axis=dim)
        initial = lax.slice_in_dim(shard, 0, width, axis=dim)
        before = lax.ppermute(last, axis, up)
        after = lax.ppermute(initial, axis, down)
        shard = jnp.concatenate([before, shard, after], axis=dim)
    return shard


def harmonic(left_val, right_val):
    return 2.0 * left_val * right_val / (left_val + right_val)


def shards(
    warm_start,
    class_map,
    conductivities,
    wavenumbers,
    weights,
    source_row,
    source_col,
    electrode_row,
):
    rows_here = class_map.shape[0]
    depth = class_map.shape[1]
    n_class = conductivities.shape[0]
    class_ids = jnp.arange(n_class, dtype=jnp.int32)
    sigma = jnp.sum(
        jnp.where(class_map[None] == class_ids[:, None, None], conductivities[:, None, None], 0.0),
        axis=0,
    )
    sigma_rim = extended(sigma, (("tile", 0),), 1)
    face_row = harmonic(sigma_rim[:-1], sigma_rim[1:])
    face_up = face_row[:-1]
    face_down = face_row[1:]
    col_inner = harmonic(sigma[:, :-1], sigma[:, 1:])
    face_left = jnp.concatenate([jnp.zeros((rows_here, 1), jnp.float32), col_inner], axis=1)
    face_right = jnp.concatenate([col_inner, sigma[:, -1:]], axis=1)
    base = face_up + face_down + face_left + face_right
    wave_num = wavenumbers[0]
    diag = base + wave_num * wave_num * sigma
    global_row = lax.axis_index("tile") * rows_here + jnp.arange(rows_here, dtype=jnp.int32)
    col_ids = jnp.arange(depth, dtype=jnp.int32)
    hits = (global_row[None, :, None] == source_row[:, None, None]) & (
        col_ids[None, None, :] == source_col[:, None, None]
    )
    rhs = source_strength * hits.astype(jnp.float32)

    def operate(values):
        row_padded = extended(values, (("tile", 1),), 1)
        col_padded = jnp.pad(values, ((0, 0), (0, 0), (1, 1)))
        return (
            diag * values
            - face_up * row_padded[:, :-2]
            - face_down * row_padded[:, 2:]
            - face_left * col_padded[:, :, :-2]
            - face_right * col_padded[:, :, 2:]
        )

    def local_inner(first, second):
        return jnp.sum(first * second, axis=(1, 2))

    def paired_inner(residual, scaled, image):
        totals = lax.psum((local_inner(residual, scaled), local_inner(scaled, image)), "tile")
        return (totals[0][:, None, None], totals[1][:, None, None])

    field = warm_start[0]
    residual = rhs - operate(field)
    scaled = residual / diag
    image = operate(scaled)
    gamma_now, delta = paired_inner(residual, scaled, image)
    step_size = gamma_now / delta
    direction = scaled
    along = image
    for iteration in range(ITERS):
        field = field + step_size * direction
        residual = residual - step_size * along
        if iteration + 1 < ITERS:
            scaled = residual / diag
            image = operate(scaled)
            gamma_next, delta = paired_inner(residual, scaled, image)
            ratio = gamma_next / gamma_now
            step_size = gamma_next / (delta - ratio * gamma_next / step_size)
            direction = scaled + ratio * direction
            along = image + ratio * along
            gamma_now = gamma_next
    weighted = weights[0] * field
    picker = (global_row[:, None] == electrode_row[None, :]).astype(jnp.float32)
    local_read = jnp.dot(
        weighted[:, :, 0],
        picker,
        precision=lax.Precision.HIGHEST,
        preferred_element_type=jnp.float32,
    )
    readings = lax.psum(local_read, ("wave", "tile"))
    summed = lax.psum(weighted, "wave")
    share = depth // lax.axis_size("wave")
    potentials = lax.dynamic_slice_in_dim(summed, lax.axis_index("wave") * share, share, 2)
    return (potentials, readings)


def solution(mesh):
    return jax.shard_map(
        shards,
        mesh=mesh,
        in_specs=(
            P("wave", None, "tile", None),
            P("tile", None),
            P(),
            P("wave"),
            P("wave"),
            P(),
            P(),
            P(),
        ),
        out_specs=(P(None, "tile", "wave"), P()),
        check_vma=False,
    )
```

profile of v0, /device:TPU:0, one launch (start us, length us, event | category | flops | bytes accessed | tf_op | source)
XLA Modules:
  0.0 142.7 jit_solution(10062995392235337752)
XLA Ops:
  7.2 0.0 copy-start.1
  7.2 1.1 select_reduce_fusion
  8.3 2.4 %collective-permute-start = (f32[1,1024]{1,0:T(1,128)S(1)}, f32[1,1024]{1,0:T(1,128)S(1)}, u32[]{:S(2)}, u32[]{:S(2)}) collective-permute-start(f32[1,1024]{1,0:T(1,128)S(1)} %get-tuple-element.38), channel_id=1, source_target_pairs={{0,1},{1,2},{2,3},{3,4},{4,5},{5,6},{6,7},{8,9},{9,10},{10,11},{11... | collective-permute-start | bytes 12296 | tf_op jit(solution)/shard_map/ppermute | solution.py:19
  10.7 1.3 collective-permute-start.1
  12.1 5.1 %collective-permute-start.2 = (f32[2,1,1024]{2,1,0:T(1,128)S(1)}, f32[2,1,1024]{2,1,0:T(1,128)S(1)}, u32[]{:S(2)}, u32[]{:S(2)}) collective-permute-start(f32[2,1,1024]{2,1,0:T(1,128)S(1)} %get-tuple-element.33), channel_id=1, source_target_pairs={{0,1},{1,2},{2,3},{3,4},{4,5},{5,6},{6,7},{8,9},{9,10},{10,11},{11... | collective-permute-start | bytes 24584 | tf_op jit(solution)/shard_map/ppermute | solution.py:19
  17.2 1.3 collective-permute-start.3
  18.5 0.1 add_divide_fusion.1
  18.6 0.0 copy-start.2
  18.7 0.6 copy-done.2
  19.3 0.1 iota_compare_fusion.1
  19.4 0.6 copy-done.3
  19.9 0.1 broadcast_compare_fusion
  20.0 0.1 slice.146
  20.7 0.0 collective-permute-done
  20.8 0.0 collective-permute-done.1
  20.8 0.1 multiply_add_fusion
  20.9 0.0 collective-permute-done.2
  21.0 0.6 collective-permute-done.3
  21.5 0.2 broadcast_divide_fusion.2
  21.8 4.3 %collective-permute-start.4 = (f32[2,1,1024]{2,1,0:T(1,128)S(1)}, f32[2,1,1024]{2,1,0:T(1,128)S(1)}, u32[]{:S(2)}, u32[]{:S(2)}) collective-permute-start(f32[2,1,1024]{2,1,0:T(1,128)S(1)} %get-tuple-element.31), channel_id=1, source_target_pairs={{0,1},{1,2},{2,3},{3,4},{4,5},{5,6},{6,7},{8,9},{9,10},{10,11},{11... | collective-permute-start | bytes 24584 | tf_op jit(solution)/shard_map/ppermute | solution.py:19
  26.1 1.3 collective-permute-start.5
  27.4 0.0 collective-permute-done.4
  27.4 2.4 %collective-permute-done.5 = f32[2,1,1024]{2,1,0:T(1,128)S(1)} collective-permute-done((f32[2,1,1024]{2,1,0:T(1,128)S(1)}, f32[2,1,1024]{2,1,0:T(1,128)S(1)}, u32[]{:S(2)}, u32[]{:S(2)}) %collective-permute-start.5) | collective-permute-done | bytes 8224 | tf_op jit(solution)/shard_map/ppermute | solution.py:20
  29.8 0.3 multiply_reduce_fusion.3
  30.1 15.5 %all-reduce.7 = (f32[2]{0:T(128)S(1)}, f32[2]{0:T(128)S(1)}) all-reduce(f32[2]{0:T(128)S(1)} %get-tuple-element.5, f32[2]{0:T(128)S(1)} %get-tuple-element.4), channel_id=1, replica_groups=mesh['wave'=4,'tile'=8] {'tile'}, use_global_device_ids=true, to_apply=%region_2.3 | all-reduce | flops 4 | bytes 32 | tf_op jit(solution)/shard_map/psum | solution.py:79
  45.6 0.1 broadcast_divide_fusion.1
  45.7 1.3 collective-permute-start.6
  47.0 1.3 collective-permute-start.7
  48.3 0.0 collective-permute-done.6
  48.3 3.4 %collective-permute-done.7 = f32[2,1,1024]{2,1,0:T(1,128)S(1)} collective-permute-done((f32[2,1,1024]{2,1,0:T(1,128)S(1)}, f32[2,1,1024]{2,1,0:T(1,128)S(1)}, u32[]{:S(2)}, u32[]{:S(2)}) %collective-permute-start.7) | collective-permute-done | bytes 8224 | tf_op jit(solution)/shard_map/ppermute | solution.py:20
  51.7 0.3 multiply_reduce_fusion.1
  52.0 16.0 %all-reduce.6 = (f32[2]{0:T(128)S(1)}, f32[2]{0:T(128)S(1)}) all-reduce(f32[2]{0:T(128)S(1)} %get-tuple-element.3, f32[2]{0:T(128)S(1)} %get-tuple-element.2), channel_id=1, replica_groups=mesh['wave'=4,'tile'=8] {'tile'}, use_global_device_ids=true, to_apply=%region_6.7 | all-reduce | flops 4 | bytes 32 | tf_op jit(solution)/shard_map/psum | solution.py:79
  68.0 0.1 broadcast_divide_fusion
  68.2 1.4 collective-permute-start.8
  69.6 1.3 collective-permute-start.9
  71.5 0.0 collective-permute-done.8
  71.5 2.9 %collective-permute-done.9 = f32[2,1,1024]{2,1,0:T(1,128)S(1)} collective-permute-done((f32[2,1,1024]{2,1,0:T(1,128)S(1)}, f32[2,1,1024]{2,1,0:T(1,128)S(1)}, u32[]{:S(2)}, u32[]{:S(2)}) %collective-permute-start.9) | collective-permute-done | bytes 8224 | tf_op jit(solution)/shard_map/ppermute | solution.py:20
  74.4 0.3 fusion.17
  74.7 16.0 %all-reduce.5 = (f32[2]{0:T(128)S(1)}, f32[2]{0:T(128)S(1)}) all-reduce(f32[2]{0:T(128)S(1)} %get-tuple-element.7, f32[2]{0:T(128)S(1)} %get-tuple-element.6), channel_id=1, replica_groups=mesh['wave'=4,'tile'=8] {'tile'}, use_global_device_ids=true, to_apply=%region_10.11 | all-reduce | flops 4 | bytes 32 | tf_op jit(solution)/shard_map/psum | solution.py:79
  90.7 0.2 add_multiply_fusion
  90.9 0.1 slice_reduce_fusion
  91.0 0.6 copy-done
  91.6 0.1 all-reduce.10.cloned.1.call-update
  91.7 0.0 copy-start.4
  91.7 0.6 copy-done.4
  92.4 0.2 fusion.35
  92.6 41.8 %psum.63 = f32[2,64]{1,0:T(2,128)} all-reduce(f32[2,64]{1,0:T(2,128)S(1)} %fusion.35), channel_id=1, replica_groups=mesh['wave'=4,'tile'=8] {'wave','tile'}, use_global_device_ids=true, to_apply=%region_14.15 | all-reduce | flops 128 | bytes 1024 | tf_op jit(solution)/shard_map/psum | solution.py:110
  134.3 1.5 %constant_dynamic-slice_fusion = f32[2,32,256]{2,1,0:T(8,128)} fusion(f32[2,32,1024]{2,1,0:T(8,128)} %all-reduce.10.cloned.1.call-done, s32[]{:T(128)S(6)} %select_n.8), kind=kLoop, calls=%fused_computation.80 | loop fusion | bytes 131076 | tf_op jit(solution)/shard_map/dynamic_slice | solution.py:113
  (15 shorter events, 0.2 us)
Async XLA Ops:
  7.2 4.9 %copy-start.1 = (f32[1,2,32,1024]{3,2,1,0:T(8,128)S(1)}, f32[1,2,32,1024]{3,2,1,0:T(8,128)}, u32[]{:S(2)}) copy-start(f32[1,2,32,1024]{3,2,1,0:T(8,128)} %param.8) | copy-start | bytes 786436
  8.3 12.4 %collective-permute-start = (f32[1,1024]{1,0:T(1,128)S(1)}, f32[1,1024]{1,0:T(1,128)S(1)}, u32[]{:S(2)}, u32[]{:S(2)}) collective-permute-start(f32[1,1024]{1,0:T(1,128)S(1)} %get-tuple-element.38), channel_id=1, source_target_pairs={{0,1},{1,2},{2,3},{3,4},{4,5},{5,6},{6,7},{8,9},{9,10},{10,11},{11... | collective-permute-start | bytes 12296 | tf_op jit(solution)/shard_map/ppermute | solution.py:19
  10.7 10.0 %collective-permute-start.1 = (f32[1,1024]{1,0:T(1,128)S(1)}, f32[1,1024]{1,0:T(1,128)S(1)}, u32[]{:S(2)}, u32[]{:S(2)}) collective-permute-start(f32[1,1024]{1,0:T(1,128)S(1)} %get-tuple-element.39), channel_id=1, source_target_pairs={{1,0},{2,1},{3,2},{4,3},{5,4},{6,5},{7,6},{9,8},{10,9},{11,10},{12... | collective-permute-start | bytes 12296 | tf_op jit(solution)/shard_map/ppermute | solution.py:20
  12.1 8.9 %collective-permute-start.2 = (f32[2,1,1024]{2,1,0:T(1,128)S(1)}, f32[2,1,1024]{2,1,0:T(1,128)S(1)}, u32[]{:S(2)}, u32[]{:S(2)}) collective-permute-start(f32[2,1,1024]{2,1,0:T(1,128)S(1)} %get-tuple-element.33), channel_id=1, source_target_pairs={{0,1},{1,2},{2,3},{3,4},{4,5},{5,6},{6,7},{8,9},{9,10},{10,11},{11... | collective-permute-start | bytes 24584 | tf_op jit(solution)/shard_map/ppermute | solution.py:19
  17.2 4.3 %collective-permute-start.3 = (f32[2,1,1024]{2,1,0:T(1,128)S(1)}, f32[2,1,1024]{2,1,0:T(1,128)S(1)}, u32[]{:S(2)}, u32[]{:S(2)}) collective-permute-start(f32[2,1,1024]{2,1,0:T(1,128)S(1)} %get-tuple-element.34), channel_id=1, source_target_pairs={{1,0},{2,1},{3,2},{4,3},{5,4},{6,5},{7,6},{9,8},{10,9},{11,10},{12... | collective-permute-start | bytes 24584 | tf_op jit(solution)/shard_map/ppermute | solution.py:20
  18.6 0.7 copy-start.2
  19.3 0.7 copy-start.3
  21.8 5.6 %collective-permute-start.4 = (f32[2,1,1024]{2,1,0:T(1,128)S(1)}, f32[2,1,1024]{2,1,0:T(1,128)S(1)}, u32[]{:S(2)}, u32[]{:S(2)}) collective-permute-start(f32[2,1,1024]{2,1,0:T(1,128)S(1)} %get-tuple-element.31), channel_id=1, source_target_pairs={{0,1},{1,2},{2,3},{3,4},{4,5},{5,6},{6,7},{8,9},{9,10},{10,11},{11... | collective-permute-start | bytes 24584 | tf_op jit(solution)/shard_map/ppermute | solution.py:19
  26.1 3.7 %collective-permute-start.5 = (f32[2,1,1024]{2,1,0:T(1,128)S(1)}, f32[2,1,1024]{2,1,0:T(1,128)S(1)}, u32[]{:S(2)}, u32[]{:S(2)}) collective-permute-start(f32[2,1,1024]{2,1,0:T(1,128)S(1)} %get-tuple-element.32), channel_id=1, source_target_pairs={{1,0},{2,1},{3,2},{4,3},{5,4},{6,5},{7,6},{9,8},{10,9},{11,10},{12... | collective-permute-start | bytes 24584 | tf_op jit(solution)/shard_map/ppermute | solution.py:20
  45.7 2.6 %collective-permute-start.6 = (f32[2,1,1024]{2,1,0:T(1,128)S(1)}, f32[2,1,1024]{2,1,0:T(1,128)S(1)}, u32[]{:S(2)}, u32[]{:S(2)}) collective-permute-start(f32[2,1,1024]{2,1,0:T(1,128)S(1)} %get-tuple-element.29), channel_id=1, source_target_pairs={{0,1},{1,2},{2,3},{3,4},{4,5},{5,6},{6,7},{8,9},{9,10},{10,11},{11... | collective-permute-start | bytes 24584 | tf_op jit(solution)/shard_map/ppermute | solution.py:19
  47.0 4.7 %collective-permute-start.7 = (f32[2,1,1024]{2,1,0:T(1,128)S(1)}, f32[2,1,1024]{2,1,0:T(1,128)S(1)}, u32[]{:S(2)}, u32[]{:S(2)}) collective-permute-start(f32[2,1,1024]{2,1,0:T(1,128)S(1)} %get-tuple-element.30), channel_id=1, source_target_pairs={{1,0},{2,1},{3,2},{4,3},{5,4},{6,5},{7,6},{9,8},{10,9},{11,10},{12... | collective-permute-start | bytes 24584 | tf_op jit(solution)/shard_map/ppermute | solution.py:20
  68.2 3.3 %collective-permute-start.8 = (f32[2,1,1024]{2,1,0:T(1,128)S(1)}, f32[2,1,1024]{2,1,0:T(1,128)S(1)}, u32[]{:S(2)}, u32[]{:S(2)}) collective-permute-start(f32[2,1,1024]{2,1,0:T(1,128)S(1)} %get-tuple-element.27), channel_id=1, source_target_pairs={{0,1},{1,2},{2,3},{3,4},{4,5},{5,6},{6,7},{8,9},{9,10},{10,11},{11... | collective-permute-start | bytes 24584 | tf_op jit(solution)/shard_map/ppermute | solution.py:19
  69.6 4.9 %collective-permute-start.9 = (f32[2,1,1024]{2,1,0:T(1,128)S(1)}, f32[2,1,1024]{2,1,0:T(1,128)S(1)}, u32[]{:S(2)}, u32[]{:S(2)}) collective-permute-start(f32[2,1,1024]{2,1,0:T(1,128)S(1)} %get-tuple-element.28), channel_id=1, source_target_pairs={{1,0},{2,1},{3,2},{4,3},{5,4},{6,5},{7,6},{9,8},{10,9},{11,10},{12... | collective-permute-start | bytes 24584 | tf_op jit(solution)/shard_map/ppermute | solution.py:20
  90.9 0.7 copy-start
  91.0 43.3 %all-reduce.10.cloned.1.call-start = ((), (), s32[]{:S(2)}) async-start(), calls=%async_computation | async-start | bytes 524288 | tf_op jit(solution)/shard_map/psum | solution.py:111
  91.7 0.7 copy-start.4
Sparse Core Ops, SparseCore 0:
  94.1 38.5 all-reduce.9
where the time goes:
time: 143 us
  blocking collectives  89.1 us (62%)
  starting transfers between devices  21 us (15%)
  between operations  15.6 us (11%)
  waiting for transfers between devices  9.38 us (7%)
  local copies, waits for them, and re-layouts  4.17 us (3%)
  other arithmetic  3.21 us (2%)
    psum x3, blocking collectives, paired_inner(): lax.psum((local_inner(residual, scaled), local_inner(scaled, image)), 'ti...  47.4 us
    psum x1, blocking collectives, shards(): readings = lax.psum(local_read, ('wave', 'tile'))  41.8 us
    ppermute x5, starting transfers between devices, extended(): before = lax.ppermute(last, axis, up)  14.5 us
    ppermute x5, waiting for transfers between devices, extended(): after = lax.ppermute(initial, axis, down)  9.25 us
    ppermute x5, starting transfers between devices, extended(): after = lax.ppermute(initial, axis, down)  6.46 us
  transfers between devices with their start and end apart: 11, of which 4 were waited for; matrix products, arithmetic and copies ran while one was open for 0% of the time, Pallas kernels for 0%

commit v1 on v0

v1 whole, which is shorter than its diff:
```python
import jax
import jax.numpy as jnp
from jax import lax
from jax.sharding import PartitionSpec as P

ITERS = 3
SOURCE_STRENGTH = 50.0
TINY = 1e-30


def harmonic(left_val, right_val):
    return 2.0 * left_val * right_val / jnp.maximum(left_val + right_val, TINY)


def safe_div(num, den):
    return jnp.where(den > 0.0, num / jnp.where(den > 0.0, den, 1.0), 0.0)


def tree_sum(values):
    values = list(values)
    while len(values) > 1:
        values = [values[i] + values[i + 1] for i in range(0, len(values), 2)]
    return values[0]


def swap(value, axis, mask, size):
    return lax.ppermute(value, axis, [(i, i ^ mask) for i in range(size)])


def tile_total(value, axis):
    size = lax.axis_size(axis)
    bit = 1
    while bit < size:
        masks = [bit]
        if bit > 1 and bit * 2 < size:
            masks.append(bit * 2)
        offsets = [0]
        for mask in masks:
            offsets += [o ^ mask for o in offsets]
        value = tree_sum([value] + [swap(value, axis, o, size) for o in offsets[1:]])
        bit = masks[-1] * 2
    return value


def step_polynomial(moments):
    def inner(poly):
        return sum(a * b * moments[i + j] for i, a in enumerate(poly) for j, b in enumerate(poly))

    def energy(poly):
        return sum(
            a * b * (moments[i + j] - moments[i + j + 1])
            for i, a in enumerate(poly)
            for j, b in enumerate(poly)
        )

    one = jnp.ones_like(moments[0])
    zero = jnp.zeros_like(moments[0])
    res, way, total = [one], [one], [zero] * ITERS
    gamma = moments[0]
    for iteration in range(ITERS):
        alpha = safe_div(gamma, energy(way))
        total = [t + alpha * (way[i] if i < len(way) else zero) for i, t in enumerate(total)]
        if iteration + 1 < ITERS:
            longer = way + [zero]
            shifted = [zero] + way
            res = [r - alpha * (a - b) for r, a, b in zip(res + [zero], longer, shifted)]
            gamma_next = jnp.maximum(inner(res), 0.0)
            ratio = safe_div(gamma_next, gamma)
            way = [r + ratio * a for r, a in zip(res, longer)]
            gamma = gamma_next
    return total


def shards(
    warm_start,
    class_map,
    conductivities,
    wavenumbers,
    weights,
    source_row,
    source_col,
    electrode_row,
):
    rows, depth = class_map.shape
    sources = warm_start.shape[1]
    tiles, waves = lax.axis_size("tile"), lax.axis_size("wave")
    tile, wave = lax.axis_index("tile"), lax.axis_index("wave")
    halo = ITERS + 1
    even = tile % 2 == 0
    field = warm_start[0]
    ids = class_map.astype(jnp.float32) + 1.0
    stacked = jnp.concatenate([field, ids[None]], axis=0)
    first, last = stacked[:, :halo], stacked[:, rows - halo :]
    near = swap(jnp.where(even, last, first), "tile", 1, tiles)
    far_pairs = [(i, i + 1) for i in range(1, tiles - 1, 2)]
    far = lax.ppermute(
        jnp.where(even, first, last), "tile", far_pairs + [(j, i) for i, j in far_pairs]
    )
    before = jnp.where(even, far, near)
    after = jnp.where(even, near, far)
    wide = jnp.concatenate([before, stacked, after], axis=1)
    start, ids = wide[:sources], wide[sources]
    total_rows = rows + 2 * halo
    sigma = jnp.zeros_like(ids)
    for c in range(conductivities.shape[0]):
        sigma = jnp.where(ids == c + 1.0, conductivities[c], sigma)
    edge_row = jnp.zeros((1, depth), jnp.float32)
    edge_col = jnp.zeros((total_rows, 1), jnp.float32)
    face_row = harmonic(sigma[:-1], sigma[1:])
    face_up = jnp.concatenate([edge_row, face_row], axis=0)
    face_down = jnp.concatenate([face_row, edge_row], axis=0)
    col_inner = harmonic(sigma[:, :-1], sigma[:, 1:])
    face_left = jnp.concatenate([edge_col, col_inner], axis=1)
    face_right = jnp.concatenate([col_inner, sigma[:, -1:]], axis=1)
    wave_num = wavenumbers[0]
    diag = face_up + face_down + face_left + face_right + wave_num * wave_num * sigma
    inverse = 1.0 / jnp.maximum(diag, TINY)
    global_row = tile * rows - halo + jnp.arange(total_rows, dtype=jnp.int32)
    col_ids = jnp.arange(depth, dtype=jnp.int32)
    hits = (global_row[None, :, None] == source_row[:, None, None]) & (
        col_ids[None, None, :] == source_col[:, None, None]
    )

    def spread(values):
        row_padded = jnp.pad(values, ((0, 0), (1, 1), (0, 0)))
        col_padded = jnp.pad(values, ((0, 0), (0, 0), (1, 1)))
        return (
            face_up * row_padded[:, :-2]
            + face_down * row_padded[:, 2:]
            + face_left * col_padded[:, :, :-2]
            + face_right * col_padded[:, :, 2:]
        ) * inverse

    basis = [jnp.where(hits, SOURCE_STRENGTH, 0.0) * inverse - (start - spread(start))]
    for _ in range(ITERS):
        basis.append(spread(basis[-1]))
    own = [b[:, halo : halo + rows] for b in basis]
    own_diag = diag[halo : halo + rows]
    moments = [
        jnp.sum(own_diag * own[n // 2] * own[n - n // 2], axis=(1, 2)) for n in range(2 * ITERS)
    ]
    parts = [field] + own[:ITERS]
    tops = jnp.stack([p[:, :, 0] for p in parts])
    own_row = tile * rows + jnp.arange(rows, dtype=jnp.int32)
    picker = own_row[:, None] == electrode_row[None, :]
    picked = jnp.sum(jnp.where(picker, tops[:, :, :, None], 0.0), axis=2)
    electrodes = electrode_row.shape[0]
    packed = jnp.concatenate([picked.reshape(-1), jnp.stack(moments).reshape(-1)])
    packed = tile_total(packed, "tile")
    picked = packed[: picked.size].reshape(picked.shape)
    moments = packed[picked.size :].reshape(2 * ITERS, sources)
    poly = step_polynomial([moments[n] for n in range(2 * ITERS)])

    def combine(vectors):
        out = vectors[0]
        for coefficient, vector in zip(poly, vectors[1:]):
            out = out + coefficient.reshape((sources,) + (1,) * (vector.ndim - 1)) * vector
        return weights[0] * out

    weighted = combine(parts)
    local_read = combine([picked[i] for i in range(ITERS + 1)])
    share = depth // waves
    pieces, reads = [], []
    for mask in range(waves):
        block = lax.dynamic_slice_in_dim(weighted, (wave ^ mask) * share, share, 2)
        payload = jnp.concatenate([block.reshape(-1), local_read.reshape(-1)])
        if mask:
            payload = swap(payload, "wave", mask, waves)
        pieces.append(payload[: block.size])
        reads.append(payload[block.size :])
    potentials = tree_sum(pieces).reshape(sources, rows, share)
    readings = tree_sum(reads).reshape(sources, electrodes)
    return (potentials, readings)


def solution(mesh):
    return jax.shard_map(
        shards,
        mesh=mesh,
        in_specs=(
            P("wave", None, "tile", None),
            P("tile", None),
            P(),
            P("wave"),
            P("wave"),
            P(),
            P(),
            P(),
        ),
        out_specs=(P(None, "tile", "wave"), P()),
        check_vma=False,
    )
```

time: 143 us -> 38.8 us (0.27)
  blocking collectives: 89.1 us -> 0 us
  between operations: 15.6 us -> 2.23 us
  starting transfers between devices: 21 us -> 13.1 us
  other arithmetic: 3.21 us -> 9.84 us
    psum x4 -> x0, blocking collectives: 89.1 us -> none  [the longest x3 47.4 us: paired_inner(): lax.psum((local_inner(residual, scaled), local_inner(scaled, image)), 'ti...]
    ppermute x10 -> x9, starting transfers between devices: 21 us -> 13.1 us  [the longest x8 12.4 us: swap(): return lax.ppermute(value, axis, [(i, i ^ mask) for i in range(size)])]
    select_n x0 -> x4, other arithmetic: none -> 5.2 us  [the longest x1 5.13 us: shards(): sigma = jnp.where(ids == c + 1.0, conductivities[c], sigma)]
    slice x6 -> x18, local copies, waits for them, and re-layouts: 0.15 us -> 1.89 us  [the longest x1 0.69 us: shards(): sigma = jnp.where(ids == c + 1.0, conductivities[c], sigma)]
    reduce_sum x4 -> x2, other arithmetic: 2.08 us -> 0.61 us  [the longest x1 0.49 us: shards(): jnp.sum(own_diag * own[n // 2] * own[n - n // 2], axis=(1, 2))]
    dynamic_slice x1, local copies, waits for them, and re-layouts: 1.47 us -> 0.01 us  [shards(): block = lax.dynamic_slice_in_dim(weighted, (wave ^ mask) * share, share, 2)]
    ppermute x10 -> x9, waiting for transfers between devices: 9.26 us -> 8.68 us  [the longest x8 8.67 us: swap(): return lax.ppermute(value, axis, [(i, i ^ mask) for i in range(size)])]
  transfers between devices with their start and end apart: 11 -> 9, of which waited for: 4 -> 7; matrix products, arithmetic and copies ran while one was open for 0% -> 4% of each run, Pallas kernels for 0% -> 0%
where the time goes in v1:
time: 38.8 us; the launch traced here: 38.5 us
  starting transfers between devices  13.1 us (34%)
  other arithmetic  9.84 us (25%)
  waiting for transfers between devices  8.68 us (22%)
  local copies, waits for them, and re-layouts  4.69 us (12%)
  between operations  2.23 us (6%)
    ppermute x8, starting transfers between devices, swap(): return lax.ppermute(value, axis, [(i, i ^ mask) for i in range(size)])  12.4 us
    ppermute x8, waiting for transfers between devices, swap(): return lax.ppermute(value, axis, [(i, i ^ mask) for i in range(size)])  8.67 us
    select_n x1, other arithmetic, shards(): sigma = jnp.where(ids == c + 1.0, conductivities[c], sigma)  5.13 us
    unnamed x14, local copies, waits for them, and re-layouts  1.95 us
    add x6, other arithmetic, tree_sum(): values = [values[i] + values[i + 1] for i in range(0, len(values), 2)]  1.3 us
    broadcast_in_dim x1, other arithmetic, shards(): stacked = jnp.concatenate([field, ids[None]], axis=0)  0.96 us
  transfers between devices with their start and end apart: 9, of which 7 were waited for; matrix products, arithmetic and copies ran while one was open for 4% of the time, Pallas kernels for 0%

profile of v1, /device:TPU:0, one launch (start us, length us, event | category | flops | bytes accessed | tf_op | source)
XLA Modules:
  0.0 38.5 jit_solution(14766263724082448135)
XLA Ops:
  0.7 1.0 %add_bitcast_fusion = f32[1,32,1024]{2,1,0:T(8,128)S(1)} fusion(s32[32,1024]{1,0:T(8,128)} %param.9), kind=kLoop, calls=%fused_computation.76 | loop fusion | flops 65536 | bytes 262144 | tf_op jit(solution)/shard_map/broadcast_in_dim | solution.py:92
  1.7 0.6 %collective-permute-start.1 = (f32[3,4,1024]{2,1,0:T(4,128)S(1)}, f32[3,4,1024]{2,1,0:T(4,128)S(1)}, u32[]{:S(2)}, u32[]{:S(2)}) collective-permute-start(f32[3,4,1024]{2,1,0:T(4,128)S(1)} %broadcast_select_fusion.2), channel_id=1, source_target_pairs={{0,1},{1,0},{2,3},{3,2},{4,5},{5,4},{6,7},{7,6},{8,9},{9,8},{10,11... | collective-permute-start | bytes 147464 | tf_op jit(solution)/shard_map/ppermute | solution.py:27
  2.3 0.7 %collective-permute-start = (f32[3,4,1024]{2,1,0:T(4,128)S(1)}, f32[3,4,1024]{2,1,0:T(4,128)S(1)}, u32[]{:S(2)}, u32[]{:S(2)}) collective-permute-start(f32[3,4,1024]{2,1,0:T(4,128)S(1)} %get-tuple-element.19), channel_id=1, source_target_pairs={{1,2},{3,4},{5,6},{2,1},{4,3},{6,5},{9,10},{11,12},{13,14},{10,9},... | collective-permute-start | bytes 147464 | tf_op jit(solution)/shard_map/ppermute | solution.py:96
  2.9 0.1 slice_reduce_fusion.3
  3.0 0.6 %copy-done.2 = s32[2]{0:T(128)S(1)} copy-done((s32[2]{0:T(128)S(1)}, s32[2]{0:T(128)}, u32[]{:S(2)}) %copy-start.2) | copy-done | bytes 32
  3.7 0.6 %copy-done.4 = s32[2]{0:T(128)S(1)} copy-done((s32[2]{0:T(128)S(1)}, s32[2]{0:T(128)}, u32[]{:S(2)}) %copy-start.4) | copy-done | bytes 32
  4.4 0.6 %copy-done.3 = s32[64]{0:T(128)S(1)} copy-done((s32[64]{0:T(128)S(1)}, s32[64]{0:T(128)}, u32[]{:S(2)}) %copy-start.3) | copy-done | bytes 280
  5.1 0.7 %fusion.47 = (f32[1]{0:T(128)}, f32[1]{0:T(128)}, f32[1]{0:T(128)}, f32[1]{0:T(128)}, f32[1]{0:T(128)}, /*index=5*/f32[1]{0:T(128)}, f32[1]{0:T(128)}, f32[1]{0:T(128)}) fusion(f32[8]{0:T(128)S(1)} %copy-done.1), kind=kLoop, calls=%fused_computation.145 | loop fusion | bytes 64 | tf_op jit(solution)/shard_map/slice | solution.py:106
  6.5 5.1 %select_select_fusion = f32[1,40,1024]{2,1,0:T(8,128)S(1)} fusion(f32[3,4,1024]{2,1,0:T(4,128)S(1)} %get-tuple-element.35, f32[1,32,1024]{2,1,0:T(8,128)S(1)} %add_bitcast_fusion, f32[2,32,1024]{2,1,0:T(8,128)S(1)} %bitcast.49, f32[3,4,1024]{2,1,0:T(4,128)S(1)} %get-tuple-element.34, f32[]{:T(128)} %bitcast.3, f32[]{:T(128)} %bitcast.4, f32[]{:T(128)} %bitcast.5, ...), kind=kLoop, calls=%fused_computation.70 | loop fusion | flops 778240 | bytes 655392 | tf_op jit(solution)/shard_map/jit(_where)/select_n | solution.py:106
  11.7 0.1 maximum_divide_fusion.1
  11.9 0.1 pad_slice_fusion.18
  12.0 0.1 maximum_divide_fusion
  12.2 0.3 fusion.5
  12.5 0.1 slice_reduce_fusion.2
  12.6 0.3 fusion.10
  12.8 0.3 fusion.15
  13.1 0.1 slice_reduce_fusion.1
  13.2 0.1 slice_reduce_fusion
  13.3 0.3 pad_slice_fusion.1
  13.6 0.1 select_reduce_fusion
  13.7 0.1 reshape.194
  13.8 0.5 %fusion.31 = (f32[2]{0:T(128)S(1)}, f32[2]{0:T(128)S(1)}, f32[2]{0:T(128)S(1)}, f32[2]{0:T(128)S(1)}, f32[2]{0:T(128)S(1)}, /*index=5*/f32[2]{0:T(128)S(1)}) fusion(f32[2,40,1024]{2,1,0:T(8,128)S(1)} %get-tuple-element.23, f32[2,40,1024]{2,1,0:T(8,128)S(1)} %get-tuple-element.25, f32[2,40,1024]{2,1,0:T(8,128)S(1)} %get-tuple-element.24, ...), kind=kLoop, calls=%fused_computation.56 | loop fusion | flops 1507316 | bytes 2621488 | tf_op jit(solution)/shard_map/reduce_sum | solution.py:140
  14.4 3.9 %collective-permute-start.2 = (f32[524]{0:T(1024)S(1)}, f32[524]{0:T(1024)S(1)}, u32[]{:S(2)}, u32[]{:S(2)}) collective-permute-start(f32[524]{0:T(1024)S(1)} %constant_dynamic-update-slice_fusion), channel_id=1, source_target_pairs={{0,1},{1,0},{2,3},{3,2},{4,5},{5,4},{6,7},{7,6},{8,9},{9,8},{10,11... | collective-permute-start | bytes 6296 | tf_op jit(solution)/shard_map/ppermute | solution.py:27
  18.3 0.8 %collective-permute-done.2 = f32[524]{0:T(1024)S(1)} collective-permute-done((f32[524]{0:T(1024)S(1)}, f32[524]{0:T(1024)S(1)}, u32[]{:S(2)}, u32[]{:S(2)}) %collective-permute-start.2) | collective-permute-done | bytes 2128 | tf_op jit(solution)/shard_map/ppermute | solution.py:27
  19.1 1.8 %collective-permute-start.5 = (f32[524]{0:T(1024)S(1)}, f32[524]{0:T(1024)S(1)}, u32[]{:S(2)}, u32[]{:S(2)}) collective-permute-start(f32[524]{0:T(1024)S(1)} %add.312), channel_id=1, source_target_pairs={{0,6},{1,7},{2,4},{3,5},{4,2},{5,3},{6,0},{7,1},{8,14},{9,15},{10,... | collective-permute-start | bytes 6296 | tf_op jit(solution)/shard_map/ppermute | solution.py:27
  21.0 1.1 %collective-permute-start.4 = (f32[524]{0:T(1024)S(1)}, f32[524]{0:T(1024)S(1)}, u32[]{:S(2)}, u32[]{:S(2)}) collective-permute-start(f32[524]{0:T(1024)S(1)} %add.312), channel_id=1, source_target_pairs={{0,4},{1,5},{2,6},{3,7},{4,0},{5,1},{6,2},{7,3},{8,12},{9,13},{10,... | collective-permute-start | bytes 6296 | tf_op jit(solution)/shard_map/ppermute | solution.py:27
  22.1 0.5 %collective-permute-start.3 = (f32[524]{0:T(1024)S(1)}, f32[524]{0:T(1024)S(1)}, u32[]{:S(2)}, u32[]{:S(2)}) collective-permute-start(f32[524]{0:T(1024)S(1)} %add.312), channel_id=1, source_target_pairs={{0,2},{1,3},{2,0},{3,1},{4,6},{5,7},{6,4},{7,5},{8,10},{9,11},{10,... | collective-permute-start | bytes 6296 | tf_op jit(solution)/shard_map/ppermute | solution.py:27
  23.3 0.4 collective-permute-done.5
  23.7 0.9 %collective-permute-done.4 = f32[524]{0:T(1024)S(1)} collective-permute-done((f32[524]{0:T(1024)S(1)}, f32[524]{0:T(1024)S(1)}, u32[]{:S(2)}, u32[]{:S(2)}) %collective-permute-start.4) | collective-permute-done | bytes 2128 | tf_op jit(solution)/shard_map/ppermute | solution.py:27
  24.6 1.1 %collective-permute-done.3 = f32[524]{0:T(1024)S(1)} collective-permute-done((f32[524]{0:T(1024)S(1)}, f32[524]{0:T(1024)S(1)}, u32[]{:S(2)}, u32[]{:S(2)}) %collective-permute-start.3) | collective-permute-done | bytes 2128 | tf_op jit(solution)/shard_map/ppermute | solution.py:27
  25.7 0.1 add_maximum_fusion
  25.8 0.1 multiply_add_fusion.3
  26.0 0.1 mul.592
  26.2 0.1 mul.595
  26.3 0.2 add_multiply_fusion
  26.5 0.1 mul.589
  26.8 1.6 %collective-permute-start.6 = (f32[16512]{0:T(1024)S(1)}, f32[16512]{0:T(1024)S(1)}, u32[]{:S(2)}, u32[]{:S(2)}) collective-permute-start(f32[16512]{0:T(1024)S(1)} %get-tuple-element.43), channel_id=1, source_target_pairs={{0,8},{8,0},{16,24},{24,16},{1,9},{9,1},{17,25},{25,17},{2,10},{10... | collective-permute-start | bytes 198152 | tf_op jit(solution)/shard_map/ppermute | solution.py:27
  28.4 2.6 %collective-permute-start.7 = (f32[16512]{0:T(1024)S(1)}, f32[16512]{0:T(1024)S(1)}, u32[]{:S(2)}, u32[]{:S(2)}) collective-permute-start(f32[16512]{0:T(1024)S(1)} %get-tuple-element.44), channel_id=1, source_target_pairs={{0,16},{8,24},{16,0},{24,8},{1,17},{9,25},{17,1},{25,9},{2,18},{10... | collective-permute-start | bytes 198152 | tf_op jit(solution)/shard_map/ppermute | solution.py:27
  31.0 0.2 collective-permute-start.8
  31.2 0.1 slice.300
  31.3 0.1 slice.299
  31.5 0.3 collective-permute-done.6
  31.8 0.1 slice.304
  31.9 3.2 %collective-permute-done.7 = f32[16512]{0:T(1024)S(1)} collective-permute-done((f32[16512]{0:T(1024)S(1)}, f32[16512]{0:T(1024)S(1)}, u32[]{:S(2)}, u32[]{:S(2)}) %collective-permute-start.7) | collective-permute-done | bytes 66080 | tf_op jit(solution)/shard_map/ppermute | solution.py:27
  35.1 2.0 %collective-permute-done.8 = f32[16512]{0:T(1024)S(1)} collective-permute-done((f32[16512]{0:T(1024)S(1)}, f32[16512]{0:T(1024)S(1)}, u32[]{:S(2)}, u32[]{:S(2)}) %collective-permute-start.8) | collective-permute-done | bytes 66080 | tf_op jit(solution)/shard_map/ppermute | solution.py:27
  37.2 0.1 add.368
  37.2 0.6 %add_add_fusion = f32[2,32,256]{2,1,0:T(8,128)} fusion(f32[2,32,256]{2,1,0:T(8,128)S(1)} %add.361, f32[2,32,256]{2,1,0:T(8,128)S(1)} %slice.296, f32[2,32,1024]{2,1,0:T(8,128)S(1)} %add_multiply_fusion, s32[]{:T(128)S(6)} %select_n.135), kind=kLoop, calls=%fused_computation.81 | loop fusion | flops 32768 | bytes 262148 | tf_op jit(solution)/shard_map/add | solution.py:22
  37.9 0.6 %add_add_fusion.2 = f32[2,64]{1,0:T(2,128)} fusion(f32[2,64]{1,0:T(2,128)S(1)} %add.368, f32[2,64]{1,0:T(2,128)S(1)} %slice.304, f32[2,64]{1,0:T(2,128)S(1)} %slice.302, f32[2,64]{1,0:T(2,128)S(1)} %slice.301, f32[2,64]{1,0:T(2,128)S(1)} %slice.299, f32[2,64]{1,0:T(2,128)S(1)} %slice.300, f32[]{:T(128)} %bitcast.43, f32[2]{0:T(128)S(1)} %get-tuple-element.42, ...), kind=kLoop, calls=%fused_computation.108 | loop fusion | flops 1152 | bytes 3612 | tf_op jit(solution)/shard_map/add | solution.py:22
  (49 shorter events, 1.3 us)
Async XLA Ops:
  0.6 1.0 %copy-start = (f32[1,2,32,1024]{3,2,1,0:T(8,128)S(1)}, f32[1,2,32,1024]{3,2,1,0:T(8,128)}, u32[]{:S(2)}) copy-start(f32[1,2,32,1024]{3,2,1,0:T(8,128)} %param.8) | copy-start | bytes 786436
  1.7 4.7 %collective-permute-start.1 = (f32[3,4,1024]{2,1,0:T(4,128)S(1)}, f32[3,4,1024]{2,1,0:T(4,128)S(1)}, u32[]{:S(2)}, u32[]{:S(2)}) collective-permute-start(f32[3,4,1024]{2,1,0:T(4,128)S(1)} %broadcast_select_fusion.2), channel_id=1, source_target_pairs={{0,1},{1,0},{2,3},{3,2},{4,5},{5,4},{6,7},{7,6},{8,9},{9,8},{10,11... | collective-permute-start | bytes 147464 | tf_op jit(solution)/shard_map/ppermute | solution.py:27
  2.3 4.2 %collective-permute-start = (f32[3,4,1024]{2,1,0:T(4,128)S(1)}, f32[3,4,1024]{2,1,0:T(4,128)S(1)}, u32[]{:S(2)}, u32[]{:S(2)}) collective-permute-start(f32[3,4,1024]{2,1,0:T(4,128)S(1)} %get-tuple-element.19), channel_id=1, source_target_pairs={{1,2},{3,4},{5,6},{2,1},{4,3},{6,5},{9,10},{11,12},{13,14},{10,9},... | collective-permute-start | bytes 147464 | tf_op jit(solution)/shard_map/ppermute | solution.py:96
  3.0 0.7 %copy-start.2 = (s32[2]{0:T(128)S(1)}, s32[2]{0:T(128)}, u32[]{:S(2)}) copy-start(s32[2]{0:T(128)} %param.14) | copy-start | bytes 28
  3.7 0.7 %copy-start.4 = (s32[2]{0:T(128)S(1)}, s32[2]{0:T(128)}, u32[]{:S(2)}) copy-start(s32[2]{0:T(128)} %param.13) | copy-start | bytes 28
  3.7 1.4 %copy-start.1 = (f32[8]{0:T(128)S(1)}, f32[8]{0:T(128)}, u32[]{:S(2)}) copy-start(f32[8]{0:T(128)} %param.10) | copy-start | bytes 100
  4.3 0.7 %copy-start.3 = (s32[64]{0:T(128)S(1)}, s32[64]{0:T(128)}, u32[]{:S(2)}) copy-start(s32[64]{0:T(128)} %param.15) | copy-start | bytes 772
  14.4 4.7 %collective-permute-start.2 = (f32[524]{0:T(1024)S(1)}, f32[524]{0:T(1024)S(1)}, u32[]{:S(2)}, u32[]{:S(2)}) collective-permute-start(f32[524]{0:T(1024)S(1)} %constant_dynamic-update-slice_fusion), channel_id=1, source_target_pairs={{0,1},{1,0},{2,3},{3,2},{4,5},{5,4},{6,7},{7,6},{8,9},{9,8},{10,11... | collective-permute-start | bytes 6296 | tf_op jit(solution)/shard_map/ppermute | solution.py:27
  19.1 4.5 %collective-permute-start.5 = (f32[524]{0:T(1024)S(1)}, f32[524]{0:T(1024)S(1)}, u32[]{:S(2)}, u32[]{:S(2)}) collective-permute-start(f32[524]{0:T(1024)S(1)} %add.312), channel_id=1, source_target_pairs={{0,6},{1,7},{2,4},{3,5},{4,2},{5,3},{6,0},{7,1},{8,14},{9,15},{10,... | collective-permute-start | bytes 6296 | tf_op jit(solution)/shard_map/ppermute | solution.py:27
  21.0 3.6 %collective-permute-start.4 = (f32[524]{0:T(1024)S(1)}, f32[524]{0:T(1024)S(1)}, u32[]{:S(2)}, u32[]{:S(2)}) collective-permute-start(f32[524]{0:T(1024)S(1)} %add.312), channel_id=1, source_target_pairs={{0,4},{1,5},{2,6},{3,7},{4,0},{5,1},{6,2},{7,3},{8,12},{9,13},{10,... | collective-permute-start | bytes 6296 | tf_op jit(solution)/shard_map/ppermute | solution.py:27
  22.1 3.6 %collective-permute-start.3 = (f32[524]{0:T(1024)S(1)}, f32[524]{0:T(1024)S(1)}, u32[]{:S(2)}, u32[]{:S(2)}) collective-permute-start(f32[524]{0:T(1024)S(1)} %add.312), channel_id=1, source_target_pairs={{0,2},{1,3},{2,0},{3,1},{4,6},{5,7},{6,4},{7,5},{8,10},{9,11},{10,... | collective-permute-start | bytes 6296 | tf_op jit(solution)/shard_map/ppermute | solution.py:27
  26.8 5.0 %collective-permute-start.6 = (f32[16512]{0:T(1024)S(1)}, f32[16512]{0:T(1024)S(1)}, u32[]{:S(2)}, u32[]{:S(2)}) collective-permute-start(f32[16512]{0:T(1024)S(1)} %get-tuple-element.43), channel_id=1, source_target_pairs={{0,8},{8,0},{16,24},{24,16},{1,9},{9,1},{17,25},{25,17},{2,10},{10... | collective-permute-start | bytes 198152 | tf_op jit(solution)/shard_map/ppermute | solution.py:27
  28.4 6.7 %collective-permute-start.7 = (f32[16512]{0:T(1024)S(1)}, f32[16512]{0:T(1024)S(1)}, u32[]{:S(2)}, u32[]{:S(2)}) collective-permute-start(f32[16512]{0:T(1024)S(1)} %get-tuple-element.44), channel_id=1, source_target_pairs={{0,16},{8,24},{16,0},{24,8},{1,17},{9,25},{17,1},{25,9},{2,18},{10... | collective-permute-start | bytes 198152 | tf_op jit(solution)/shard_map/ppermute | solution.py:27
  31.0 6.1 %collective-permute-start.8 = (f32[16512]{0:T(1024)S(1)}, f32[16512]{0:T(1024)S(1)}, u32[]{:S(2)}, u32[]{:S(2)}) collective-permute-start(f32[16512]{0:T(1024)S(1)} %get-tuple-element.45), channel_id=1, source_target_pairs={{0,24},{8,16},{16,8},{24,0},{1,25},{9,17},{17,9},{25,1},{2,26},{10... | collective-permute-start | bytes 198152 | tf_op jit(solution)/shard_map/ppermute | solution.py:27

commit v2 on v1

v2 whole, which is shorter than its diff:
```python
import functools

import jax
import jax.numpy as jnp
from jax import lax
from jax.experimental import pallas as pl
from jax.experimental.pallas import tpu as pltpu
from jax.sharding import PartitionSpec as P

ITERS = 3
SOURCE_STRENGTH = 50.0
TINY = 1e-30
LANES = 128
SUBLANES = 8


def harmonic(left_val, right_val):
    return 2.0 * left_val * right_val / jnp.maximum(left_val + right_val, TINY)


def safe_div(num, den):
    return jnp.where(den > 0.0, num / jnp.where(den > 0.0, den, 1.0), 0.0)


def tree_sum(values):
    values = list(values)
    while len(values) > 1:
        values = [values[i] + values[i + 1] for i in range(0, len(values), 2)]
    return values[0]


def swap(value, axis, mask, size):
    return lax.ppermute(value, axis, [(i, i ^ mask) for i in range(size)])


def tile_total(value, axis):
    size = lax.axis_size(axis)
    bit = 1
    while bit < size:
        masks = [bit]
        if bit > 1 and bit * 2 < size:
            masks.append(bit * 2)
        offsets = [0]
        for mask in masks:
            offsets += [o ^ mask for o in offsets]
        value = tree_sum([value] + [swap(value, axis, o, size) for o in offsets[1:]])
        bit = masks[-1] * 2
    return value


def step_polynomial(moments):
    def inner(poly):
        return sum(a * b * moments[i + j] for i, a in enumerate(poly) for j, b in enumerate(poly))

    def energy(poly):
        return sum(
            a * b * (moments[i + j] - moments[i + j + 1])
            for i, a in enumerate(poly)
            for j, b in enumerate(poly)
        )

    one = jnp.ones_like(moments[0])
    zero = jnp.zeros_like(moments[0])
    res, way, total = [one], [one], [zero] * ITERS
    gamma = moments[0]
    for iteration in range(ITERS):
        alpha = safe_div(gamma, energy(way))
        total = [t + alpha * (way[i] if i < len(way) else zero) for i, t in enumerate(total)]
        if iteration + 1 < ITERS:
            longer = way + [zero]
            shifted = [zero] + way
            res = [r - alpha * (a - b) for r, a, b in zip(res + [zero], longer, shifted)]
            gamma_next = jnp.maximum(inner(res), 0.0)
            ratio = safe_div(gamma_next, gamma)
            way = [r + ratio * a for r, a in zip(res, longer)]
            gamma = gamma_next
    return total


def vmem_call(kernel, out_shape, inputs, scratch=()):
    spec = pl.BlockSpec(memory_space=pltpu.VMEM)
    return pl.pallas_call(
        kernel,
        out_shape=out_shape,
        in_specs=[spec] * len(inputs),
        out_specs=jax.tree.map(lambda _: spec, out_shape),
        scratch_shapes=list(scratch),
    )(*inputs)


def stencil_kernel(
    n_class, par_ref, field_ref, class_ref, halo_ref, *refs
):
    x_ref = refs[0]
    basis_refs = refs[1 : 1 + ITERS]
    pay_ref, sig_ref, left_ref, up_ref, down_ref, west_ref, east_ref, diag_ref = refs[1 + ITERS :]
    sources, rows, depth = field_ref.shape
    total = x_ref.shape[2]
    chunks = depth // LANES
    lane = lax.broadcasted_iota(jnp.int32, (total, LANES), 1)
    row = lax.broadcasted_iota(jnp.int32, (total, LANES), 0)

    def scalar(i):
        return par_ref[0:1, i : i + 1]

    def cols(c):
        return slice(c * LANES, (c + 1) * LANES)

    values = [scalar(i) for i in range(n_class)]
    square = scalar(n_class) * scalar(n_class)
    base = scalar(n_class + 2)
    for c in range(chunks):
        ids = jnp.concatenate(
            [class_ref[:, cols(c)].astype(jnp.float32) + 1.0, halo_ref[sources, :, cols(c)]], axis=0
        )
        sigma = jnp.zeros((total, LANES), jnp.float32)
        for i, value in enumerate(values):
            sigma = jnp.where(ids == i + 1.0, value, sigma)
        sig_ref[c] = sigma
        for s in range(sources):
            x_ref[s, c] = jnp.concatenate([field_ref[s, :, cols(c)], halo_ref[s, :, cols(c)]], axis=0)

    def from_left(ref, c):
        here = pltpu.roll(ref[c], 1, 1)
        other = pltpu.roll(ref[c - 1 if c else chunks - 1], 1, 1)
        return jnp.where(lane == 0, other, here)

    def from_right(ref, c):
        here = pltpu.roll(ref[c], LANES - 1, 1)
        other = pltpu.roll(ref[(c + 1) % chunks], LANES - 1, 1)
        return jnp.where(lane == LANES - 1, other, here)

    for c in range(chunks):
        face = harmonic(from_left(sig_ref, c), sig_ref[c])
        left_ref[c] = jnp.where(lane == 0, 0.0, face) if c == 0 else face

    far_row = jnp.where(row < total - (total - rows) // 2, row, row - total).astype(jnp.float32)
    for c in range(chunks):
        sigma = sig_ref[c]
        up = harmonic(pltpu.roll(sigma, 1, 0), sigma)
        down = pltpu.roll(up, total - 1, 0)
        left = left_ref[c]
        right = from_right(left_ref, c)
        diag = up + down + left + right + square * sigma
        if c == chunks - 1:
            diag = diag + jnp.where(lane == LANES - 1, sigma, 0.0)
        inverse = 1.0 / jnp.maximum(diag, TINY)
        diag_ref[c] = diag
        up_ref[c] = up * inverse
        down_ref[c] = down * inverse
        west_ref[c] = left * inverse
        east_ref[c] = right * inverse
        for s in range(sources):
            hit = (far_row + base == scalar(n_class + 3 + s)) & (
                (lane + c * LANES).astype(jnp.float32) == scalar(n_class + 3 + sources + s)
            )
            basis_refs[0][s, c] = jnp.where(hit, SOURCE_STRENGTH * inverse, 0.0)

    def spread(ref, s, c):
        here = ref[s, c]
        return (
            up_ref[c] * pltpu.roll(here, 1, 0)
            + down_ref[c] * pltpu.roll(here, total - 1, 0)
            + west_ref[c] * from_left(ref.at[s], c)
            + east_ref[c] * from_right(ref.at[s], c)
        )

    def fold(value):
        out = value[0:SUBLANES]
        for r in range(SUBLANES, rows, SUBLANES):
            out = out + value[r : r + SUBLANES]
        return out

    moments = [[None] * sources for _ in range(2 * ITERS)]

    def add(n, s, value):
        moments[n][s] = value if moments[n][s] is None else moments[n][s] + value

    for c in range(chunks):
        for s in range(sources):
            first = basis_refs[0][s, c] - (x_ref[s, c] - spread(x_ref, s, c))
            basis_refs[0][s, c] = first
            own = first[:rows]
            add(0, s, fold(diag_ref[c, :rows] * own * own))
    for i in range(ITERS):
        for c in range(chunks):
            for s in range(sources):
                new = spread(basis_refs[i], s, c)
                own = new[:rows]
                weighted = diag_ref[c, :rows] * own
                add(2 * i + 1, s, fold(weighted * basis_refs[i][s, c, :rows]))
                if i + 1 < ITERS:
                    basis_refs[i + 1][s, c] = new
                    add(2 * i + 2, s, fold(weighted * own))

    spot = (lax.broadcasted_iota(jnp.int32, (rows, LANES), 0)).astype(jnp.float32) + base
    picker = spot == par_ref[1:2, :]
    lines = []
    for ref in (x_ref, *basis_refs):
        for s in range(sources):
            top = jnp.broadcast_to(ref[s, 0, :rows, 0:1], (rows, LANES))
            lines.append(jnp.sum(fold(jnp.where(picker, top, 0.0)), axis=0, keepdims=True))
    for n in range(2 * ITERS):
        for s in range(sources):
            lines.append(jnp.sum(moments[n][s], axis=0, keepdims=True))
    pay_ref[...] = jnp.zeros(pay_ref.shape, jnp.float32)
    for i, line in enumerate(lines):
        pay_ref[i : i + 1, :] = line


def combine_kernel(waves, par_ref, pay_ref, *refs):
    part_refs = refs[: ITERS + 1]
    out_refs = refs[ITERS + 1 :]
    sources, chunks, total, _ = part_refs[0].shape
    n_parts = ITERS + 1
    first = n_parts * sources
    sums = jnp.sum(pay_ref[first : first + 2 * ITERS * sources, :], axis=1, keepdims=True)
    poly = step_polynomial(
        [sums[n * sources : (n + 1) * sources] for n in range(2 * ITERS)]
    )
    weight = par_ref[0:1, 0:1]
    scale = [[weight * p[s : s + 1] for p in poly] for s in range(sources)]
    read = []
    for s in range(sources):
        line = weight * pay_ref[s : s + 1, :]
        for i in range(ITERS):
            line = line + scale[s][i] * pay_ref[(i + 1) * sources + s : (i + 1) * sources + s + 1, :]
        read.append(line)
    share = out_refs[0].shape[1]
    rows = (out_refs[0].shape[0] - SUBLANES) // sources
    split = share % LANES == 0
    wave = lax.axis_index("wave") if split else 0
    per = share // LANES
    for mask, out_ref in enumerate(out_refs):
        block = wave ^ mask if split else 0
        for s in range(sources):
            for k in range(per):
                value = weight * part_refs[0][s, block * per + k, :rows]
                for i in range(ITERS):
                    value = value + scale[s][i] * part_refs[i + 1][s, block * per + k, :rows]
                out_ref[s * rows : (s + 1) * rows, k * LANES : (k + 1) * LANES] = value
        out_ref[sources * rows :, :] = jnp.zeros((SUBLANES, share), jnp.float32)
        for s in range(sources):
            out_ref[sources * rows + s : sources * rows + s + 1, :LANES] = read[s]


def sum_kernel(*refs):
    part_refs, (field_ref, read_ref) = refs[:-2], refs[-2:]
    sources, rows, share = field_ref.shape
    electrodes = read_ref.shape[1]
    for s in range(sources):
        field_ref[s] = tree_sum([r[s * rows : (s + 1) * rows, :] for r in part_refs])
    last = tree_sum([r[sources * rows :, :LANES] for r in part_refs])
    read_ref[...] = last[:sources, :electrodes]


def shards(
    warm_start,
    class_map,
    conductivities,
    wavenumbers,
    weights,
    source_row,
    source_col,
    electrode_row,
):
    rows, depth = class_map.shape
    sources = warm_start.shape[1]
    n_class = conductivities.shape[0]
    electrodes = electrode_row.shape[0]
    tiles, waves = lax.axis_size("tile"), lax.axis_size("wave")
    tile, wave = lax.axis_index("tile"), lax.axis_index("wave")
    halo = ITERS + 1
    even = tile % 2 == 0
    field = warm_start[0]

    def rim(at):
        ids = class_map[at : at + halo].astype(jnp.float32) + 1.0
        return jnp.concatenate([field[:, at : at + halo], ids[None]], axis=0)

    first, last = rim(0), rim(rows - halo)
    near = swap(jnp.where(even, last, first), "tile", 1, tiles)
    far_pairs = [(i, i + 1) for i in range(1, tiles - 1, 2)]
    far = lax.ppermute(
        jnp.where(even, first, last), "tile", far_pairs + [(j, i) for i, j in far_pairs]
    )
    params = jnp.concatenate(
        [
            conductivities,
            wavenumbers,
            weights,
            (tile * rows).astype(jnp.float32)[None],
            source_row.astype(jnp.float32),
            source_col.astype(jnp.float32),
        ]
    )
    params = jnp.stack(
        [
            jnp.pad(params, (0, LANES - params.shape[0])),
            jnp.pad(
                electrode_row.astype(jnp.float32), (0, LANES - electrodes), constant_values=-1.0
            ),
        ]
    )
    rim_wide = jnp.where(
        even, jnp.concatenate([near, far], axis=1), jnp.concatenate([far, near], axis=1)
    )
    total, chunks = rows + 2 * halo, depth // LANES
    f32 = jnp.float32
    wide = jax.ShapeDtypeStruct((sources, chunks, total, LANES), f32)
    n_lines = sources * (3 * ITERS + 1)
    lines = -(-n_lines // SUBLANES) * SUBLANES
    parts = vmem_call(
        functools.partial(stencil_kernel, n_class),
        [wide] * (ITERS + 1) + [jax.ShapeDtypeStruct((lines, LANES), f32)],
        [params, field, class_map, rim_wide],
        [pltpu.VMEM((chunks, total, LANES), f32)] * 7,
    )
    parts, packed = parts[:-1], parts[-1]
    packed = tile_total(packed, "tile")
    share = depth // waves
    split = share % LANES == 0
    width = share if split else depth
    block = jax.ShapeDtypeStruct((sources * rows + SUBLANES, width), f32)
    pieces = vmem_call(
        functools.partial(combine_kernel, waves),
        [block] * (waves if split else 1),
        [params[:, n_class + 1 : n_class + 2], packed, *parts],
    )
    if not split:
        n = sources * rows
        read = pieces[0][n : n + sources, :electrodes].reshape(-1, share)
        pieces = [
            jnp.concatenate(
                [lax.dynamic_slice_in_dim(pieces[0][:n], (wave ^ mask) * share, share, 1), read]
            )
            for mask in range(waves)
        ]
    pieces = [pieces[0]] + [swap(pieces[m], "wave", m, waves) for m in range(1, waves)]
    if not split:
        final = tree_sum(pieces)
        return (
            final[: sources * rows].reshape(sources, rows, share),
            final[sources * rows :].reshape(sources, electrodes),
        )
    return tuple(
        vmem_call(
            sum_kernel,
            [
                jax.ShapeDtypeStruct((sources, rows, share), f32),
                jax.ShapeDtypeStruct((sources, electrodes), f32),
            ],
            pieces,
        )
    )


def solution(mesh):
    return jax.shard_map(
        shards,
        mesh=mesh,
        in_specs=(
            P("wave", None, "tile", None),
            P("tile", None),
            P(),
            P("wave"),
            P("wave"),
            P(),
            P(),
            P(),
        ),
        out_specs=(P(None, "tile", "wave"), P()),
        check_vma=False,
    )
```

time: 38.8 us -> 40.3 us (1.039)
  Pallas kernels: 0 us -> 7.57 us
  other arithmetic: 9.84 us -> 3.4 us
  waiting for transfers between devices: 8.68 us -> 9.7 us
  local copies, waits for them, and re-layouts: 4.69 us -> 4.21 us
    pallas_call x0 -> x3, Pallas kernels: none -> 7.57 us  [vmem_call(): pl.pallas_call(kernel, out_shape=out_shape, in_specs=[spec] * len(inputs)...]
    select_n x3 -> x1, other arithmetic: 5.18 us -> 0.69 us  [shards(): jnp.where(even, jnp.concatenate([near, far], axis=1), jnp.concatenate([fa...]
    ppermute x8, waiting for transfers between devices: 8.67 us -> 9.7 us  [swap(): return lax.ppermute(value, axis, [(i, i ^ mask) for i in range(size)])]
    mul x3 -> x0, other arithmetic: 0.66 us -> none  [the longest x2 0.51 us: spread(): (face_up * row_padded[:, :-2] + face_down * row_padded[:, 2:] + face_left...]
    unnamed x14 -> x16, local copies, waits for them, and re-layouts: 1.95 us -> 2.6 us
    reduce_sum x2 -> x0, other arithmetic: 0.61 us -> none  [the longest x1 0.49 us: shards(): jnp.sum(own_diag * own[n // 2] * own[n - n // 2], axis=(1, 2))]
    another operation x1, other arithmetic: 0.01 us -> 0.57 us  [shards(): jnp.stack([jnp.pad(params, (0, LANES - params.shape[0])), jnp.pad(electro...]
    mul x6 -> x0, local copies, waits for them, and re-layouts: 0.46 us -> none  [combine(): coefficient.reshape((sources,) + (1,) * (vector.ndim - 1)) * vector]
  transfers between devices with their start and end apart: 9 -> 9, of which waited for: 7 -> 7; matrix products, arithmetic and copies ran while one was open for 4% -> 3% of each run, Pallas kernels for 0% -> 0%
where the time goes in v2:
time: 40.3 us; the launch traced here: 39.9 us
  starting transfers between devices  12.9 us (32%)
  waiting for transfers between devices  9.7 us (24%)
  Pallas kernels  7.57 us (19%)
  local copies, waits for them, and re-layouts  4.21 us (10%)
  other arithmetic  3.4 us (8%)
  between operations  2.03 us (5%)
    ppermute x8, starting transfers between devices, swap(): return lax.ppermute(value, axis, [(i, i ^ mask) for i in range(size)])  12.3 us
    ppermute x8, waiting for transfers between devices, swap(): return lax.ppermute(value, axis, [(i, i ^ mask) for i in range(size)])  9.7 us
    pallas_call x3, Pallas kernels, vmem_call(): pl.pallas_call(kernel, out_shape=out_shape, in_specs=[spec] * len(inputs)...  7.57 us
    unnamed x16, local copies, waits for them, and re-layouts  2.6 us
    add x2, other arithmetic, tree_sum(): values = [values[i] + values[i + 1] for i in range(0, len(values), 2)]  1.31 us
    slice x1, local copies, waits for them, and re-layouts, rim(): return jnp.concatenate([field[:, at:at + halo], ids[None]], axis=0)  0.89 us
  transfers between devices with their start and end apart: 9, of which 7 were waited for; matrix products, arithmetic and copies ran while one was open for 3% of the time, Pallas kernels for 0%

profile of v2, /device:TPU:0, one launch (start us, length us, event | category | flops | bytes accessed | tf_op | source)
XLA Modules:
  0.0 39.9 jit_solution(78124328241714675)
XLA Ops:
  0.6 0.8 %add_bitcast_fusion.1 = (f32[1,4,1024]{2,1,0:T(4,128)S(1)}, f32[1,4,1024]{2,1,0:T(4,128)S(1)}) fusion(s32[32,1024]{1,0:T(8,128)} %class_ref.1), kind=kLoop, calls=%fused_computation.6 | loop fusion | flops 16384 | bytes 65536 | tf_op jit(solution)/shard_map/broadcast_in_dim | solution.py:279
  1.4 0.9 %fusion.2 = (f32[2,4,1024]{2,1,0:T(4,128)S(1)}, f32[2,4,1024]{2,1,0:T(4,128)S(1)}) fusion(f32[2,32,1024]{2,1,0:T(8,128)} %bitcast.10), kind=kLoop, calls=%fused_computation.11 | loop fusion | bytes 131072 | tf_op jit(solution)/shard_map/slice | solution.py:279
  2.4 0.6 %collective-permute-start = (f32[3,4,1024]{2,1,0:T(4,128)S(1)}, f32[3,4,1024]{2,1,0:T(4,128)S(1)}, u32[]{:S(2)}, u32[]{:S(2)}) collective-permute-start(f32[3,4,1024]{2,1,0:T(4,128)S(1)} %get-tuple-element.24), channel_id=1, source_target_pairs={{0,1},{1,0},{2,3},{3,2},{4,5},{5,4},{6,7},{7,6},{8,9},{9,8},{10,11... | collective-permute-start | bytes 147464 | tf_op jit(solution)/shard_map/ppermute | solution.py:33
  2.9 0.7 %collective-permute-start.1 = (f32[3,4,1024]{2,1,0:T(4,128)S(1)}, f32[3,4,1024]{2,1,0:T(4,128)S(1)}, u32[]{:S(2)}, u32[]{:S(2)}) collective-permute-start(f32[3,4,1024]{2,1,0:T(4,128)S(1)} %get-tuple-element.25), channel_id=1, source_target_pairs={{1,2},{3,4},{5,6},{2,1},{4,3},{6,5},{9,10},{11,12},{13,14},{10,9},... | collective-permute-start | bytes 147464 | tf_op jit(solution)/shard_map/ppermute | solution.py:284
  4.2 0.0 copy-start.5
  4.9 0.0 copy-done.5
  4.9 0.0 copy-start.6
  4.9 0.6 %copy-done.6 = s32[2]{0:T(128)S(1)} copy-done((s32[2]{0:T(128)S(1)}, s32[2]{0:T(128)}, u32[]{:S(2)}) %copy-start.6) | copy-done | bytes 32
  5.6 0.0 copy-start.7
  5.6 0.7 %copy-done.7 = s32[64]{0:T(128)S(1)} copy-done((s32[64]{0:T(128)S(1)}, s32[64]{0:T(128)}, u32[]{:S(2)}) %copy-start.7) | copy-done | bytes 280
  6.2 0.0 copy-start.4
  6.2 0.7 %copy-done.4 = f32[8]{0:T(128)S(1)} copy-done((f32[8]{0:T(128)S(1)}, f32[8]{0:T(128)}, u32[]{:S(2)}) %copy-start.4) | copy-done | bytes 56
  6.9 0.1 concatenate.15
  7.0 0.6 %pad_maximum_fusion.2.par_ref = f32[2,128]{1,0:T(2,128)} fusion(f32[1,128]{1,0:T(1,128)S(1)} %get-tuple-element.26, f32[1,128]{1,0:T(1,128)S(1)} %get-tuple-element.27), kind=kLoop, calls=%fused_computation.8 | loop fusion | flops 256 | bytes 2048 | tf_op jit(solution)/shard_map/stack | solution.py:297
  7.5 0.0 collective-permute-done
  7.6 0.0 collective-permute-done.1
  7.6 0.7 %maximum_select_fusion.halo_ref = f32[3,8,1024]{2,1,0:T(8,128)} fusion(f32[3,4,1024]{2,1,0:T(4,128)S(1)} %collective-permute-done.1, f32[3,4,1024]{2,1,0:T(4,128)S(1)} %collective-permute-done, pred[]{:T(512)S(6)} %eq.5), kind=kLoop, calls=%fused_computation | loop fusion | flops 73728 | bytes 196609 | tf_op jit(solution)/shard_map/jit(_where)/select_n | solution.py:305
  8.2 3.6 %shard_map.95 = (f32[2,8,40,128]{3,2,1,0:T(8,128)}, f32[2,8,40,128]{3,2,1,0:T(8,128)}, f32[2,8,40,128]{3,2,1,0:T(8,128)}, f32[2,8,40,128]{3,2,1,0:T(8,128)}, f32[24,128]{1,0:T(8,128)}) custom-call(f32[2,128]{1,0:T(2,128)} %pad_maximum_fusion.2.par_ref, f32[2,32,1024]{2,1,0:T(8,128)} %bitcast.11, s32[32,1024]{1,0:T(8,128)} %class_ref.1, ...), custom_call_target="tpu_custom_call" | custom-call | tf_op jit(solution)/shard_map/pallas_call | solution.py:82
  11.9 0.0 copy-start.3
  11.9 3.9 %collective-permute-start.2 = (f32[24,128]{1,0:T(8,128)}, f32[24,128]{1,0:T(8,128)S(1)}, u32[]{:S(2)}, u32[]{:S(2)}) collective-permute-start(f32[24,128]{1,0:T(8,128)} %get-tuple-element.11), channel_id=1, source_target_pairs={{0,1},{1,0},{2,3},{3,2},{4,5},{5,4},{6,7},{7,6},{8,9},{9,8},{10,11... | collective-permute-start | bytes 36872 | tf_op jit(solution)/shard_map/ppermute | solution.py:33
  15.8 1.0 %collective-permute-done.2 = f32[24,128]{1,0:T(8,128)S(1)} collective-permute-done((f32[24,128]{1,0:T(8,128)}, f32[24,128]{1,0:T(8,128)S(1)}, u32[]{:S(2)}, u32[]{:S(2)}) %collective-permute-start.2) | collective-permute-done | bytes 12320 | tf_op jit(solution)/shard_map/ppermute | solution.py:33
  16.8 0.7 %add.29 = f32[24,128]{1,0:T(8,128)S(1)} add(f32[24,128]{1,0:T(8,128)} %get-tuple-element.11, f32[24,128]{1,0:T(8,128)S(1)} %collective-permute-done.2) | non-fusion elementwise | flops 3072 | bytes 36864 | tf_op jit(solution)/shard_map/add | solution.py:28
  17.5 1.8 %collective-permute-start.5 = (f32[24,128]{1,0:T(8,128)S(1)}, f32[24,128]{1,0:T(8,128)S(1)}, u32[]{:S(2)}, u32[]{:S(2)}) collective-permute-start(f32[24,128]{1,0:T(8,128)S(1)} %add.29), channel_id=1, source_target_pairs={{0,6},{1,7},{2,4},{3,5},{4,2},{5,3},{6,0},{7,1},{8,14},{9,15},{10,... | collective-permute-start | bytes 36872 | tf_op jit(solution)/shard_map/ppermute | solution.py:33
  19.3 1.1 %collective-permute-start.4 = (f32[24,128]{1,0:T(8,128)S(1)}, f32[24,128]{1,0:T(8,128)S(1)}, u32[]{:S(2)}, u32[]{:S(2)}) collective-permute-start(f32[24,128]{1,0:T(8,128)S(1)} %add.29), channel_id=1, source_target_pairs={{0,4},{1,5},{2,6},{3,7},{4,0},{5,1},{6,2},{7,3},{8,12},{9,13},{10,... | collective-permute-start | bytes 36872 | tf_op jit(solution)/shard_map/ppermute | solution.py:33
  20.5 0.5 %collective-permute-start.3 = (f32[24,128]{1,0:T(8,128)S(1)}, f32[24,128]{1,0:T(8,128)S(1)}, u32[]{:S(2)}, u32[]{:S(2)}) collective-permute-start(f32[24,128]{1,0:T(8,128)S(1)} %add.29), channel_id=1, source_target_pairs={{0,2},{1,3},{2,0},{3,1},{4,6},{5,7},{6,4},{7,5},{8,10},{9,11},{10,... | collective-permute-start | bytes 36872 | tf_op jit(solution)/shard_map/ppermute | solution.py:33
  21.0 0.0 copy-done.3
  21.0 0.6 %slice.15.par_ref = f32[2,1]{1,0:T(2,128)} slice(f32[2,128]{1,0:T(2,128)S(1)} %copy-done.3), slice={[0:2], [9:10]} | slice | bytes 16 | tf_op jit(solution)/shard_map/slice | solution.py:328
  21.6 0.5 %collective-permute-done.5 = f32[24,128]{1,0:T(8,128)S(1)} collective-permute-done((f32[24,128]{1,0:T(8,128)S(1)}, f32[24,128]{1,0:T(8,128)S(1)}, u32[]{:S(2)}, u32[]{:S(2)}) %collective-permute-start.5) | collective-permute-done | bytes 12320 | tf_op jit(solution)/shard_map/ppermute | solution.py:33
  22.1 0.9 %collective-permute-done.4 = f32[24,128]{1,0:T(8,128)S(1)} collective-permute-done((f32[24,128]{1,0:T(8,128)S(1)}, f32[24,128]{1,0:T(8,128)S(1)}, u32[]{:S(2)}, u32[]{:S(2)}) %collective-permute-start.4) | collective-permute-done | bytes 12320 | tf_op jit(solution)/shard_map/ppermute | solution.py:33
  23.0 1.1 %collective-permute-done.3 = f32[24,128]{1,0:T(8,128)S(1)} collective-permute-done((f32[24,128]{1,0:T(8,128)S(1)}, f32[24,128]{1,0:T(8,128)S(1)}, u32[]{:S(2)}, u32[]{:S(2)}) %collective-permute-start.3) | collective-permute-done | bytes 12320 | tf_op jit(solution)/shard_map/ppermute | solution.py:33
  24.2 0.6 %add_add_fusion.pay_ref = f32[24,128]{1,0:T(8,128)} fusion(f32[24,128]{1,0:T(8,128)S(1)} %collective-permute-done.4, f32[24,128]{1,0:T(8,128)S(1)} %collective-permute-done.5, f32[24,128]{1,0:T(8,128)S(1)} %add.29, f32[24,128]{1,0:T(8,128)S(1)} %collective-permute-done.3), kind=kLoop, calls=%fused_computation.7 | loop fusion | flops 9216 | bytes 61440 | tf_op jit(solution)/shard_map/add | solution.py:28
  24.8 2.3 %shard_map.96 = (f32[72,256]{1,0:T(8,128)}, f32[72,256]{1,0:T(8,128)}, f32[72,256]{1,0:T(8,128)}, f32[72,256]{1,0:T(8,128)}) custom-call(f32[2,1]{1,0:T(2,128)} %slice.15.par_ref, f32[24,128]{1,0:T(8,128)} %add_add_fusion.pay_ref, f32[2,8,40,128]{3,2,1,0:T(8,128)} %get-tuple-element.12.refs_0_, f32[2,8,40,128]{3,2,1,0:T(8,128)} %get-tuple-element.13.refs_1_, ...), custom_call_target="tpu_custom_call" | custom-call | tf_op jit(solution)/shard_map/pallas_call | solution.py:82
  27.1 1.6 %collective-permute-start.6 = (f32[72,256]{1,0:T(8,128)}, f32[72,256]{1,0:T(8,128)S(1)}, u32[]{:S(2)}, u32[]{:S(2)}) collective-permute-start(f32[72,256]{1,0:T(8,128)} %get-tuple-element.17), channel_id=1, source_target_pairs={{0,8},{8,0},{16,24},{24,16},{1,9},{9,1},{17,25},{25,17},{2,10},{10... | collective-permute-start | bytes 221192 | tf_op jit(solution)/shard_map/ppermute | solution.py:33
  28.6 2.6 %collective-permute-start.7 = (f32[72,256]{1,0:T(8,128)}, f32[72,256]{1,0:T(8,128)S(1)}, u32[]{:S(2)}, u32[]{:S(2)}) collective-permute-start(f32[72,256]{1,0:T(8,128)} %get-tuple-element.18), channel_id=1, source_target_pairs={{0,16},{8,24},{16,0},{24,8},{1,17},{9,25},{17,1},{25,9},{2,18},{10... | collective-permute-start | bytes 221192 | tf_op jit(solution)/shard_map/ppermute | solution.py:33
  31.2 0.2 collective-permute-start.8
  31.4 0.9 %collective-permute-done.6.refs_1_ = f32[72,256]{1,0:T(8,128)S(1)} collective-permute-done((f32[72,256]{1,0:T(8,128)}, f32[72,256]{1,0:T(8,128)S(1)}, u32[]{:S(2)}, u32[]{:S(2)}) %collective-permute-start.6) | collective-permute-done | bytes 73760 | tf_op jit(solution)/shard_map/ppermute | solution.py:33
  32.3 0.0 copy-start
  32.3 3.4 %collective-permute-done.7.refs_2_ = f32[72,256]{1,0:T(8,128)S(1)} collective-permute-done((f32[72,256]{1,0:T(8,128)}, f32[72,256]{1,0:T(8,128)S(1)}, u32[]{:S(2)}, u32[]{:S(2)}) %collective-permute-start.7) | collective-permute-done | bytes 73760 | tf_op jit(solution)/shard_map/ppermute | solution.py:33
  35.7 0.0 copy-start.1
  35.7 1.9 %collective-permute-done.8.refs_3_ = f32[72,256]{1,0:T(8,128)S(1)} collective-permute-done((f32[72,256]{1,0:T(8,128)}, f32[72,256]{1,0:T(8,128)S(1)}, u32[]{:S(2)}, u32[]{:S(2)}) %collective-permute-start.8) | collective-permute-done | bytes 73760 | tf_op jit(solution)/shard_map/ppermute | solution.py:33
  37.6 0.0 copy-start.2
  37.6 0.0 copy-done
  37.6 0.0 copy-done.1
  37.6 0.6 %copy-done.2 = f32[72,256]{1,0:T(8,128)} copy-done((f32[72,256]{1,0:T(8,128)}, f32[72,256]{1,0:T(8,128)S(1)}, u32[]{:S(2)}) %copy-start.2) | copy-done | bytes 73752
  38.2 1.6 %shard_map.97 = (f32[2,32,256]{2,1,0:T(8,128)}, f32[2,64]{1,0:T(2,128)}) custom-call(f32[72,256]{1,0:T(8,128)} %get-tuple-element.16.refs_0_, f32[72,256]{1,0:T(8,128)} %copy-done, f32[72,256]{1,0:T(8,128)} %copy-done.1, f32[72,256]{1,0:T(8,128)} %copy-done.2), custom_call_target="tpu_custom_call" | custom-call | tf_op jit(solution)/shard_map/pallas_call | solution.py:82
  (5 shorter events, 0.0 us)
Async XLA Ops:
  2.4 5.2 %collective-permute-start = (f32[3,4,1024]{2,1,0:T(4,128)S(1)}, f32[3,4,1024]{2,1,0:T(4,128)S(1)}, u32[]{:S(2)}, u32[]{:S(2)}) collective-permute-start(f32[3,4,1024]{2,1,0:T(4,128)S(1)} %get-tuple-element.24), channel_id=1, source_target_pairs={{0,1},{1,0},{2,3},{3,2},{4,5},{5,4},{6,7},{7,6},{8,9},{9,8},{10,11... | collective-permute-start | bytes 147464 | tf_op jit(solution)/shard_map/ppermute | solution.py:33
  2.9 4.6 %collective-permute-start.1 = (f32[3,4,1024]{2,1,0:T(4,128)S(1)}, f32[3,4,1024]{2,1,0:T(4,128)S(1)}, u32[]{:S(2)}, u32[]{:S(2)}) collective-permute-start(f32[3,4,1024]{2,1,0:T(4,128)S(1)} %get-tuple-element.25), channel_id=1, source_target_pairs={{1,2},{3,4},{5,6},{2,1},{4,3},{6,5},{9,10},{11,12},{13,14},{10,9},... | collective-permute-start | bytes 147464 | tf_op jit(solution)/shard_map/ppermute | solution.py:284
  4.2 0.7 %copy-start.5 = (s32[2]{0:T(128)S(1)}, s32[2]{0:T(128)}, u32[]{:S(2)}) copy-start(s32[2]{0:T(128)} %param.13) | copy-start | bytes 28
  4.9 0.7 %copy-start.6 = (s32[2]{0:T(128)S(1)}, s32[2]{0:T(128)}, u32[]{:S(2)}) copy-start(s32[2]{0:T(128)} %param.14) | copy-start | bytes 28
  5.6 0.7 %copy-start.7 = (s32[64]{0:T(128)S(1)}, s32[64]{0:T(128)}, u32[]{:S(2)}) copy-start(s32[64]{0:T(128)} %param.15) | copy-start | bytes 772
  6.2 0.7 %copy-start.4 = (f32[8]{0:T(128)S(1)}, f32[8]{0:T(128)}, u32[]{:S(2)}) copy-start(f32[8]{0:T(128)} %param.10) | copy-start | bytes 100
  11.9 9.1 %copy-start.3 = (f32[2,128]{1,0:T(2,128)S(1)}, f32[2,128]{1,0:T(2,128)}, u32[]{:S(2)}) copy-start(f32[2,128]{1,0:T(2,128)} %pad_maximum_fusion.2.par_ref) | copy-start | bytes 3076
  11.9 4.9 %collective-permute-start.2 = (f32[24,128]{1,0:T(8,128)}, f32[24,128]{1,0:T(8,128)S(1)}, u32[]{:S(2)}, u32[]{:S(2)}) collective-permute-start(f32[24,128]{1,0:T(8,128)} %get-tuple-element.11), channel_id=1, source_target_pairs={{0,1},{1,0},{2,3},{3,2},{4,5},{5,4},{6,7},{7,6},{8,9},{9,8},{10,11... | collective-permute-start | bytes 36872 | tf_op jit(solution)/shard_map/ppermute | solution.py:33
  17.5 4.6 %collective-permute-start.5 = (f32[24,128]{1,0:T(8,128)S(1)}, f32[24,128]{1,0:T(8,128)S(1)}, u32[]{:S(2)}, u32[]{:S(2)}) collective-permute-start(f32[24,128]{1,0:T(8,128)S(1)} %add.29), channel_id=1, source_target_pairs={{0,6},{1,7},{2,4},{3,5},{4,2},{5,3},{6,0},{7,1},{8,14},{9,15},{10,... | collective-permute-start | bytes 36872 | tf_op jit(solution)/shard_map/ppermute | solution.py:33
  19.3 3.7 %collective-permute-start.4 = (f32[24,128]{1,0:T(8,128)S(1)}, f32[24,128]{1,0:T(8,128)S(1)}, u32[]{:S(2)}, u32[]{:S(2)}) collective-permute-start(f32[24,128]{1,0:T(8,128)S(1)} %add.29), channel_id=1, source_target_pairs={{0,4},{1,5},{2,6},{3,7},{4,0},{5,1},{6,2},{7,3},{8,12},{9,13},{10,... | collective-permute-start | bytes 36872 | tf_op jit(solution)/shard_map/ppermute | solution.py:33
  20.5 3.7 %collective-permute-start.3 = (f32[24,128]{1,0:T(8,128)S(1)}, f32[24,128]{1,0:T(8,128)S(1)}, u32[]{:S(2)}, u32[]{:S(2)}) collective-permute-start(f32[24,128]{1,0:T(8,128)S(1)} %add.29), channel_id=1, source_target_pairs={{0,2},{1,3},{2,0},{3,1},{4,6},{5,7},{6,4},{7,5},{8,10},{9,11},{10,... | collective-permute-start | bytes 36872 | tf_op jit(solution)/shard_map/ppermute | solution.py:33
  27.1 5.3 %collective-permute-start.6 = (f32[72,256]{1,0:T(8,128)}, f32[72,256]{1,0:T(8,128)S(1)}, u32[]{:S(2)}, u32[]{:S(2)}) collective-permute-start(f32[72,256]{1,0:T(8,128)} %get-tuple-element.17), channel_id=1, source_target_pairs={{0,8},{8,0},{16,24},{24,16},{1,9},{9,1},{17,25},{25,17},{2,10},{10... | collective-permute-start | bytes 221192 | tf_op jit(solution)/shard_map/ppermute | solution.py:33
  28.6 7.1 %collective-permute-start.7 = (f32[72,256]{1,0:T(8,128)}, f32[72,256]{1,0:T(8,128)S(1)}, u32[]{:S(2)}, u32[]{:S(2)}) collective-permute-start(f32[72,256]{1,0:T(8,128)} %get-tuple-element.18), channel_id=1, source_target_pairs={{0,16},{8,24},{16,0},{24,8},{1,17},{9,25},{17,1},{25,9},{2,18},{10... | collective-permute-start | bytes 221192 | tf_op jit(solution)/shard_map/ppermute | solution.py:33
  31.2 6.4 %collective-permute-start.8 = (f32[72,256]{1,0:T(8,128)}, f32[72,256]{1,0:T(8,128)S(1)}, u32[]{:S(2)}, u32[]{:S(2)}) collective-permute-start(f32[72,256]{1,0:T(8,128)} %get-tuple-element.19), channel_id=1, source_target_pairs={{0,24},{8,16},{16,8},{24,0},{1,25},{9,17},{17,9},{25,1},{2,26},{10... | collective-permute-start | bytes 221192 | tf_op jit(solution)/shard_map/ppermute | solution.py:33
  32.3 5.2 %copy-start = (f32[72,256]{1,0:T(8,128)}, f32[72,256]{1,0:T(8,128)S(1)}, u32[]{:S(2)}) copy-start(f32[72,256]{1,0:T(8,128)S(1)} %collective-permute-done.6.refs_1_) | copy-start | bytes 221188
  35.7 1.9 %copy-start.1 = (f32[72,256]{1,0:T(8,128)}, f32[72,256]{1,0:T(8,128)S(1)}, u32[]{:S(2)}) copy-start(f32[72,256]{1,0:T(8,128)S(1)} %collective-permute-done.7.refs_2_) | copy-start | bytes 221188
  37.6 0.6 %copy-start.2 = (f32[72,256]{1,0:T(8,128)}, f32[72,256]{1,0:T(8,128)S(1)}, u32[]{:S(2)}) copy-start(f32[72,256]{1,0:T(8,128)S(1)} %collective-permute-done.8.refs_3_) | copy-start | bytes 221188

commit v3 on v2

--- a/solution.py
+++ b/solution.py
@@ -85,6 +85,7 @@
         in_specs=[spec] * len(inputs),
         out_specs=jax.tree.map(lambda _: spec, out_shape),
         scratch_shapes=list(scratch),
+        compiler_params=pltpu.CompilerParams(vmem_limit_bytes=16 << 20),
     )(*inputs)
 
 

time: 40.3 us -> 31.8 us (0.79)
  Pallas kernels: 7.57 us -> 2.71 us
  local copies, waits for them, and re-layouts: 4.21 us -> 1.13 us
  other arithmetic: 3.4 us -> 0.89 us
  starting transfers between devices: 12.9 us -> 14.3 us
  waiting for transfers between devices: 9.7 us -> 10.4 us
    pallas_call x3, Pallas kernels: 7.57 us -> 2.71 us  [vmem_call(): pl.pallas_call(kernel, out_shape=out_shape, in_specs=[spec] * len(inputs)...]
    unnamed x16 -> x12, local copies, waits for them, and re-layouts: 2.6 us -> 0.04 us
    ppermute x8, starting transfers between devices: 12.3 us -> 13.7 us  [swap(): return lax.ppermute(value, axis, [(i, i ^ mask) for i in range(size)])]
    add x2, other arithmetic: 1.31 us -> 0.01 us  [tree_sum(): values = [values[i] + values[i + 1] for i in range(0, len(values), 2)]]
    ppermute x8, waiting for transfers between devices: 9.7 us -> 10.4 us  [swap(): return lax.ppermute(value, axis, [(i, i ^ mask) for i in range(size)])]
    select_n x1, other arithmetic: 0.69 us -> 0.04 us  [shards(): jnp.where(even, jnp.concatenate([near, far], axis=1), jnp.concatenate([fa...]
    another operation x1, other arithmetic: 0.57 us -> 0.01 us  [shards(): jnp.stack([jnp.pad(params, (0, LANES - params.shape[0])), jnp.pad(electro...]
    slice x1, local copies, waits for them, and re-layouts: 0.63 us -> 0.07 us  [shards(): params[:, n_class + 1:n_class + 2]]
  transfers between devices with their start and end apart: 9 -> 9, of which waited for: 7 -> 7; matrix products, arithmetic and copies ran while one was open for 3% -> 1% of each run, Pallas kernels for 0% -> 0%
where the time goes in v3:
time: 31.8 us; the launch traced here: 31.5 us
  starting transfers between devices  14.3 us (45%)
  waiting for transfers between devices  10.4 us (33%)
  Pallas kernels  2.71 us (9%)
  between operations  2.12 us (7%)
  local copies, waits for them, and re-layouts  1.13 us (4%)
  other arithmetic  0.89 us (3%)
    ppermute x8, starting transfers between devices, swap(): return lax.ppermute(value, axis, [(i, i ^ mask) for i in range(size)])  13.7 us
    ppermute x8, waiting for transfers between devices, swap(): return lax.ppermute(value, axis, [(i, i ^ mask) for i in range(size)])  10.4 us
    pallas_call x3, Pallas kernels, vmem_call(): pl.pallas_call(kernel, out_shape=out_shape, in_specs=[spec] * len(inputs)...  2.71 us
    slice x1, local copies, waits for them, and re-layouts, rim(): return jnp.concatenate([field[:, at:at + halo], ids[None]], axis=0)  0.93 us
    broadcast_in_dim x1, other arithmetic, rim(): return jnp.concatenate([field[:, at:at + halo], ids[None]], axis=0)  0.79 us
    ppermute x1, starting transfers between devices, shards(): lax.ppermute(jnp.where(even, first, last), 'tile', far_pairs + [(j, i) fo...  0.65 us
  transfers between devices with their start and end apart: 9, of which 7 were waited for; matrix products, arithmetic and copies ran while one was open for 1% of the time, Pallas kernels for 0%

profile of v3, /device:TPU:0, one launch (start us, length us, event | category | flops | bytes accessed | tf_op | source)
XLA Modules:
  0.0 31.5 jit_solution(892557659976525581)
XLA Ops:
  0.6 0.8 %add_bitcast_fusion.1 = (f32[1,4,1024]{2,1,0:T(4,128)S(1)}, f32[1,4,1024]{2,1,0:T(4,128)S(1)}) fusion(s32[32,1024]{1,0:T(8,128)} %class_ref.1), kind=kLoop, calls=%fused_computation.6 | loop fusion | flops 16384 | bytes 65536 | tf_op jit(solution)/shard_map/broadcast_in_dim | solution.py:280
  1.4 0.0 copy-start
  1.4 0.9 %fusion.2 = (f32[2,4,1024]{2,1,0:T(4,128)S(1)}, f32[2,4,1024]{2,1,0:T(4,128)S(1)}) fusion(f32[2,32,1024]{2,1,0:T(8,128)} %bitcast.10), kind=kLoop, calls=%fused_computation.11 | loop fusion | bytes 131072 | tf_op jit(solution)/shard_map/slice | solution.py:280
  2.4 0.0 copy-start.3
  2.4 0.0 copy-start.4
  2.4 0.0 copy-start.5
  2.4 0.0 copy-start.2
  2.5 0.0 copy-start.1
  2.5 0.6 %collective-permute-start = (f32[3,4,1024]{2,1,0:T(4,128)S(1)}, f32[3,4,1024]{2,1,0:T(4,128)S(1)}, u32[]{:S(2)}, u32[]{:S(2)}) collective-permute-start(f32[3,4,1024]{2,1,0:T(4,128)S(1)} %get-tuple-element.24), channel_id=1, source_target_pairs={{0,1},{1,0},{2,3},{3,2},{4,5},{5,4},{6,7},{7,6},{8,9},{9,8},{10,11... | collective-permute-start | bytes 147464 | tf_op jit(solution)/shard_map/ppermute | solution.py:33
  3.0 0.7 %collective-permute-start.1 = (f32[3,4,1024]{2,1,0:T(4,128)S(1)}, f32[3,4,1024]{2,1,0:T(4,128)S(1)}, u32[]{:S(2)}, u32[]{:S(2)}) collective-permute-start(f32[3,4,1024]{2,1,0:T(4,128)S(1)} %get-tuple-element.25), channel_id=1, source_target_pairs={{1,2},{3,4},{5,6},{2,1},{4,3},{6,5},{9,10},{11,12},{13,14},{10,9},... | collective-permute-start | bytes 147464 | tf_op jit(solution)/shard_map/ppermute | solution.py:285
  5.0 0.0 copy-done.3
  5.0 0.0 copy-done.4
  5.0 0.0 copy-done.5
  5.1 0.0 copy-done.2
  5.1 0.1 concatenate.15
  5.2 0.0 collective-permute-done
  5.2 0.0 collective-permute-done.1
  5.2 0.0 copy-done
  5.2 0.0 copy-done.1
  5.3 1.8 %shard_map.95 = (f32[2,8,40,128]{3,2,1,0:T(8,128)S(1)}, f32[2,8,40,128]{3,2,1,0:T(8,128)S(1)}, f32[2,8,40,128]{3,2,1,0:T(8,128)S(1)}, f32[2,8,40,128]{3,2,1,0:T(8,128)S(1)}, f32[24,128]{1,0:T(8,128)S(1)}) custom-call(f32[2,128]{1,0:T(2,128)S(1)} %pad_maximum_fusion.2.par_ref, f32[2,32,1024]{2,1,0:T(8,128)S(1)} %bitcast.11, s32[32,1024]{1,0:T(8,128)S(1)} %copy-done.1, ...), custom_call_target="tpu_custom_call" | custom-call | tf_op jit(solution)/shard_map/pallas_call | solution.py:82
  7.0 4.2 %collective-permute-start.2 = (f32[24,128]{1,0:T(8,128)S(1)}, f32[24,128]{1,0:T(8,128)S(1)}, u32[]{:S(2)}, u32[]{:S(2)}) collective-permute-start(f32[24,128]{1,0:T(8,128)S(1)} %get-tuple-element.11), channel_id=1, source_target_pairs={{0,1},{1,0},{2,3},{3,2},{4,5},{5,4},{6,7},{7,6},{8,9},{9,8},{10,11... | collective-permute-start | bytes 36872 | tf_op jit(solution)/shard_map/ppermute | solution.py:33
  11.2 0.8 %collective-permute-done.2 = f32[24,128]{1,0:T(8,128)S(1)} collective-permute-done((f32[24,128]{1,0:T(8,128)S(1)}, f32[24,128]{1,0:T(8,128)S(1)}, u32[]{:S(2)}, u32[]{:S(2)}) %collective-permute-start.2) | collective-permute-done | bytes 12320 | tf_op jit(solution)/shard_map/ppermute | solution.py:33
  12.1 2.9 %collective-permute-start.5 = (f32[24,128]{1,0:T(8,128)S(1)}, f32[24,128]{1,0:T(8,128)S(1)}, u32[]{:S(2)}, u32[]{:S(2)}) collective-permute-start(f32[24,128]{1,0:T(8,128)S(1)} %add.29), channel_id=1, source_target_pairs={{0,6},{1,7},{2,4},{3,5},{4,2},{5,3},{6,0},{7,1},{8,14},{9,15},{10,... | collective-permute-start | bytes 36872 | tf_op jit(solution)/shard_map/ppermute | solution.py:33
  15.0 1.5 %collective-permute-start.4 = (f32[24,128]{1,0:T(8,128)S(1)}, f32[24,128]{1,0:T(8,128)S(1)}, u32[]{:S(2)}, u32[]{:S(2)}) collective-permute-start(f32[24,128]{1,0:T(8,128)S(1)} %add.29), channel_id=1, source_target_pairs={{0,4},{1,5},{2,6},{3,7},{4,0},{5,1},{6,2},{7,3},{8,12},{9,13},{10,... | collective-permute-start | bytes 36872 | tf_op jit(solution)/shard_map/ppermute | solution.py:33
  16.5 0.0 collective-permute-start.3
  16.5 0.1 slice.15.par_ref
  16.6 0.1 collective-permute-done.5
  16.7 2.0 %collective-permute-done.4 = f32[24,128]{1,0:T(8,128)S(1)} collective-permute-done((f32[24,128]{1,0:T(8,128)S(1)}, f32[24,128]{1,0:T(8,128)S(1)}, u32[]{:S(2)}, u32[]{:S(2)}) %collective-permute-start.4) | collective-permute-done | bytes 12320 | tf_op jit(solution)/shard_map/ppermute | solution.py:33
  18.7 1.5 %collective-permute-done.3 = f32[24,128]{1,0:T(8,128)S(1)} collective-permute-done((f32[24,128]{1,0:T(8,128)S(1)}, f32[24,128]{1,0:T(8,128)S(1)}, u32[]{:S(2)}, u32[]{:S(2)}) %collective-permute-start.3) | collective-permute-done | bytes 12320 | tf_op jit(solution)/shard_map/ppermute | solution.py:33
  20.2 0.3 shard_map.96
  20.5 1.6 %collective-permute-start.6 = (f32[72,256]{1,0:T(8,128)S(1)}, f32[72,256]{1,0:T(8,128)S(1)}, u32[]{:S(2)}, u32[]{:S(2)}) collective-permute-start(f32[72,256]{1,0:T(8,128)S(1)} %get-tuple-element.17), channel_id=1, source_target_pairs={{0,8},{8,0},{16,24},{24,16},{1,9},{9,1},{17,25},{25,17},{2,10},{10... | collective-permute-start | bytes 221192 | tf_op jit(solution)/shard_map/ppermute | solution.py:33
  22.2 2.6 %collective-permute-start.7 = (f32[72,256]{1,0:T(8,128)S(1)}, f32[72,256]{1,0:T(8,128)S(1)}, u32[]{:S(2)}, u32[]{:S(2)}) collective-permute-start(f32[72,256]{1,0:T(8,128)S(1)} %get-tuple-element.18), channel_id=1, source_target_pairs={{0,16},{8,24},{16,0},{24,8},{1,17},{9,25},{17,1},{25,9},{2,18},{10... | collective-permute-start | bytes 221192 | tf_op jit(solution)/shard_map/ppermute | solution.py:33
  24.7 0.2 collective-permute-start.8
  25.0 0.5 %collective-permute-done.6.refs_1_ = f32[72,256]{1,0:T(8,128)S(1)} collective-permute-done((f32[72,256]{1,0:T(8,128)S(1)}, f32[72,256]{1,0:T(8,128)S(1)}, u32[]{:S(2)}, u32[]{:S(2)}) %collective-permute-start.6) | collective-permute-done | bytes 73760 | tf_op jit(solution)/shard_map/ppermute | solution.py:33
  25.5 3.5 %collective-permute-done.7.refs_2_ = f32[72,256]{1,0:T(8,128)S(1)} collective-permute-done((f32[72,256]{1,0:T(8,128)S(1)}, f32[72,256]{1,0:T(8,128)S(1)}, u32[]{:S(2)}, u32[]{:S(2)}) %collective-permute-start.7) | collective-permute-done | bytes 73760 | tf_op jit(solution)/shard_map/ppermute | solution.py:33
  29.0 1.9 %collective-permute-done.8.refs_3_ = f32[72,256]{1,0:T(8,128)S(1)} collective-permute-done((f32[72,256]{1,0:T(8,128)S(1)}, f32[72,256]{1,0:T(8,128)S(1)}, u32[]{:S(2)}, u32[]{:S(2)}) %collective-permute-start.8) | collective-permute-done | bytes 73760 | tf_op jit(solution)/shard_map/ppermute | solution.py:33
  30.9 0.6 %shard_map.97 = (f32[2,32,256]{2,1,0:T(8,128)}, f32[2,64]{1,0:T(2,128)}) custom-call(f32[72,256]{1,0:T(8,128)S(1)} %get-tuple-element.16.refs_0_, f32[72,256]{1,0:T(8,128)S(1)} %collective-permute-done.6.refs_1_, f32[72,256]{1,0:T(8,128)S(1)} %collective-permute-done.7.refs_2_, f32[72,256]{1,0:T(8,128)S(1)} %collective-permute-done.8.refs_3_), custom_call_target="tpu_custom_call" | custom-call | tf_op jit(solution)/shard_map/pallas_call | solution.py:82
  (9 shorter events, 0.1 us)
Async XLA Ops:
  1.4 3.8 %copy-start = (f32[1,2,32,1024]{3,2,1,0:T(8,128)S(1)}, f32[1,2,32,1024]{3,2,1,0:T(8,128)}, u32[]{:S(2)}) copy-start(f32[1,2,32,1024]{3,2,1,0:T(8,128)} %param.8) | copy-start | bytes 786436
  2.4 2.6 %copy-start.3 = (s32[2]{0:T(128)S(1)}, s32[2]{0:T(128)}, u32[]{:S(2)}) copy-start(s32[2]{0:T(128)} %param.13) | copy-start | bytes 28
  2.4 2.6 %copy-start.4 = (s32[2]{0:T(128)S(1)}, s32[2]{0:T(128)}, u32[]{:S(2)}) copy-start(s32[2]{0:T(128)} %param.14) | copy-start | bytes 28
  2.4 2.6 %copy-start.5 = (s32[64]{0:T(128)S(1)}, s32[64]{0:T(128)}, u32[]{:S(2)}) copy-start(s32[64]{0:T(128)} %param.15) | copy-start | bytes 772
  2.4 2.6 %copy-start.2 = (f32[8]{0:T(128)S(1)}, f32[8]{0:T(128)}, u32[]{:S(2)}) copy-start(f32[8]{0:T(128)} %param.10) | copy-start | bytes 100
  2.5 2.8 %copy-start.1 = (s32[32,1024]{1,0:T(8,128)S(1)}, s32[32,1024]{1,0:T(8,128)}, u32[]{:S(2)}) copy-start(s32[32,1024]{1,0:T(8,128)} %class_ref.1) | copy-start | bytes 393220
  2.5 2.7 %collective-permute-start = (f32[3,4,1024]{2,1,0:T(4,128)S(1)}, f32[3,4,1024]{2,1,0:T(4,128)S(1)}, u32[]{:S(2)}, u32[]{:S(2)}) collective-permute-start(f32[3,4,1024]{2,1,0:T(4,128)S(1)} %get-tuple-element.24), channel_id=1, source_target_pairs={{0,1},{1,0},{2,3},{3,2},{4,5},{5,4},{6,7},{7,6},{8,9},{9,8},{10,11... | collective-permute-start | bytes 147464 | tf_op jit(solution)/shard_map/ppermute | solution.py:33
  3.0 2.1 %collective-permute-start.1 = (f32[3,4,1024]{2,1,0:T(4,128)S(1)}, f32[3,4,1024]{2,1,0:T(4,128)S(1)}, u32[]{:S(2)}, u32[]{:S(2)}) collective-permute-start(f32[3,4,1024]{2,1,0:T(4,128)S(1)} %get-tuple-element.25), channel_id=1, source_target_pairs={{1,2},{3,4},{5,6},{2,1},{4,3},{6,5},{9,10},{11,12},{13,14},{10,9},... | collective-permute-start | bytes 147464 | tf_op jit(solution)/shard_map/ppermute | solution.py:285
  7.0 5.0 %collective-permute-start.2 = (f32[24,128]{1,0:T(8,128)S(1)}, f32[24,128]{1,0:T(8,128)S(1)}, u32[]{:S(2)}, u32[]{:S(2)}) collective-permute-start(f32[24,128]{1,0:T(8,128)S(1)} %get-tuple-element.11), channel_id=1, source_target_pairs={{0,1},{1,0},{2,3},{3,2},{4,5},{5,4},{6,7},{7,6},{8,9},{9,8},{10,11... | collective-permute-start | bytes 36872 | tf_op jit(solution)/shard_map/ppermute | solution.py:33
  12.1 4.6 %collective-permute-start.5 = (f32[24,128]{1,0:T(8,128)S(1)}, f32[24,128]{1,0:T(8,128)S(1)}, u32[]{:S(2)}, u32[]{:S(2)}) collective-permute-start(f32[24,128]{1,0:T(8,128)S(1)} %add.29), channel_id=1, source_target_pairs={{0,6},{1,7},{2,4},{3,5},{4,2},{5,3},{6,0},{7,1},{8,14},{9,15},{10,... | collective-permute-start | bytes 36872 | tf_op jit(solution)/shard_map/ppermute | solution.py:33
  15.0 3.7 %collective-permute-start.4 = (f32[24,128]{1,0:T(8,128)S(1)}, f32[24,128]{1,0:T(8,128)S(1)}, u32[]{:S(2)}, u32[]{:S(2)}) collective-permute-start(f32[24,128]{1,0:T(8,128)S(1)} %add.29), channel_id=1, source_target_pairs={{0,4},{1,5},{2,6},{3,7},{4,0},{5,1},{6,2},{7,3},{8,12},{9,13},{10,... | collective-permute-start | bytes 36872 | tf_op jit(solution)/shard_map/ppermute | solution.py:33
  16.5 3.7 %collective-permute-start.3 = (f32[24,128]{1,0:T(8,128)S(1)}, f32[24,128]{1,0:T(8,128)S(1)}, u32[]{:S(2)}, u32[]{:S(2)}) collective-permute-start(f32[24,128]{1,0:T(8,128)S(1)} %add.29), channel_id=1, source_target_pairs={{0,2},{1,3},{2,0},{3,1},{4,6},{5,7},{6,4},{7,5},{8,10},{9,11},{10,... | collective-permute-start | bytes 36872 | tf_op jit(solution)/shard_map/ppermute | solution.py:33
  20.5 5.0 %collective-permute-start.6 = (f32[72,256]{1,0:T(8,128)S(1)}, f32[72,256]{1,0:T(8,128)S(1)}, u32[]{:S(2)}, u32[]{:S(2)}) collective-permute-start(f32[72,256]{1,0:T(8,128)S(1)} %get-tuple-element.17), channel_id=1, source_target_pairs={{0,8},{8,0},{16,24},{24,16},{1,9},{9,1},{17,25},{25,17},{2,10},{10... | collective-permute-start | bytes 221192 | tf_op jit(solution)/shard_map/ppermute | solution.py:33
  22.2 6.8 %collective-permute-start.7 = (f32[72,256]{1,0:T(8,128)S(1)}, f32[72,256]{1,0:T(8,128)S(1)}, u32[]{:S(2)}, u32[]{:S(2)}) collective-permute-start(f32[72,256]{1,0:T(8,128)S(1)} %get-tuple-element.18), channel_id=1, source_target_pairs={{0,16},{8,24},{16,0},{24,8},{1,17},{9,25},{17,1},{25,9},{2,18},{10... | collective-permute-start | bytes 221192 | tf_op jit(solution)/shard_map/ppermute | solution.py:33
  24.7 6.2 %collective-permute-start.8 = (f32[72,256]{1,0:T(8,128)S(1)}, f32[72,256]{1,0:T(8,128)S(1)}, u32[]{:S(2)}, u32[]{:S(2)}) collective-permute-start(f32[72,256]{1,0:T(8,128)S(1)} %get-tuple-element.19), channel_id=1, source_target_pairs={{0,24},{8,16},{16,8},{24,0},{1,25},{9,17},{17,9},{25,1},{2,26},{10... | collective-permute-start | bytes 221192 | tf_op jit(solution)/shard_map/ppermute | solution.py:33

commit v4 on v2

v4 whole, which is shorter than its diff:
```python
import functools

import jax
import jax.numpy as jnp
from jax import lax
from jax.experimental import pallas as pl
from jax.experimental.pallas import tpu as pltpu
from jax.sharding import PartitionSpec as P

ITERS = 3
SOURCE_STRENGTH = 50.0
TINY = 1e-30
LANES = 128
SUBLANES = 8


def harmonic(left_val, right_val):
    return 2.0 * left_val * right_val / jnp.maximum(left_val + right_val, TINY)


def safe_div(num, den):
    return jnp.where(den > 0.0, num / jnp.where(den > 0.0, den, 1.0), 0.0)


def tree_sum(values):
    values = list(values)
    while len(values) > 1:
        values = [values[i] + values[i + 1] for i in range(0, len(values), 2)]
    return values[0]


def swap(value, axis, mask, size):
    return lax.ppermute(value, axis, [(i, i ^ mask) for i in range(size)])


def tile_parts(value, axis):
    size = lax.axis_size(axis)
    parts = [value]
    bit = 1
    while bit < size:
        value = tree_sum(parts)
        masks = [bit]
        if bit > 1 and bit * 2 < size:
            masks.append(bit * 2)
        offsets = [0]
        for mask in masks:
            offsets += [o ^ mask for o in offsets]
        parts = [value] + [swap(value, axis, o, size) for o in offsets[1:]]
        bit = masks[-1] * 2
    return parts


def step_polynomial(moments):
    def inner(poly):
        return sum(a * b * moments[i + j] for i, a in enumerate(poly) for j, b in enumerate(poly))

    def energy(poly):
        return sum(
            a * b * (moments[i + j] - moments[i + j + 1])
            for i, a in enumerate(poly)
            for j, b in enumerate(poly)
        )

    one = jnp.ones_like(moments[0])
    zero = jnp.zeros_like(moments[0])
    res, way, total = [one], [one], [zero] * ITERS
    gamma = moments[0]
    for iteration in range(ITERS):
        alpha = safe_div(gamma, energy(way))
        total = [t + alpha * (way[i] if i < len(way) else zero) for i, t in enumerate(total)]
        if iteration + 1 < ITERS:
            longer = way + [zero]
            shifted = [zero] + way
            res = [r - alpha * (a - b) for r, a, b in zip(res + [zero], longer, shifted)]
            gamma_next = jnp.maximum(inner(res), 0.0)
            ratio = safe_div(gamma_next, gamma)
            way = [r + ratio * a for r, a in zip(res, longer)]
            gamma = gamma_next
    return total


VMEM = pl.BlockSpec(memory_space=pltpu.VMEM)
PARAMS = pltpu.CompilerParams(vmem_limit_bytes=16 << 20)


def vmem_call(kernel, out_shape, inputs, scratch=()):
    return pl.pallas_call(
        kernel,
        out_shape=out_shape,
        in_specs=[VMEM] * len(inputs),
        out_specs=jax.tree.map(lambda _: VMEM, out_shape),
        scratch_shapes=list(scratch),
        compiler_params=PARAMS,
    )(*inputs)


def cols(c):
    return slice(c * LANES, (c + 1) * LANES)


def add(sums, key, value):
    sums[key] = sums[key] + value if key in sums else value


def edge_kernel(field_hbm, class_hbm, far_ref, near_ref, field_ref, class_ref, sems):
    sources, rows, _ = field_hbm.shape
    halo = far_ref.shape[1]
    copies = []
    for i, at in enumerate((0, rows - SUBLANES)):
        copies.append(
            pltpu.make_async_copy(
                field_hbm.at[:, pl.ds(at, SUBLANES)], field_ref.at[i], sems.at[2 * i]
            )
        )
        copies.append(
            pltpu.make_async_copy(
                class_hbm.at[pl.ds(at, SUBLANES)], class_ref.at[i], sems.at[2 * i + 1]
            )
        )
    for copy in copies:
        copy.start()
    for copy in copies:
        copy.wait()
    even = lax.axis_index("tile") % 2 == 0
    spare = SUBLANES - halo
    for s in range(sources):
        first, last = field_ref[0, s, :halo], field_ref[1, s, spare:]
        far_ref[s] = jnp.where(even, first, last)
        near_ref[s] = jnp.where(even, last, first)
    first = class_ref[0, :halo].astype(jnp.float32) + 1.0
    last = class_ref[1, spare:].astype(jnp.float32) + 1.0
    far_ref[sources] = jnp.where(even, first, last)
    near_ref[sources] = jnp.where(even, last, first)


def from_left(value, other, lane):
    return jnp.where(lane == 0, pltpu.roll(other, 1, 1), pltpu.roll(value, 1, 1))


def from_right(value, other, lane):
    last = LANES - 1
    return jnp.where(lane == last, pltpu.roll(other, last, 1), pltpu.roll(value, last, 1))


def conductivity(ids, cond_ref):
    sigma = jnp.zeros(ids.shape, jnp.float32)
    for i in range(cond_ref.shape[1]):
        sigma = jnp.where(ids == i + 1.0, cond_ref[0:1, i : i + 1], sigma)
    return sigma


def west_faces(sigmas, lane):
    faces = []
    for c, sigma in enumerate(sigmas):
        face = harmonic(from_left(sigma, sigmas[c - 1], lane), sigma)
        faces.append(jnp.where(lane == 0, 0.0, face) if c == 0 else face)
    return faces


def diagonal(up, down, west, east, sigma, square, lane, bottom):
    diag = up + down + west + east + square * sigma
    if bottom:
        diag = diag + jnp.where(lane == LANES - 1, sigma, 0.0)
    return diag, 1.0 / jnp.maximum(diag, TINY)


def source_term(rows_at, lane, c, s, row_ref, col_ref, inverse):
    hit = (rows_at == row_ref[0:1, s : s + 1]) & (lane + c * LANES == col_ref[0:1, s : s + 1])
    return jnp.where(hit, SOURCE_STRENGTH * inverse, 0.0)


def line_sum(value):
    return jnp.sum(value, axis=0, keepdims=True)


def lines_of(tops, sums, sources):
    lines = list(tops)
    for n in range(2 * ITERS):
        for s in range(sources):
            lines.append(line_sum(sums[n, s]))
    return lines


def inner_kernel(
    field_ref, class_ref, cond_ref, wave_ref, row_ref, col_ref, pick_ref, *refs
):
    x_ref, *basis_refs = refs[: 1 + ITERS]
    pay_ref, sig_ref, face_ref = refs[1 + ITERS : 4 + ITERS]
    up_ref, down_ref, west_ref, east_ref, diag_ref, scaled_ref = refs[4 + ITERS :]
    sources, rows, _ = field_ref.shape
    chunks, total = x_ref.shape[1:3]
    halo = (total - rows) // 2
    lane = lax.broadcasted_iota(jnp.int32, (total, LANES), 1)
    row = lax.broadcasted_iota(jnp.int32, (total, LANES), 0)
    rows_at = row + (lax.axis_index("tile") * rows - halo)
    blank = jnp.zeros((halo, LANES), jnp.float32)
    square = wave_ref[...] * wave_ref[...]
    inner = slice(SUBLANES, total - SUBLANES)

    def widened(value):
        return jnp.concatenate([blank, value, blank], axis=0)

    for c in range(chunks):
        ids = class_ref[:, cols(c)].astype(jnp.float32) + 1.0
        sig_ref[c] = widened(conductivity(ids, cond_ref))
        for s in range(sources):
            x_ref[s, c] = widened(field_ref[s, :, cols(c)])
    for c in range(chunks):
        sigma = sig_ref[c]
        face = harmonic(from_left(sigma, sig_ref[c - 1 if c else chunks - 1], lane), sigma)
        west_ref[c] = jnp.where(lane == 0, 0.0, face) if c == 0 else face
    for c in range(chunks):
        sigma = sig_ref[c]
        up = harmonic(pltpu.roll(sigma, 1, 0), sigma)
        face_ref[c] = up
        down = pltpu.roll(up, total - 1, 0)
        east = from_right(west_ref[c], west_ref[(c + 1) % chunks], lane)
        diag, inverse = diagonal(
            up, down, west_ref[c], east, sigma, square, lane, c == chunks - 1
        )
        diag_ref[c] = diag
        up_ref[c] = up * inverse
        down_ref[c] = down * inverse
        for s in range(sources):
            basis_refs[0][s, c] = source_term(rows_at, lane, c, s, row_ref, col_ref, inverse)
        east_ref[c] = east * inverse
        scaled_ref[c] = west_ref[c] * inverse

    def spread(ref, s, c):
        here = ref[s, c]
        return (
            up_ref[c] * pltpu.roll(here, 1, 0)
            + down_ref[c] * pltpu.roll(here, total - 1, 0)
            + scaled_ref[c] * from_left(here, ref[s, c - 1 if c else chunks - 1], lane)
            + east_ref[c] * from_right(here, ref[s, (c + 1) % chunks], lane)
        )

    def fold(value):
        return sum(value[r : r + SUBLANES] for r in range(0, value.shape[0], SUBLANES))

    sums = {}
    for c in range(chunks):
        for s in range(sources):
            first = basis_refs[0][s, c] - (x_ref[s, c] - spread(x_ref, s, c))
            basis_refs[0][s, c] = first
            own = first[inner]
            add(sums, (0, s), fold(diag_ref[c, inner] * own * own))
    for i in range(ITERS):
        for c in range(chunks):
            for s in range(sources):
                new = spread(basis_refs[i], s, c)
                own = new[inner]
                weighted = diag_ref[c, inner] * own
                add(sums, (2 * i + 1, s), fold(weighted * basis_refs[i][s, c, inner]))
                if i + 1 < ITERS:
                    basis_refs[i + 1][s, c] = new
                    add(sums, (2 * i + 2, s), fold(weighted * own))
    picker = rows_at[inner] == pick_ref[...]
    tops = []
    for ref in (x_ref, *basis_refs):
        for s in range(sources):
            top = jnp.broadcast_to(ref[s, 0, inner, 0:1], (total - 2 * SUBLANES, LANES))
            tops.append(line_sum(fold(jnp.where(picker, top, 0.0))))
    pay_ref[...] = jnp.zeros(pay_ref.shape, jnp.float32)
    for i, line in enumerate(lines_of(tops, sums, sources)):
        pay_ref[i : i + 1, :] = line


def outer_kernel(
    far_ref, near_ref, cond_ref, wave_ref, row_ref, col_ref, pick_ref, *refs
):
    x_in, *basis_in = refs[: 1 + ITERS]
    pay_in, sig_in, face_in = refs[1 + ITERS : 4 + ITERS]
    outs = refs[4 + ITERS :]
    x_ref, *basis_refs = outs[: 1 + ITERS]
    pay_ref = outs[1 + ITERS]
    up_ref, down_ref, west_ref, east_ref, diag_ref = outs[2 + ITERS :]
    sources, chunks, total, _ = x_in.shape
    halo = far_ref.shape[1]
    rows = total - 2 * halo
    lane = lax.broadcasted_iota(jnp.int32, (SUBLANES, LANES), 1)
    row = lax.broadcasted_iota(jnp.int32, (SUBLANES, LANES), 0)
    tile = lax.axis_index("tile")
    even = tile % 2 == 0
    square = wave_ref[...] * wave_ref[...]
    ends = (0, 1)
    starts = (0, total - SUBLANES)
    own = (row >= halo, row < SUBLANES - halo)
    rows_at = [row + (tile * rows - halo + at) for at in starts]

    def edge(index, c, inside):
        far, near = far_ref[index, :, cols(c)], near_ref[index, :, cols(c)]
        before, after = jnp.where(even, far, near), jnp.where(even, near, far)
        return (
            jnp.concatenate([before, inside[0]], axis=0),
            jnp.concatenate([inside[1], after], axis=0),
        )

    inside = (slice(halo, SUBLANES), slice(total - SUBLANES, total - halo))
    sigmas = []
    for c in range(chunks):
        both = edge(sources, c, [jnp.zeros((SUBLANES - halo, LANES), jnp.float32)] * 2)
        kept = (sig_in[c, :SUBLANES], sig_in[c, total - SUBLANES :])
        sigmas.append(
            [jnp.where(own[e], kept[e], conductivity(both[e], cond_ref)) for e in ends]
        )
        for s in range(sources):
            both = edge(s, c, [x_in[s, c, i] for i in inside])
            for e in ends:
                x_ref[e, s, c] = both[e]
    west = [west_faces([sigmas[c][e] for c in range(chunks)], lane) for e in ends]
    last = total - SUBLANES
    for c in range(chunks):
        for e in ends:
            sigma = sigmas[c][e]
            above = pltpu.roll(sigma, 1, 0)
            if e:
                above = jnp.where(row == 0, pltpu.roll(sig_in[c, last - SUBLANES : last], 1, 0), above)
            up = harmonic(above, sigma)
            down = pltpu.roll(up, SUBLANES - 1, 0)
            if not e:
                down = jnp.where(
                    row == SUBLANES - 1,
                    pltpu.roll(face_in[c, SUBLANES : 2 * SUBLANES], SUBLANES - 1, 0),
                    down,
                )
            east = from_right(west[e][c], west[e][(c + 1) % chunks], lane)
            diag, inverse = diagonal(
                up, down, west[e][c], east, sigma, square, lane, c == chunks - 1
            )
            diag_ref[e, c] = jnp.where(own[e], diag, 0.0)
            up_ref[e, c] = up * inverse
            down_ref[e, c] = down * inverse
            west_ref[e, c] = west[e][c] * inverse
            east_ref[e, c] = east * inverse
            for s in range(sources):
                basis_refs[0][e, s, c] = source_term(
                    rows_at[e], lane, c, s, row_ref, col_ref, inverse
                )

    def spread(ref, whole, e, s, c):
        here = ref[e, s, c]
        above = pltpu.roll(here, 1, 0)
        below = pltpu.roll(here, SUBLANES - 1, 0)
        if e:
            above = jnp.where(
                row == 0, pltpu.roll(whole[s, c, last - SUBLANES : last], 1, 0), above
            )
        else:
            below = jnp.where(
                row == SUBLANES - 1,
                pltpu.roll(whole[s, c, SUBLANES : 2 * SUBLANES], SUBLANES - 1, 0),
                below,
            )
        return (
            up_ref[e, c] * above
            + down_ref[e, c] * below
            + west_ref[e, c] * from_left(here, ref[e, s, c - 1 if c else chunks - 1], lane)
            + east_ref[e, c] * from_right(here, ref[e, s, (c + 1) % chunks], lane)
        )

    sums = {}
    for c in range(chunks):
        for e in ends:
            for s in range(sources):
                first = basis_refs[0][e, s, c] - (x_ref[e, s, c] - spread(x_ref, x_in, e, s, c))
                basis_refs[0][e, s, c] = first
                add(sums, (0, s), diag_ref[e, c] * first * first)
    for i in range(ITERS):
        for c in range(chunks):
            for e in ends:
                for s in range(sources):
                    new = spread(basis_refs[i], basis_in[i], e, s, c)
                    weighted = diag_ref[e, c] * new
                    add(sums, (2 * i + 1, s), weighted * basis_refs[i][e, s, c])
                    if i + 1 < ITERS:
                        basis_refs[i + 1][e, s, c] = new
                        add(sums, (2 * i + 2, s), weighted * new)
    tops = []
    for ref in (x_ref, *basis_refs):
        for s in range(sources):
            line = 0.0
            for e in ends:
                picker = own[e] & (rows_at[e] == pick_ref[...])
                top = jnp.broadcast_to(ref[e, s, 0, :, 0:1], (SUBLANES, LANES))
                line = line + jnp.where(picker, top, 0.0)
            tops.append(line_sum(line))
    pay_ref[...] = pay_in[...]
    for i, line in enumerate(lines_of(tops, sums, sources)):
        pay_ref[i : i + 1, :] += line


def combine_kernel(n_pay, weight_ref, *refs):
    n_parts = ITERS + 1
    packed = tree_sum([r[...] for r in refs[:n_pay]])
    part_refs = refs[n_pay : n_pay + n_parts]
    edge_refs = refs[n_pay + n_parts : n_pay + 2 * n_parts]
    out_refs = refs[n_pay + 2 * n_parts :]
    sources, _, total, _ = part_refs[0].shape
    share = out_refs[0].shape[1]
    rows = (out_refs[0].shape[0] - SUBLANES) // sources
    halo = (total - rows) // 2
    first = n_parts * sources
    totals = jnp.sum(packed[first : first + 2 * ITERS * sources], axis=1, keepdims=True)
    poly = step_polynomial([totals[n * sources : (n + 1) * sources] for n in range(2 * ITERS)])
    weight = weight_ref[...]
    scale = [[weight] + [weight * p[s : s + 1] for p in poly] for s in range(sources)]
    read = [
        sum(scale[s][i] * packed[i * sources + s : i * sources + s + 1] for i in range(n_parts))
        for s in range(sources)
    ]
    split = len(out_refs) > 1
    wave = lax.axis_index("wave") if split else 0
    per = share // LANES
    inner = slice(SUBLANES, total - SUBLANES)
    for mask, out_ref in enumerate(out_refs):
        block = wave ^ mask if split else 0
        for s in range(sources):
            for k in range(per):
                c = block * per + k
                middle = sum(scale[s][i] * part_refs[i][s, c, inner] for i in range(n_parts))
                top, end = (
                    sum(scale[s][i] * edge_refs[i][e, s, c] for i in range(n_parts)) for e in (0, 1)
                )
                value = jnp.concatenate([top[halo:], middle, end[: SUBLANES - halo]], axis=0)
                out_ref[s * rows : (s + 1) * rows, cols(k)] = value
        out_ref[sources * rows :, :] = jnp.zeros((SUBLANES, share), jnp.float32)
        for s in range(sources):
            out_ref[sources * rows + s : sources * rows + s + 1, :LANES] = read[s]


def sum_kernel(*refs):
    part_refs, (field_ref, read_ref) = refs[:-2], refs[-2:]
    sources, rows, _ = field_ref.shape
    electrodes = read_ref.shape[1]
    for s in range(sources):
        field_ref[s] = tree_sum([r[s * rows : (s + 1) * rows, :] for r in part_refs])
    last = tree_sum([r[sources * rows :, :LANES] for r in part_refs])
    read_ref[...] = last[:sources, :electrodes]


def shards(
    warm_start,
    class_map,
    conductivities,
    wavenumbers,
    weights,
    source_row,
    source_col,
    electrode_row,
):
    rows, depth = class_map.shape
    sources = warm_start.shape[1]
    electrodes = electrode_row.shape[0]
    tiles, waves = lax.axis_size("tile"), lax.axis_size("wave")
    wave = lax.axis_index("wave")
    halo = ITERS + 1
    field = warm_start[0]
    f32 = jnp.float32
    rim = jax.ShapeDtypeStruct((sources + 1, halo, depth), f32)
    hbm = pl.BlockSpec(memory_space=pltpu.HBM)
    far, near = pl.pallas_call(
        edge_kernel,
        out_shape=[rim, rim],
        in_specs=[hbm, hbm],
        out_specs=[VMEM, VMEM],
        scratch_shapes=[
            pltpu.VMEM((2, sources, SUBLANES, depth), f32),
            pltpu.VMEM((2, SUBLANES, depth), jnp.int32),
            pltpu.SemaphoreType.DMA((4,)),
        ],
        compiler_params=PARAMS,
    )(field, class_map)
    far_pairs = [(i, i + 1) for i in range(1, tiles - 1, 2)]
    far = lax.ppermute(far, "tile", far_pairs + [(j, i) for i, j in far_pairs])
    near = swap(near, "tile", 1, tiles)
    total, chunks = rows + 2 * halo, depth // LANES
    small = [
        conductivities[None],
        wavenumbers[None],
        source_row[None],
        source_col[None],
        jnp.pad(electrode_row, (0, LANES - electrodes), constant_values=-1)[None],
    ]
    wide = jax.ShapeDtypeStruct((sources, chunks, total, LANES), f32)
    flat = jax.ShapeDtypeStruct((chunks, total, LANES), f32)
    n_lines = sources * (3 * ITERS + 1)
    pay = jax.ShapeDtypeStruct((-(-n_lines // SUBLANES) * SUBLANES, LANES), f32)
    inside = vmem_call(
        inner_kernel,
        [wide] * (ITERS + 1) + [pay, flat, flat],
        [field, class_map, *small],
        [pltpu.VMEM((chunks, total, LANES), f32)] * 6,
    )
    ends = jax.ShapeDtypeStruct((2, sources, chunks, SUBLANES, LANES), f32)
    outside = vmem_call(
        outer_kernel,
        [ends] * (ITERS + 1) + [pay],
        [far, near, *small, *inside],
        [pltpu.VMEM((2, chunks, SUBLANES, LANES), f32)] * 5,
    )
    packed = tile_parts(outside[-1], "tile")
    share = depth // waves
    split = share % LANES == 0
    width = share if split else depth
    block = jax.ShapeDtypeStruct((sources * rows + SUBLANES, width), f32)
    pieces = vmem_call(
        functools.partial(combine_kernel, len(packed)),
        [block] * (waves if split else 1),
        [weights[None], *packed, *inside[: ITERS + 1], *outside[: ITERS + 1]],
    )
    if not split:
        n = sources * rows
        read = pieces[0][n : n + sources, :electrodes].reshape(-1, share)
        pieces = [
            jnp.concatenate(
                [lax.dynamic_slice_in_dim(pieces[0][:n], (wave ^ mask) * share, share, 1), read]
            )
            for mask in range(waves)
        ]
    pieces = [pieces[0]] + [swap(pieces[m], "wave", m, waves) for m in range(1, waves)]
    if not split:
        final = tree_sum(pieces)
        return (
            final[: sources * rows].reshape(sources, rows, share),
            final[sources * rows :].reshape(sources, electrodes),
        )
    return tuple(
        vmem_call(
            sum_kernel,
            [
                jax.ShapeDtypeStruct((sources, rows, share), f32),
                jax.ShapeDtypeStruct((sources, electrodes), f32),
            ],
            pieces,
        )
    )


def solution(mesh):
    return jax.shard_map(
        shards,
        mesh=mesh,
        in_specs=(
            P("wave", None, "tile", None),
            P("tile", None),
            P(),
            P("wave"),
            P("wave"),
            P(),
            P(),
            P(),
        ),
        out_specs=(P(None, "tile", "wave"), P()),
        check_vma=False,
    )
```

time: 40.3 us -> 31.6 us (0.78)
  other arithmetic: 3.4 us -> 0.01 us
  Pallas kernels: 7.57 us -> 4.2 us
  local copies, waits for them, and re-layouts: 4.21 us -> 2.52 us
    pallas_call x3 -> x5, Pallas kernels: 7.57 us -> 4.2 us  [the longest x4 3.98 us: vmem_call(): pl.pallas_call(kernel, out_shape=out_shape, in_specs=[VMEM] * len(inputs)...]
    slice x2 -> x0, local copies, waits for them, and re-layouts: 1.52 us -> none  [the longest x1 0.89 us: rim(): return jnp.concatenate([field[:, at:at + halo], ids[None]], axis=0)]
    add x2 -> x1, other arithmetic: 1.31 us -> 0.01 us  [tree_sum(): values = [values[i] + values[i + 1] for i in range(0, len(values), 2)]]
    broadcast_in_dim x1 -> x0, other arithmetic: 0.79 us -> none  [rim(): return jnp.concatenate([field[:, at:at + halo], ids[None]], axis=0)]
    select_n x2 -> x0, other arithmetic: 0.71 us -> none  [the longest x1 0.69 us: shards(): jnp.where(even, jnp.concatenate([near, far], axis=1), jnp.concatenate([fa...]
    another operation x1 -> x0, other arithmetic: 0.57 us -> none  [shards(): jnp.stack([jnp.pad(params, (0, LANES - params.shape[0])), jnp.pad(electro...]
    unnamed x16 -> x12, local copies, waits for them, and re-layouts: 2.6 us -> 2.52 us
  transfers between devices with their start and end apart: 9 -> 9, of which waited for: 7 -> 6; matrix products, arithmetic and copies ran while one was open for 3% -> 0% of each run, Pallas kernels for 0% -> 6%
where the time goes in v4:
time: 31.6 us; the launch traced here: 31.4 us
  starting transfers between devices  13.1 us (41%)
  waiting for transfers between devices  9.58 us (30%)
  Pallas kernels  4.2 us (13%)
  local copies, waits for them, and re-layouts  2.52 us (8%)
  between operations  2.04 us (6%)
    ppermute x8, starting transfers between devices, swap(): return lax.ppermute(value, axis, [(i, i ^ mask) for i in range(size)])  12.4 us
    ppermute x8, waiting for transfers between devices, swap(): return lax.ppermute(value, axis, [(i, i ^ mask) for i in range(size)])  9.58 us
    pallas_call x4, Pallas kernels, vmem_call(): pl.pallas_call(kernel, out_shape=out_shape, in_specs=[VMEM] * len(inputs)...  3.98 us
    unnamed x12, local copies, waits for them, and re-layouts  2.52 us
    ppermute x1, starting transfers between devices, shards(): far = lax.ppermute(far, 'tile', far_pairs + [(j, i) for i, j in far_pairs])  0.66 us
  transfers between devices with their start and end apart: 9, of which 6 were waited for; matrix products, arithmetic and copies ran while one was open for 0% of the time, Pallas kernels for 6%

profile of v4, /device:TPU:0, one launch (start us, length us, event | category | flops | bytes accessed | tf_op | source)
XLA Modules:
  0.0 31.4 jit_solution(14419463284237256835)
XLA Ops:
  0.6 0.0 copy-start
  0.6 0.9 %copy-done = f32[1,2,32,1024]{3,2,1,0:T(8,128)S(1)} copy-done((f32[1,2,32,1024]{3,2,1,0:T(8,128)S(1)}, f32[1,2,32,1024]{3,2,1,0:T(8,128)}, u32[]{:S(2)}) %copy-start) | copy-done | bytes 262168
  1.6 0.0 copy-start.1
  1.6 0.9 %copy-done.1 = s32[32,1024]{1,0:T(8,128)S(1)} copy-done((s32[32,1024]{1,0:T(8,128)S(1)}, s32[32,1024]{1,0:T(8,128)}, u32[]{:S(2)}) %copy-start.1) | copy-done | bytes 131096
  2.5 0.2 shard_map.95
  2.7 0.0 copy-start.5
  2.7 0.7 %collective-permute-start = (f32[3,4,1024]{2,1,0:T(4,128)S(1)}, f32[3,4,1024]{2,1,0:T(4,128)S(1)}, u32[]{:S(2)}, u32[]{:S(2)}) collective-permute-start(f32[3,4,1024]{2,1,0:T(4,128)S(1)} %get-tuple-element.20), channel_id=1, source_target_pairs={{1,2},{3,4},{5,6},{2,1},{4,3},{6,5},{9,10},{11,12},{13,14},{10,9},... | collective-permute-start | bytes 147464 | tf_op jit(solution)/shard_map/ppermute | solution.py:475
  3.4 4.4 %collective-permute-start.1 = (f32[3,4,1024]{2,1,0:T(4,128)S(1)}, f32[3,4,1024]{2,1,0:T(4,128)S(1)}, u32[]{:S(2)}, u32[]{:S(2)}) collective-permute-start(f32[3,4,1024]{2,1,0:T(4,128)S(1)} %get-tuple-element.21), channel_id=1, source_target_pairs={{0,1},{1,0},{2,3},{3,2},{4,5},{5,4},{6,7},{7,6},{8,9},{9,8},{10,11... | collective-permute-start | bytes 147464 | tf_op jit(solution)/shard_map/ppermute | solution.py:33
  7.8 0.0 copy-done.5
  8.4 0.0 copy-start.2
  8.5 0.0 copy-start.3
  8.5 0.0 copy-start.4
  8.5 0.6 %copy-done.2 = f32[8]{0:T(128)S(1)} copy-done((f32[8]{0:T(128)S(1)}, f32[8]{0:T(128)}, u32[]{:S(2)}) %copy-start.2) | copy-done | bytes 56
  9.1 0.0 copy-done.3
  9.1 0.0 copy-done.4
  9.1 1.9 %shard_map.96 = (f32[2,8,40,128]{3,2,1,0:T(8,128)S(1)}, f32[2,8,40,128]{3,2,1,0:T(8,128)S(1)}, f32[2,8,40,128]{3,2,1,0:T(8,128)S(1)}, f32[2,8,40,128]{3,2,1,0:T(...) custom-call(f32[2,32,1024]{2,1,0:T(8,128)S(1)} %bitcast.12, ...), custom_call_target="tpu_custom_call" | custom-call | tf_op jit(solution)/shard_map/pallas_call | solution.py:87
  11.0 0.0 collective-permute-done.far_ref
  11.0 0.0 collective-permute-done.1.near_ref
  11.1 1.1 %shard_map.97 = (f32[2,2,8,8,128]{4,3,2,1,0:T(8,128)S(1)}, f32[2,2,8,8,128]{4,3,2,1,0:T(8,128)S(1)}, f32[2,2,8,8,128]{4,3,2,1,0:T(8,128)S(1)}, f32[2,2,8,8,128]{4,3,2,1,0:T(8,128)S(1)}, f32[24,128]{1,0:T(8,128)S(1)}) custom-call(f32[3,4,1024]{2,1,0:T(4,128)S(1)} %collective-permute-done.far_ref, f32[3,4,1024]{2,1,0:T(4,128)S(1)} %collective-permute-done.1.near_ref, ...), custom_call_target="tpu_custom_call" | custom-call | tf_op jit(solution)/shard_map/pallas_call | solution.py:87
  12.2 0.1 collective-permute-start.2
  12.2 1.2 %collective-permute-done.2 = f32[24,128]{1,0:T(8,128)S(1)} collective-permute-done((f32[24,128]{1,0:T(8,128)S(1)}, f32[24,128]{1,0:T(8,128)S(1)}, u32[]{:S(2)}, u32[]{:S(2)}) %collective-permute-start.2) | collective-permute-done | bytes 12320 | tf_op jit(solution)/shard_map/ppermute | solution.py:33
  13.4 1.5 %collective-permute-start.3 = (f32[24,128]{1,0:T(8,128)S(1)}, f32[24,128]{1,0:T(8,128)S(1)}, u32[]{:S(2)}, u32[]{:S(2)}) collective-permute-start(f32[24,128]{1,0:T(8,128)S(1)} %add.5.refs_0_), channel_id=1, source_target_pairs={{0,2},{1,3},{2,0},{3,1},{4,6},{5,7},{6,4},{7,5},{8,10},{9,11},{10,... | collective-permute-start | bytes 36872 | tf_op jit(solution)/shard_map/ppermute | solution.py:33
  14.9 0.6 %collective-permute-start.4 = (f32[24,128]{1,0:T(8,128)S(1)}, f32[24,128]{1,0:T(8,128)S(1)}, u32[]{:S(2)}, u32[]{:S(2)}) collective-permute-start(f32[24,128]{1,0:T(8,128)S(1)} %add.5.refs_0_), channel_id=1, source_target_pairs={{0,4},{1,5},{2,6},{3,7},{4,0},{5,1},{6,2},{7,3},{8,12},{9,13},{10,... | collective-permute-start | bytes 36872 | tf_op jit(solution)/shard_map/ppermute | solution.py:33
  15.5 1.4 %collective-permute-start.5 = (f32[24,128]{1,0:T(8,128)S(1)}, f32[24,128]{1,0:T(8,128)S(1)}, u32[]{:S(2)}, u32[]{:S(2)}) collective-permute-start(f32[24,128]{1,0:T(8,128)S(1)} %add.5.refs_0_), channel_id=1, source_target_pairs={{0,6},{1,7},{2,4},{3,5},{4,2},{5,3},{6,0},{7,1},{8,14},{9,15},{10,... | collective-permute-start | bytes 36872 | tf_op jit(solution)/shard_map/ppermute | solution.py:33
  17.5 0.0 collective-permute-done.3.refs_1_
  17.6 1.0 %collective-permute-done.4.refs_2_ = f32[24,128]{1,0:T(8,128)S(1)} collective-permute-done((f32[24,128]{1,0:T(8,128)S(1)}, f32[24,128]{1,0:T(8,128)S(1)}, u32[]{:S(2)}, u32[]{:S(2)}) %collective-permute-start.4) | collective-permute-done | bytes 12320 | tf_op jit(solution)/shard_map/ppermute | solution.py:33
  18.6 1.4 %collective-permute-done.5.refs_3_ = f32[24,128]{1,0:T(8,128)S(1)} collective-permute-done((f32[24,128]{1,0:T(8,128)S(1)}, f32[24,128]{1,0:T(8,128)S(1)}, u32[]{:S(2)}, u32[]{:S(2)}) %collective-permute-start.5) | collective-permute-done | bytes 12320 | tf_op jit(solution)/shard_map/ppermute | solution.py:33
  20.0 0.3 %shard_map.98 = (f32[72,256]{1,0:T(8,128)S(1)}, f32[72,256]{1,0:T(8,128)S(1)}, f32[72,256]{1,0:T(8,128)S(1)}, f32[72,256]{1,0:T(8,128)S(1)}) custom-call(f32[1,1]{1,0:T(1,128)} %bitcast.10.weight_ref, f32[24,128]{1,0:T(8,128)S(1)} %add.5.refs_0_, f32[24,128]{1,0:T(8,128)S(1)} %collective-permute-done.3.refs_1_, ...), custom_call_target="tpu_custom_call" | custom-call | tf_op jit(solution)/shard_map/pallas_call | solution.py:87
  20.4 1.6 %collective-permute-start.6 = (f32[72,256]{1,0:T(8,128)S(1)}, f32[72,256]{1,0:T(8,128)S(1)}, u32[]{:S(2)}, u32[]{:S(2)}) collective-permute-start(f32[72,256]{1,0:T(8,128)S(1)} %get-tuple-element.35), channel_id=1, source_target_pairs={{0,8},{8,0},{16,24},{24,16},{1,9},{9,1},{17,25},{25,17},{2,10},{10... | collective-permute-start | bytes 221192 | tf_op jit(solution)/shard_map/ppermute | solution.py:33
  22.0 2.6 %collective-permute-start.7 = (f32[72,256]{1,0:T(8,128)S(1)}, f32[72,256]{1,0:T(8,128)S(1)}, u32[]{:S(2)}, u32[]{:S(2)}) collective-permute-start(f32[72,256]{1,0:T(8,128)S(1)} %get-tuple-element.36), channel_id=1, source_target_pairs={{0,16},{8,24},{16,0},{24,8},{1,17},{9,25},{17,1},{25,9},{2,18},{10... | collective-permute-start | bytes 221192 | tf_op jit(solution)/shard_map/ppermute | solution.py:33
  24.6 0.2 collective-permute-start.8
  24.8 0.4 %collective-permute-done.6.refs_1_ = f32[72,256]{1,0:T(8,128)S(1)} collective-permute-done((f32[72,256]{1,0:T(8,128)S(1)}, f32[72,256]{1,0:T(8,128)S(1)}, u32[]{:S(2)}, u32[]{:S(2)}) %collective-permute-start.6) | collective-permute-done | bytes 73760 | tf_op jit(solution)/shard_map/ppermute | solution.py:33
  25.3 3.6 %collective-permute-done.7.refs_2_ = f32[72,256]{1,0:T(8,128)S(1)} collective-permute-done((f32[72,256]{1,0:T(8,128)S(1)}, f32[72,256]{1,0:T(8,128)S(1)}, u32[]{:S(2)}, u32[]{:S(2)}) %collective-permute-start.7) | collective-permute-done | bytes 73760 | tf_op jit(solution)/shard_map/ppermute | solution.py:33
  28.9 1.9 %collective-permute-done.8.refs_3_ = f32[72,256]{1,0:T(8,128)S(1)} collective-permute-done((f32[72,256]{1,0:T(8,128)S(1)}, f32[72,256]{1,0:T(8,128)S(1)}, u32[]{:S(2)}, u32[]{:S(2)}) %collective-permute-start.8) | collective-permute-done | bytes 73760 | tf_op jit(solution)/shard_map/ppermute | solution.py:33
  30.8 0.6 %shard_map.99 = (f32[2,32,256]{2,1,0:T(8,128)}, f32[2,64]{1,0:T(2,128)}) custom-call(f32[72,256]{1,0:T(8,128)S(1)} %get-tuple-element.34.refs_0_, f32[72,256]{1,0:T(8,128)S(1)} %collective-permute-done.6.refs_1_, f32[72,256]{1,0:T(8,128)S(1)} %collective-permute-done.7.refs_2_, f32[72,256]{1,0:T(8,128)S(1)} %collective-permute-done.8.refs_3_), custom_call_target="tpu_custom_call" | custom-call | tf_op jit(solution)/shard_map/pallas_call | solution.py:87
  (2 shorter events, 0.0 us)
Async XLA Ops:
  0.6 1.0 %copy-start = (f32[1,2,32,1024]{3,2,1,0:T(8,128)S(1)}, f32[1,2,32,1024]{3,2,1,0:T(8,128)}, u32[]{:S(2)}) copy-start(f32[1,2,32,1024]{3,2,1,0:T(8,128)} %param.8) | copy-start | bytes 786436
  1.6 0.9 %copy-start.1 = (s32[32,1024]{1,0:T(8,128)S(1)}, s32[32,1024]{1,0:T(8,128)}, u32[]{:S(2)}) copy-start(s32[32,1024]{1,0:T(8,128)} %class_ref.1) | copy-start | bytes 393220
  2.7 5.1 %copy-start.5 = (s32[64]{0:T(128)S(1)}, s32[64]{0:T(128)}, u32[]{:S(2)}) copy-start(s32[64]{0:T(128)} %param.15) | copy-start | bytes 772
  2.7 8.3 %collective-permute-start = (f32[3,4,1024]{2,1,0:T(4,128)S(1)}, f32[3,4,1024]{2,1,0:T(4,128)S(1)}, u32[]{:S(2)}, u32[]{:S(2)}) collective-permute-start(f32[3,4,1024]{2,1,0:T(4,128)S(1)} %get-tuple-element.20), channel_id=1, source_target_pairs={{1,2},{3,4},{5,6},{2,1},{4,3},{6,5},{9,10},{11,12},{13,14},{10,9},... | collective-permute-start | bytes 147464 | tf_op jit(solution)/shard_map/ppermute | solution.py:475
  3.4 7.6 %collective-permute-start.1 = (f32[3,4,1024]{2,1,0:T(4,128)S(1)}, f32[3,4,1024]{2,1,0:T(4,128)S(1)}, u32[]{:S(2)}, u32[]{:S(2)}) collective-permute-start(f32[3,4,1024]{2,1,0:T(4,128)S(1)} %get-tuple-element.21), channel_id=1, source_target_pairs={{0,1},{1,0},{2,3},{3,2},{4,5},{5,4},{6,7},{7,6},{8,9},{9,8},{10,11... | collective-permute-start | bytes 147464 | tf_op jit(solution)/shard_map/ppermute | solution.py:33
  8.4 0.7 %copy-start.2 = (f32[8]{0:T(128)S(1)}, f32[8]{0:T(128)}, u32[]{:S(2)}) copy-start(f32[8]{0:T(128)} %param.10) | copy-start | bytes 100
  8.5 0.7 %copy-start.3 = (s32[2]{0:T(128)S(1)}, s32[2]{0:T(128)}, u32[]{:S(2)}) copy-start(s32[2]{0:T(128)} %param.13) | copy-start | bytes 28
  8.5 0.7 %copy-start.4 = (s32[2]{0:T(128)S(1)}, s32[2]{0:T(128)}, u32[]{:S(2)}) copy-start(s32[2]{0:T(128)} %param.14) | copy-start | bytes 28
  12.2 1.2 %collective-permute-start.2 = (f32[24,128]{1,0:T(8,128)S(1)}, f32[24,128]{1,0:T(8,128)S(1)}, u32[]{:S(2)}, u32[]{:S(2)}) collective-permute-start(f32[24,128]{1,0:T(8,128)S(1)} %get-tuple-element.29), channel_id=1, source_target_pairs={{0,1},{1,0},{2,3},{3,2},{4,5},{5,4},{6,7},{7,6},{8,9},{9,8},{10,11... | collective-permute-start | bytes 36872 | tf_op jit(solution)/shard_map/ppermute | solution.py:33
  13.4 4.1 %collective-permute-start.3 = (f32[24,128]{1,0:T(8,128)S(1)}, f32[24,128]{1,0:T(8,128)S(1)}, u32[]{:S(2)}, u32[]{:S(2)}) collective-permute-start(f32[24,128]{1,0:T(8,128)S(1)} %add.5.refs_0_), channel_id=1, source_target_pairs={{0,2},{1,3},{2,0},{3,1},{4,6},{5,7},{6,4},{7,5},{8,10},{9,11},{10,... | collective-permute-start | bytes 36872 | tf_op jit(solution)/shard_map/ppermute | solution.py:33
  14.9 3.7 %collective-permute-start.4 = (f32[24,128]{1,0:T(8,128)S(1)}, f32[24,128]{1,0:T(8,128)S(1)}, u32[]{:S(2)}, u32[]{:S(2)}) collective-permute-start(f32[24,128]{1,0:T(8,128)S(1)} %add.5.refs_0_), channel_id=1, source_target_pairs={{0,4},{1,5},{2,6},{3,7},{4,0},{5,1},{6,2},{7,3},{8,12},{9,13},{10,... | collective-permute-start | bytes 36872 | tf_op jit(solution)/shard_map/ppermute | solution.py:33
  15.5 4.6 %collective-permute-start.5 = (f32[24,128]{1,0:T(8,128)S(1)}, f32[24,128]{1,0:T(8,128)S(1)}, u32[]{:S(2)}, u32[]{:S(2)}) collective-permute-start(f32[24,128]{1,0:T(8,128)S(1)} %add.5.refs_0_), channel_id=1, source_target_pairs={{0,6},{1,7},{2,4},{3,5},{4,2},{5,3},{6,0},{7,1},{8,14},{9,15},{10,... | collective-permute-start | bytes 36872 | tf_op jit(solution)/shard_map/ppermute | solution.py:33
  20.4 4.9 %collective-permute-start.6 = (f32[72,256]{1,0:T(8,128)S(1)}, f32[72,256]{1,0:T(8,128)S(1)}, u32[]{:S(2)}, u32[]{:S(2)}) collective-permute-start(f32[72,256]{1,0:T(8,128)S(1)} %get-tuple-element.35), channel_id=1, source_target_pairs={{0,8},{8,0},{16,24},{24,16},{1,9},{9,1},{17,25},{25,17},{2,10},{10... | collective-permute-start | bytes 221192 | tf_op jit(solution)/shard_map/ppermute | solution.py:33
  22.0 6.8 %collective-permute-start.7 = (f32[72,256]{1,0:T(8,128)S(1)}, f32[72,256]{1,0:T(8,128)S(1)}, u32[]{:S(2)}, u32[]{:S(2)}) collective-permute-start(f32[72,256]{1,0:T(8,128)S(1)} %get-tuple-element.36), channel_id=1, source_target_pairs={{0,16},{8,24},{16,0},{24,8},{1,17},{9,25},{17,1},{25,9},{2,18},{10... | collective-permute-start | bytes 221192 | tf_op jit(solution)/shard_map/ppermute | solution.py:33
  24.6 6.2 %collective-permute-start.8 = (f32[72,256]{1,0:T(8,128)S(1)}, f32[72,256]{1,0:T(8,128)S(1)}, u32[]{:S(2)}, u32[]{:S(2)}) collective-permute-start(f32[72,256]{1,0:T(8,128)S(1)} %get-tuple-element.37), channel_id=1, source_target_pairs={{0,24},{8,16},{16,8},{24,0},{1,25},{9,17},{17,9},{25,1},{2,26},{10... | collective-permute-start | bytes 221192 | tf_op jit(solution)/shard_map/ppermute | solution.py:33

commit v5 on v4

v5 whole, which is shorter than its diff:
```python
import functools

import jax
import jax.numpy as jnp
from jax import lax
from jax.experimental import pallas as pl
from jax.experimental.pallas import tpu as pltpu
from jax.sharding import PartitionSpec as P

ITERS = 3
SOURCE_STRENGTH = 50.0
TINY = 1e-30
LANES = 128
SUBLANES = 8


def harmonic(left_val, right_val):
    return 2.0 * left_val * right_val / jnp.maximum(left_val + right_val, TINY)


def safe_div(num, den):
    return jnp.where(den > 0.0, num / jnp.where(den > 0.0, den, 1.0), 0.0)


def tree_sum(values):
    values = list(values)
    while len(values) > 1:
        values = [values[i] + values[i + 1] for i in range(0, len(values), 2)]
    return values[0]


def swap(value, axis, mask, size):
    return lax.ppermute(value, axis, [(i, i ^ mask) for i in range(size)])


def tile_parts(value, axis):
    size = lax.axis_size(axis)
    parts = [value]
    bit = 1
    while bit < size:
        value = tree_sum(parts)
        masks = [bit]
        if bit > 1 and bit * 2 < size:
            masks.append(bit * 2)
        offsets = [0]
        for mask in masks:
            offsets += [o ^ mask for o in offsets]
        parts = [value] + [swap(value, axis, o, size) for o in offsets[1:]]
        bit = masks[-1] * 2
    return parts


def step_polynomial(moments):
    def inner(poly):
        return sum(a * b * moments[i + j] for i, a in enumerate(poly) for j, b in enumerate(poly))

    def energy(poly):
        return sum(
            a * b * (moments[i + j] - moments[i + j + 1])
            for i, a in enumerate(poly)
            for j, b in enumerate(poly)
        )

    one = jnp.ones_like(moments[0])
    zero = jnp.zeros_like(moments[0])
    res, way, total = [one], [one], [zero] * ITERS
    gamma = moments[0]
    for iteration in range(ITERS):
        alpha = safe_div(gamma, energy(way))
        total = [t + alpha * (way[i] if i < len(way) else zero) for i, t in enumerate(total)]
        if iteration + 1 < ITERS:
            longer = way + [zero]
            shifted = [zero] + way
            res = [r - alpha * (a - b) for r, a, b in zip(res + [zero], longer, shifted)]
            gamma_next = jnp.maximum(inner(res), 0.0)
            ratio = safe_div(gamma_next, gamma)
            way = [r + ratio * a for r, a in zip(res, longer)]
            gamma = gamma_next
    return total


VMEM = pl.BlockSpec(memory_space=pltpu.VMEM)
PARAMS = pltpu.CompilerParams(vmem_limit_bytes=16 << 20)


def vmem_call(kernel, out_shape, inputs, scratch=()):
    return pl.pallas_call(
        kernel,
        out_shape=out_shape,
        in_specs=[VMEM] * len(inputs),
        out_specs=jax.tree.map(lambda _: VMEM, out_shape),
        scratch_shapes=list(scratch),
        compiler_params=PARAMS,
    )(*inputs)


def cols(c):
    return slice(c * LANES, (c + 1) * LANES)


def add(sums, key, value):
    sums[key] = sums[key] + value if key in sums else value


def edge_kernel(field_hbm, class_hbm, cond_hbm, row_hbm, col_hbm, *refs):
    far_ref, near_ref, par_ref, spot_ref = refs[:4]
    field_ref, class_ref, cond_ref, row_ref, col_ref, sems = refs[4:]
    sources, rows, _ = field_hbm.shape
    halo = far_ref.shape[1]
    pairs = []
    for i, at in enumerate((0, rows - SUBLANES)):
        pairs.append((field_hbm.at[:, pl.ds(at, SUBLANES)], field_ref.at[i]))
        pairs.append((class_hbm.at[pl.ds(at, SUBLANES)], class_ref.at[i]))
    pairs += [
        (cond_hbm, cond_ref),
        (row_hbm, row_ref),
        (col_hbm, col_ref),
    ]
    copies = [
        pltpu.make_async_copy(start, end, sems.at[i]) for i, (start, end) in enumerate(pairs)
    ]
    for copy in copies:
        copy.start()
    for copy in copies:
        copy.wait()
    even = lax.axis_index("tile") % 2 == 0
    spare = SUBLANES - halo
    for s in range(sources):
        first, last = field_ref[0, s, :halo], field_ref[1, s, spare:]
        far_ref[s] = jnp.where(even, first, last)
        near_ref[s] = jnp.where(even, last, first)
    first = class_ref[0, :halo].astype(jnp.float32) + 1.0
    last = class_ref[1, spare:].astype(jnp.float32) + 1.0
    far_ref[sources] = jnp.where(even, first, last)
    near_ref[sources] = jnp.where(even, last, first)
    tile = (SUBLANES, LANES)
    n_class = cond_ref.shape[0]
    for i in range(n_class):
        par_ref[i] = jnp.full(tile, cond_ref[i], jnp.float32)
    for s in range(sources):
        spot_ref[s] = jnp.full(tile, row_ref[s], jnp.int32)
        spot_ref[sources + s] = jnp.full(tile, col_ref[s], jnp.int32)


def neighbours(get, chunks, lane):
    here = get(0)
    last = LANES - 1
    from_right = pltpu.roll(here, last, 1)
    before = None
    for c in range(chunks):
        from_left = pltpu.roll(here, 1, 1)
        left = jnp.where(lane == 0, before, from_left) if c else from_left
        right = from_right
        if c + 1 < chunks:
            following = get(c + 1)
            from_next = pltpu.roll(following, last, 1)
            right = jnp.where(lane == last, from_next, from_right)
        yield c, here, left, right
        before = from_left
        if c + 1 < chunks:
            here, from_right = following, from_next


def conductivity(ids, values):
    sigma = jnp.zeros(ids.shape, jnp.float32)
    for i, value in enumerate(values):
        sigma = jnp.where(ids == i + 1.0, value, sigma)
    return sigma


def tall(tile, rows):
    return jnp.concatenate([tile] * (rows // SUBLANES), axis=0)


def line_sum(value):
    return jnp.sum(value, axis=0, keepdims=True)


def lines_of(tops, sums, sources):
    lines = list(tops)
    for n in range(2 * ITERS):
        for s in range(sources):
            lines.append(line_sum(sums[n, s]))
    return lines


def inner_kernel(field_ref, class_ref, par_ref, wave_ref, spot_ref, pick_ref, *refs):
    x_ref, *basis_refs = refs[: 1 + ITERS]
    pay_ref, sig_ref, side_ref, above_ref, below_ref, hit_ref, square_ref = refs[1 + ITERS : 8 + ITERS]
    up_ref, down_ref, west_ref, east_ref, diag_ref, inv_ref = refs[8 + ITERS :]
    sources, rows, _ = field_ref.shape
    chunks, total = x_ref.shape[1:3]
    n_class = par_ref.shape[0]
    halo = (total - rows) // 2
    lane = lax.broadcasted_iota(jnp.int32, (total, LANES), 1)
    row = lax.broadcasted_iota(jnp.int32, (total, LANES), 0)
    rows_at = row + (lax.axis_index("tile") * rows - halo)
    blank = jnp.zeros((halo, LANES), jnp.float32)
    inner = slice(SUBLANES, total - SUBLANES)
    wave = jnp.broadcast_to(wave_ref[...], (SUBLANES, LANES))
    square_ref[...] = wave * wave
    square = tall(square_ref[...], total)
    values = [tall(par_ref[i], rows) for i in range(n_class)]

    def widened(value):
        return jnp.concatenate([blank, value, blank], axis=0)

    for c in range(chunks):
        ids = class_ref[:, cols(c)].astype(jnp.float32) + 1.0
        sig_ref[c] = widened(conductivity(ids, values))
        for s in range(sources):
            x_ref[s, c] = widened(field_ref[s, :, cols(c)])
    for c, sigma, left, _ in neighbours(lambda c: sig_ref[c], chunks, lane):
        face = harmonic(left, sigma)
        side_ref[c] = jnp.where(lane == 0, 0.0, face) if c == 0 else face
        up = harmonic(pltpu.roll(sigma, 1, 0), sigma)
        above_ref[c] = up
        below_ref[c] = pltpu.roll(up, total - 1, 0)
    at_source = [rows_at == tall(spot_ref[s], total) for s in range(sources)]
    for c, west, _, east in neighbours(lambda c: side_ref[c], chunks, lane):
        up, down = above_ref[c], below_ref[c]
        sigma = sig_ref[c]
        diag = up + down + west + square * sigma
        if c == chunks - 1:
            bottom = lane == LANES - 1
            diag = diag + jnp.where(bottom, sigma, east)
            east = jnp.where(bottom, 0.0, east)
        else:
            diag = diag + east
        inverse = 1.0 / jnp.maximum(diag, TINY)
        diag_ref[c] = diag
        inv_ref[c] = inverse
        up_ref[c] = up * inverse
        down_ref[c] = down * inverse
        west_ref[c] = west * inverse
        east_ref[c] = east * inverse

    def spread(c, here, left, right):
        return (
            up_ref[c] * pltpu.roll(here, 1, 0)
            + down_ref[c] * pltpu.roll(here, total - 1, 0)
            + west_ref[c] * left
            + east_ref[c] * right
        )

    def fold(value):
        return sum(value[r : r + SUBLANES] for r in range(0, value.shape[0], SUBLANES))

    sums = {}
    for s in range(sources):
        column = tall(spot_ref[sources + s], total)
        for c, here, left, right in neighbours(lambda c: x_ref[s, c], chunks, lane):
            charge = jnp.where(
                at_source[s] & (lane + c * LANES == column), SOURCE_STRENGTH, 0.0
            )
            hit_ref[0, s, c] = charge[:SUBLANES]
            hit_ref[1, s, c] = charge[total - SUBLANES :]
            new = charge * inv_ref[c] - (here - spread(c, here, left, right))
            basis_refs[0][s, c] = new
            own = new[inner]
            add(sums, (0, s), fold(diag_ref[c, inner] * own * own))
    for i in range(ITERS):
        for s in range(sources):
            for c, here, left, right in neighbours(lambda c: basis_refs[i][s, c], chunks, lane):
                new = spread(c, here, left, right)
                own = new[inner]
                weighted = diag_ref[c, inner] * own
                add(sums, (2 * i + 1, s), fold(weighted * here[inner]))
                if i + 1 < ITERS:
                    basis_refs[i + 1][s, c] = new
                    add(sums, (2 * i + 2, s), fold(weighted * own))
    picker = rows_at[inner] == pick_ref[...]
    tops = []
    for ref in (x_ref, *basis_refs):
        for s in range(sources):
            top = jnp.broadcast_to(ref[s, 0, inner, 0:1], (total - 2 * SUBLANES, LANES))
            tops.append(line_sum(fold(jnp.where(picker, top, 0.0))))
    pay_ref[...] = jnp.zeros(pay_ref.shape, jnp.float32)
    for i, line in enumerate(lines_of(tops, sums, sources)):
        pay_ref[i : i + 1, :] = line


def outer_kernel(far_ref, near_ref, par_ref, pick_ref, *refs):
    x_in, *basis_in = refs[: 1 + ITERS]
    pay_in, sig_in, side_in, above_in, below_in, hit_in, square_in = refs[1 + ITERS : 8 + ITERS]
    outs = refs[8 + ITERS :]
    x_ref, *basis_refs = outs[: 1 + ITERS]
    pay_ref = outs[1 + ITERS]
    sigma_ref, west_raw, up_ref, down_ref, west_ref, east_ref, diag_ref, inv_ref = outs[2 + ITERS :]
    sources, chunks, total, _ = x_in.shape
    n_class = par_ref.shape[0]
    halo = far_ref.shape[1]
    rows = total - 2 * halo
    lane = lax.broadcasted_iota(jnp.int32, (SUBLANES, LANES), 1)
    row = lax.broadcasted_iota(jnp.int32, (SUBLANES, LANES), 0)
    tile = lax.axis_index("tile")
    even = tile % 2 == 0
    square = square_in[...]
    values = [par_ref[i] for i in range(n_class)]
    upper = row < halo
    last = total - SUBLANES
    own = (jnp.logical_not(upper), upper)

    def came_in(index, c):
        far, near = far_ref[index, :, cols(c)], near_ref[index, :, cols(c)]
        return jnp.concatenate(
            [jnp.where(even, far, near), jnp.where(even, near, far)], axis=0
        )

    def set_in(new, kept):
        return jnp.where(upper, new, kept[:SUBLANES]), jnp.where(upper, kept[last:], new)

    for c in range(chunks):
        sigma_ref[c] = conductivity(came_in(sources, c), values)
        for s in range(sources):
            x_ref[0, s, c], x_ref[1, s, c] = set_in(came_in(s, c), x_in.at[s, c])
    for c, fresh, left, _ in neighbours(lambda c: sigma_ref[c], chunks, lane):
        face = harmonic(left, fresh)
        face = jnp.where(lane == 0, 0.0, face) if c == 0 else face
        west_raw[0, c], west_raw[1, c] = set_in(face, side_in.at[c])
    for e in (0, 1):
        for c, west, _, east in neighbours(lambda c: west_raw[e, c], chunks, lane):
            fresh = sigma_ref[c]
            first, end = set_in(fresh, sig_in.at[c])
            sigma = end if e else first
            face = harmonic(
                jnp.where(upper, pltpu.roll(first, SUBLANES - 1, 0), pltpu.roll(end, 1, 0)), fresh
            )
            if e:
                up = jnp.where(upper, above_in[c, last:], face)
                down = pltpu.roll(up, SUBLANES - 1, 0)
            else:
                down = jnp.where(upper, face, below_in[c, :SUBLANES])
                up = pltpu.roll(down, 1, 0)
            diag = up + down + west + square * sigma
            if c == chunks - 1:
                bottom = lane == LANES - 1
                diag = diag + jnp.where(bottom, sigma, east)
                east = jnp.where(bottom, 0.0, east)
            else:
                diag = diag + east
            inverse = 1.0 / jnp.maximum(diag, TINY)
            diag_ref[e, c] = jnp.where(own[e], diag, 0.0)
            inv_ref[e, c] = inverse
            up_ref[e, c] = up * inverse
            down_ref[e, c] = down * inverse
            west_ref[e, c] = west * inverse
            east_ref[e, c] = east * inverse

    def spread(whole, e, s, c, here, left, right):
        above = pltpu.roll(here, 1, 0)
        below = pltpu.roll(here, SUBLANES - 1, 0)
        if e:
            above = jnp.where(row == 0, whole[s, c, last - 1 : last], above)
        else:
            below = jnp.where(row == SUBLANES - 1, whole[s, c, SUBLANES : SUBLANES + 1], below)
        return (
            up_ref[e, c] * above
            + down_ref[e, c] * below
            + west_ref[e, c] * left
            + east_ref[e, c] * right
        )

    sums = {}
    both = [(e, s) for e in (0, 1) for s in range(sources)]
    for e, s in both:
        for c, here, left, right in neighbours(lambda c: x_ref[e, s, c], chunks, lane):
            new = hit_in[e, s, c] * inv_ref[e, c] - (
                here - spread(x_in, e, s, c, here, left, right)
            )
            basis_refs[0][e, s, c] = new
            add(sums, (0, s), diag_ref[e, c] * new * new)
    for i in range(ITERS):
        for e, s in both:
            for c, here, left, right in neighbours(
                lambda c: basis_refs[i][e, s, c], chunks, lane
            ):
                new = spread(basis_in[i], e, s, c, here, left, right)
                weighted = diag_ref[e, c] * new
                add(sums, (2 * i + 1, s), weighted * here)
                if i + 1 < ITERS:
                    basis_refs[i + 1][e, s, c] = new
                    add(sums, (2 * i + 2, s), weighted * new)
    pickers = [
        own[e] & (row + (tile * rows - halo + at) == pick_ref[...]) for e, at in ((0, 0), (1, last))
    ]
    tops = []
    for ref in (x_ref, *basis_refs):
        for s in range(sources):
            line = 0.0
            for e in (0, 1):
                top = jnp.broadcast_to(ref[e, s, 0, :, 0:1], (SUBLANES, LANES))
                line = line + jnp.where(pickers[e], top, 0.0)
            tops.append(line_sum(line))
    pay_ref[...] = pay_in[...]
    for i, line in enumerate(lines_of(tops, sums, sources)):
        pay_ref[i : i + 1, :] += line


def combine_kernel(n_pay, weight_ref, *refs):
    n_parts = ITERS + 1
    packed = tree_sum([r[...] for r in refs[:n_pay]])
    part_refs = refs[n_pay : n_pay + n_parts]
    edge_refs = refs[n_pay + n_parts : n_pay + 2 * n_parts]
    out_refs = refs[n_pay + 2 * n_parts :]
    sources, _, total, _ = part_refs[0].shape
    share = out_refs[0].shape[1]
    rows = (out_refs[0].shape[0] - SUBLANES) // sources
    halo = (total - rows) // 2
    first = n_parts * sources
    totals = jnp.sum(packed[first : first + 2 * ITERS * sources], axis=1, keepdims=True)
    poly = step_polynomial([totals[n * sources : (n + 1) * sources] for n in range(2 * ITERS)])
    weight = weight_ref[...]
    scale = [[weight] + [weight * p[s : s + 1] for p in poly] for s in range(sources)]
    read = [
        sum(scale[s][i] * packed[i * sources + s : i * sources + s + 1] for i in range(n_parts))
        for s in range(sources)
    ]
    split = len(out_refs) > 1
    wave = lax.axis_index("wave") if split else 0
    per = share // LANES
    inner = slice(SUBLANES, total - SUBLANES)
    for mask, out_ref in enumerate(out_refs):
        block = wave ^ mask if split else 0
        for s in range(sources):
            for k in range(per):
                c = block * per + k
                middle = sum(scale[s][i] * part_refs[i][s, c, inner] for i in range(n_parts))
                top, end = (
                    sum(scale[s][i] * edge_refs[i][e, s, c] for i in range(n_parts)) for e in (0, 1)
                )
                value = jnp.concatenate([top[halo:], middle, end[: SUBLANES - halo]], axis=0)
                out_ref[s * rows : (s + 1) * rows, cols(k)] = value
        out_ref[sources * rows :, :] = jnp.zeros((SUBLANES, share), jnp.float32)
        for s in range(sources):
            out_ref[sources * rows + s : sources * rows + s + 1, :LANES] = read[s]


def sum_kernel(*refs):
    part_refs, (field_ref, read_ref) = refs[:-2], refs[-2:]
    sources, rows, _ = field_ref.shape
    electrodes = read_ref.shape[1]
    for s in range(sources):
        field_ref[s] = tree_sum([r[s * rows : (s + 1) * rows, :] for r in part_refs])
    last = tree_sum([r[sources * rows :, :LANES] for r in part_refs])
    read_ref[...] = last[:sources, :electrodes]


def shards(
    warm_start,
    class_map,
    conductivities,
    wavenumbers,
    weights,
    source_row,
    source_col,
    electrode_row,
):
    rows, depth = class_map.shape
    sources = warm_start.shape[1]
    electrodes = electrode_row.shape[0]
    tiles, waves = lax.axis_size("tile"), lax.axis_size("wave")
    wave = lax.axis_index("wave")
    halo = ITERS + 1
    field = warm_start[0]
    f32 = jnp.float32
    n_class = conductivities.shape[0]
    rim = jax.ShapeDtypeStruct((sources + 1, halo, depth), f32)
    raw = [
        field,
        class_map,
        conductivities,
        source_row,
        source_col,
    ]
    far, near, params, spots = pl.pallas_call(
        edge_kernel,
        out_shape=[
            rim,
            rim,
            jax.ShapeDtypeStruct((n_class, SUBLANES, LANES), f32),
            jax.ShapeDtypeStruct((2 * sources, SUBLANES, LANES), jnp.int32),
        ],
        in_specs=[pl.BlockSpec(memory_space=pltpu.HBM)] * len(raw),
        out_specs=[VMEM] * 4,
        scratch_shapes=[
            pltpu.VMEM((2, sources, SUBLANES, depth), f32),
            pltpu.VMEM((2, SUBLANES, depth), jnp.int32),
            *[pltpu.SMEM(a.shape, a.dtype) for a in raw[2:]],
            pltpu.SemaphoreType.DMA((len(raw) + 2,)),
        ],
        compiler_params=PARAMS,
    )(*[pltpu.with_memory_space_constraint(a, pltpu.HBM) for a in raw])
    far_pairs = [(i, i + 1) for i in range(1, tiles - 1, 2)]
    far = lax.ppermute(far, "tile", far_pairs + [(j, i) for i, j in far_pairs])
    near = swap(near, "tile", 1, tiles)
    total, chunks = rows + 2 * halo, depth // LANES
    picks = jnp.pad(electrode_row, (0, LANES - electrodes), constant_values=-1)[None]
    wide = jax.ShapeDtypeStruct((sources, chunks, total, LANES), f32)
    flat = jax.ShapeDtypeStruct((chunks, total, LANES), f32)
    n_lines = sources * (3 * ITERS + 1)
    pay = jax.ShapeDtypeStruct((-(-n_lines // SUBLANES) * SUBLANES, LANES), f32)
    ends = jax.ShapeDtypeStruct((2, sources, chunks, SUBLANES, LANES), f32)
    tile = jax.ShapeDtypeStruct((SUBLANES, LANES), f32)
    inside = vmem_call(
        inner_kernel,
        [wide] * (ITERS + 1) + [pay, flat, flat, flat, flat, ends, tile],
        [field, class_map, params, wavenumbers[None], spots, picks],
        [pltpu.VMEM((chunks, total, LANES), f32)] * 6,
    )
    pair = pltpu.VMEM((2, chunks, SUBLANES, LANES), f32)
    outside = vmem_call(
        outer_kernel,
        [ends] * (ITERS + 1) + [pay],
        [far, near, params, picks, *inside],
        [pltpu.VMEM((chunks, SUBLANES, LANES), f32)] + [pair] * 7,
    )
    packed = tile_parts(outside[-1], "tile")
    share = depth // waves
    split = share % LANES == 0
    width = share if split else depth
    block = jax.ShapeDtypeStruct((sources * rows + SUBLANES, width), f32)
    pieces = vmem_call(
        functools.partial(combine_kernel, len(packed)),
        [block] * (waves if split else 1),
        [weights[None], *packed, *inside[: ITERS + 1], *outside[: ITERS + 1]],
    )
    if not split:
        n = sources * rows
        read = pieces[0][n : n + sources, :electrodes].reshape(-1, share)
        pieces = [
            jnp.concatenate(
                [lax.dynamic_slice_in_dim(pieces[0][:n], (wave ^ mask) * share, share, 1), read]
            )
            for mask in range(waves)
        ]
    pieces = [pieces[0]] + [swap(pieces[m], "wave", m, waves) for m in range(1, waves)]
    if not split:
        final = tree_sum(pieces)
        return (
            final[: sources * rows].reshape(sources, rows, share),
            final[sources * rows :].reshape(sources, electrodes),
        )
    return tuple(
        vmem_call(
            sum_kernel,
            [
                jax.ShapeDtypeStruct((sources, rows, share), f32),
                jax.ShapeDtypeStruct((sources, electrodes), f32),
            ],
            pieces,
        )
    )


def solution(mesh):
    return jax.shard_map(
        shards,
        mesh=mesh,
        in_specs=(
            P("wave", None, "tile", None),
            P("tile", None),
            P(),
            P("wave"),
            P("wave"),
            P(),
            P(),
            P(),
        ),
        out_specs=(P(None, "tile", "wave"), P()),
        check_vma=False,
    )
```

time: 31.6 us -> 30.2 us (0.956)
  local copies, waits for them, and re-layouts: 2.52 us -> 0.02 us
  waiting for transfers between devices: 9.58 us -> 10.6 us
  Pallas kernels: 4.2 us -> 3.8 us
  starting transfers between devices: 13.1 us -> 13.5 us
    unnamed x12 -> x6, local copies, waits for them, and re-layouts: 2.52 us -> 0.01 us
    pallas_call x4, Pallas kernels: 3.98 us -> 2.74 us  [vmem_call(): pl.pallas_call(kernel, out_shape=out_shape, in_specs=[VMEM] * len(inputs)...]
    ppermute x8, waiting for transfers between devices: 9.58 us -> 10.6 us  [swap(): return lax.ppermute(value, axis, [(i, i ^ mask) for i in range(size)])]
    pallas_call x1, Pallas kernels: 0.22 us -> 1.06 us  [shards(): pl.pallas_call(edge_kernel, out_shape=[rim, rim, jax.ShapeDtypeStruct((n_...]
    ppermute x8, starting transfers between devices: 12.4 us -> 12.8 us  [swap(): return lax.ppermute(value, axis, [(i, i ^ mask) for i in range(size)])]
  transfers between devices with their start and end apart: 9 -> 9, of which waited for: 6 -> 6; matrix products, arithmetic and copies ran while one was open for 0% -> 0% of each run, Pallas kernels for 6% -> 4%
where the time goes in v5:
time: 30.2 us; the launch traced here: 30 us
  starting transfers between devices  13.5 us (45%)
  waiting for transfers between devices  10.6 us (35%)
  Pallas kernels  3.8 us (13%)
  between operations  2.04 us (7%)
    ppermute x8, starting transfers between devices, swap(): return lax.ppermute(value, axis, [(i, i ^ mask) for i in range(size)])  12.8 us
    ppermute x8, waiting for transfers between devices, swap(): return lax.ppermute(value, axis, [(i, i ^ mask) for i in range(size)])  10.6 us
    pallas_call x4, Pallas kernels, vmem_call(): pl.pallas_call(kernel, out_shape=out_shape, in_specs=[VMEM] * len(inputs)...  2.74 us
    pallas_call x1, Pallas kernels, shards(): pl.pallas_call(edge_kernel, out_shape=[rim, rim, jax.ShapeDtypeStruct((n_...  1.06 us
    ppermute x1, starting transfers between devices, shards(): far = lax.ppermute(far, 'tile', far_pairs + [(j, i) for i, j in far_pairs])  0.66 us
  transfers between devices with their start and end apart: 9, of which 6 were waited for; matrix products, arithmetic and copies ran while one was open for 0% of the time, Pallas kernels for 4%

profile of v5, /device:TPU:0, one launch (start us, length us, event | category | flops | bytes accessed | tf_op | source)
XLA Modules:
  0.0 30.0 jit_solution(17770505807419304494)
XLA Ops:
  0.6 0.0 copy-start
  0.6 0.0 copy-start.1
  0.7 1.1 %shard_map.95 = (f32[3,4,1024]{2,1,0:T(4,128)S(1)}, f32[3,4,1024]{2,1,0:T(4,128)S(1)}, f32[8,8,128]{2,1,0:T(8,128)S(1)}, s32[4,8,128]{2,1,0:T(8,128)S(1)}) custom-call(f32[2,32,1024]{2,1,0:T(8,128)} %bitcast.7, s32[32,1024]{1,0:T(8,128)} %class_ref.1, f32[8]{0:T(128)} %cond_hbm.1, s32[2]{0:T(128)} %row_hbm.1, s32[2]{0:T(128)} %col_hbm.1), custom_call_target="tpu_custom_call" | custom-call | tf_op jit(solution)/shard_map/pallas_call | solution.py:476
  1.7 0.0 copy-start.2
  1.7 0.7 %collective-permute-start = (f32[3,4,1024]{2,1,0:T(4,128)S(1)}, f32[3,4,1024]{2,1,0:T(4,128)S(1)}, u32[]{:S(2)}, u32[]{:S(2)}) collective-permute-start(f32[3,4,1024]{2,1,0:T(4,128)S(1)} %get-tuple-element.26), channel_id=1, source_target_pairs={{1,2},{3,4},{5,6},{2,1},{4,3},{6,5},{9,10},{11,12},{13,14},{10,9},... | collective-permute-start | bytes 147464 | tf_op jit(solution)/shard_map/ppermute | solution.py:495
  2.4 4.4 %collective-permute-start.1 = (f32[3,4,1024]{2,1,0:T(4,128)S(1)}, f32[3,4,1024]{2,1,0:T(4,128)S(1)}, u32[]{:S(2)}, u32[]{:S(2)}) collective-permute-start(f32[3,4,1024]{2,1,0:T(4,128)S(1)} %get-tuple-element.27), channel_id=1, source_target_pairs={{0,1},{1,0},{2,3},{3,2},{4,5},{5,4},{6,7},{7,6},{8,9},{9,8},{10,11... | collective-permute-start | bytes 147464 | tf_op jit(solution)/shard_map/ppermute | solution.py:33
  6.8 0.0 copy-done.2
  7.5 0.0 copy-done
  7.5 0.0 copy-done.1
  7.5 1.1 %shard_map.96 = (f32[2,8,40,128]{3,2,1,0:T(8,128)S(1)}, f32[2,8,40,128]{3,2,1,0:T(8,128)S(1)}, f32[2,8,40,128]{3,2,1,0:T(8,128)S(1)}, f32[2,8,40,128]{3,2,1,0:T(...) custom-call(f32[2,32,1024]{2,1,0:T(8,128)S(1)} %bitcast.8, ...), custom_call_target="tpu_custom_call" | custom-call | tf_op jit(solution)/shard_map/pallas_call | solution.py:87
  8.6 0.0 collective-permute-done.far_ref
  8.6 0.0 collective-permute-done.1.near_ref
  8.6 0.7 %shard_map.97 = (f32[2,2,8,8,128]{4,3,2,1,0:T(8,128)S(1)}, f32[2,2,8,8,128]{4,3,2,1,0:T(8,128)S(1)}, f32[2,2,8,8,128]{4,3,2,1,0:T(8,128)S(1)}, f32[2,2,8,8,128]{4,3,2,1,0:T(8,128)S(1)}, f32[24,128]{1,0:T(8,128)S(1)}) custom-call(f32[3,4,1024]{2,1,0:T(4,128)S(1)} %collective-permute-done.far_ref, f32[3,4,1024]{2,1,0:T(4,128)S(1)} %collective-permute-done.1.near_ref, ...), custom_call_target="tpu_custom_call" | custom-call | tf_op jit(solution)/shard_map/pallas_call | solution.py:87
  9.3 0.1 collective-permute-start.2
  9.3 1.2 %collective-permute-done.2 = f32[24,128]{1,0:T(8,128)S(1)} collective-permute-done((f32[24,128]{1,0:T(8,128)S(1)}, f32[24,128]{1,0:T(8,128)S(1)}, u32[]{:S(2)}, u32[]{:S(2)}) %collective-permute-start.2) | collective-permute-done | bytes 12320 | tf_op jit(solution)/shard_map/ppermute | solution.py:33
  10.5 2.4 %collective-permute-start.3 = (f32[24,128]{1,0:T(8,128)S(1)}, f32[24,128]{1,0:T(8,128)S(1)}, u32[]{:S(2)}, u32[]{:S(2)}) collective-permute-start(f32[24,128]{1,0:T(8,128)S(1)} %add.5.refs_0_), channel_id=1, source_target_pairs={{0,2},{1,3},{2,0},{3,1},{4,6},{5,7},{6,4},{7,5},{8,10},{9,11},{10,... | collective-permute-start | bytes 36872 | tf_op jit(solution)/shard_map/ppermute | solution.py:33
  12.9 1.1 %collective-permute-start.4 = (f32[24,128]{1,0:T(8,128)S(1)}, f32[24,128]{1,0:T(8,128)S(1)}, u32[]{:S(2)}, u32[]{:S(2)}) collective-permute-start(f32[24,128]{1,0:T(8,128)S(1)} %add.5.refs_0_), channel_id=1, source_target_pairs={{0,4},{1,5},{2,6},{3,7},{4,0},{5,1},{6,2},{7,3},{8,12},{9,13},{10,... | collective-permute-start | bytes 36872 | tf_op jit(solution)/shard_map/ppermute | solution.py:33
  14.0 0.4 %collective-permute-start.5 = (f32[24,128]{1,0:T(8,128)S(1)}, f32[24,128]{1,0:T(8,128)S(1)}, u32[]{:S(2)}, u32[]{:S(2)}) collective-permute-start(f32[24,128]{1,0:T(8,128)S(1)} %add.5.refs_0_), channel_id=1, source_target_pairs={{0,6},{1,7},{2,4},{3,5},{4,2},{5,3},{6,0},{7,1},{8,14},{9,15},{10,... | collective-permute-start | bytes 36872 | tf_op jit(solution)/shard_map/ppermute | solution.py:33
  15.1 0.0 collective-permute-done.3.refs_1_
  15.1 1.5 %collective-permute-done.4.refs_2_ = f32[24,128]{1,0:T(8,128)S(1)} collective-permute-done((f32[24,128]{1,0:T(8,128)S(1)}, f32[24,128]{1,0:T(8,128)S(1)}, u32[]{:S(2)}, u32[]{:S(2)}) %collective-permute-start.4) | collective-permute-done | bytes 12320 | tf_op jit(solution)/shard_map/ppermute | solution.py:33
  16.6 2.0 %collective-permute-done.5.refs_3_ = f32[24,128]{1,0:T(8,128)S(1)} collective-permute-done((f32[24,128]{1,0:T(8,128)S(1)}, f32[24,128]{1,0:T(8,128)S(1)}, u32[]{:S(2)}, u32[]{:S(2)}) %collective-permute-start.5) | collective-permute-done | bytes 12320 | tf_op jit(solution)/shard_map/ppermute | solution.py:33
  18.6 0.3 %shard_map.98 = (f32[72,256]{1,0:T(8,128)S(1)}, f32[72,256]{1,0:T(8,128)S(1)}, f32[72,256]{1,0:T(8,128)S(1)}, f32[72,256]{1,0:T(8,128)S(1)}) custom-call(f32[1,1]{1,0:T(1,128)} %bitcast.6.weight_ref, f32[24,128]{1,0:T(8,128)S(1)} %add.5.refs_0_, f32[24,128]{1,0:T(8,128)S(1)} %collective-permute-done.3.refs_1_, f32[24,128]{1,0:T(8,128)S(1)} %collective-permute-done.4.refs_2_, ...), custom_call_target="tpu_custom_call" | custom-call | tf_op jit(solution)/shard_map/pallas_call | solution.py:87
  19.0 1.6 %collective-permute-start.6 = (f32[72,256]{1,0:T(8,128)S(1)}, f32[72,256]{1,0:T(8,128)S(1)}, u32[]{:S(2)}, u32[]{:S(2)}) collective-permute-start(f32[72,256]{1,0:T(8,128)S(1)} %get-tuple-element.47), channel_id=1, source_target_pairs={{0,8},{8,0},{16,24},{24,16},{1,9},{9,1},{17,25},{25,17},{2,10},{10... | collective-permute-start | bytes 221192 | tf_op jit(solution)/shard_map/ppermute | solution.py:33
  20.6 2.6 %collective-permute-start.7 = (f32[72,256]{1,0:T(8,128)S(1)}, f32[72,256]{1,0:T(8,128)S(1)}, u32[]{:S(2)}, u32[]{:S(2)}) collective-permute-start(f32[72,256]{1,0:T(8,128)S(1)} %get-tuple-element.48), channel_id=1, source_target_pairs={{0,16},{8,24},{16,0},{24,8},{1,17},{9,25},{17,1},{25,9},{2,18},{10... | collective-permute-start | bytes 221192 | tf_op jit(solution)/shard_map/ppermute | solution.py:33
  23.2 0.2 collective-permute-start.8
  23.4 0.4 %collective-permute-done.6.refs_1_ = f32[72,256]{1,0:T(8,128)S(1)} collective-permute-done((f32[72,256]{1,0:T(8,128)S(1)}, f32[72,256]{1,0:T(8,128)S(1)}, u32[]{:S(2)}, u32[]{:S(2)}) %collective-permute-start.6) | collective-permute-done | bytes 73760 | tf_op jit(solution)/shard_map/ppermute | solution.py:33
  23.8 3.7 %collective-permute-done.7.refs_2_ = f32[72,256]{1,0:T(8,128)S(1)} collective-permute-done((f32[72,256]{1,0:T(8,128)S(1)}, f32[72,256]{1,0:T(8,128)S(1)}, u32[]{:S(2)}, u32[]{:S(2)}) %collective-permute-start.7) | collective-permute-done | bytes 73760 | tf_op jit(solution)/shard_map/ppermute | solution.py:33
  27.4 1.9 %collective-permute-done.8.refs_3_ = f32[72,256]{1,0:T(8,128)S(1)} collective-permute-done((f32[72,256]{1,0:T(8,128)S(1)}, f32[72,256]{1,0:T(8,128)S(1)}, u32[]{:S(2)}, u32[]{:S(2)}) %collective-permute-start.8) | collective-permute-done | bytes 73760 | tf_op jit(solution)/shard_map/ppermute | solution.py:33
  29.3 0.6 %shard_map.99 = (f32[2,32,256]{2,1,0:T(8,128)}, f32[2,64]{1,0:T(2,128)}) custom-call(f32[72,256]{1,0:T(8,128)S(1)} %get-tuple-element.46.refs_0_, f32[72,256]{1,0:T(8,128)S(1)} %collective-permute-done.6.refs_1_, f32[72,256]{1,0:T(8,128)S(1)} %collective-permute-done.7.refs_2_, f32[72,256]{1,0:T(8,128)S(1)} %collective-permute-done.8.refs_3_), custom_call_target="tpu_custom_call" | custom-call | tf_op jit(solution)/shard_map/pallas_call | solution.py:87
  (2 shorter events, 0.0 us)
Async XLA Ops:
  0.6 6.8 %copy-start = (f32[1,2,32,1024]{3,2,1,0:T(8,128)S(1)}, f32[1,2,32,1024]{3,2,1,0:T(8,128)}, u32[]{:S(2)}) copy-start(f32[1,2,32,1024]{3,2,1,0:T(8,128)} %param.8) | copy-start | bytes 786436
  0.6 6.8 %copy-start.1 = (s32[32,1024]{1,0:T(8,128)S(1)}, s32[32,1024]{1,0:T(8,128)}, u32[]{:S(2)}) copy-start(s32[32,1024]{1,0:T(8,128)} %class_ref.1) | copy-start | bytes 393220
  1.7 5.1 %copy-start.2 = (s32[64]{0:T(128)S(1)}, s32[64]{0:T(128)}, u32[]{:S(2)}) copy-start(s32[64]{0:T(128)} %param.15) | copy-start | bytes 772
  1.7 6.8 %collective-permute-start = (f32[3,4,1024]{2,1,0:T(4,128)S(1)}, f32[3,4,1024]{2,1,0:T(4,128)S(1)}, u32[]{:S(2)}, u32[]{:S(2)}) collective-permute-start(f32[3,4,1024]{2,1,0:T(4,128)S(1)} %get-tuple-element.26), channel_id=1, source_target_pairs={{1,2},{3,4},{5,6},{2,1},{4,3},{6,5},{9,10},{11,12},{13,14},{10,9},... | collective-permute-start | bytes 147464 | tf_op jit(solution)/shard_map/ppermute | solution.py:495
  2.4 6.2 %collective-permute-start.1 = (f32[3,4,1024]{2,1,0:T(4,128)S(1)}, f32[3,4,1024]{2,1,0:T(4,128)S(1)}, u32[]{:S(2)}, u32[]{:S(2)}) collective-permute-start(f32[3,4,1024]{2,1,0:T(4,128)S(1)} %get-tuple-element.27), channel_id=1, source_target_pairs={{0,1},{1,0},{2,3},{3,2},{4,5},{5,4},{6,7},{7,6},{8,9},{9,8},{10,11... | collective-permute-start | bytes 147464 | tf_op jit(solution)/shard_map/ppermute | solution.py:33
  9.3 1.2 %collective-permute-start.2 = (f32[24,128]{1,0:T(8,128)S(1)}, f32[24,128]{1,0:T(8,128)S(1)}, u32[]{:S(2)}, u32[]{:S(2)}) collective-permute-start(f32[24,128]{1,0:T(8,128)S(1)} %get-tuple-element.41), channel_id=1, source_target_pairs={{0,1},{1,0},{2,3},{3,2},{4,5},{5,4},{6,7},{7,6},{8,9},{9,8},{10,11... | collective-permute-start | bytes 36872 | tf_op jit(solution)/shard_map/ppermute | solution.py:33
  10.5 4.6 %collective-permute-start.3 = (f32[24,128]{1,0:T(8,128)S(1)}, f32[24,128]{1,0:T(8,128)S(1)}, u32[]{:S(2)}, u32[]{:S(2)}) collective-permute-start(f32[24,128]{1,0:T(8,128)S(1)} %add.5.refs_0_), channel_id=1, source_target_pairs={{0,2},{1,3},{2,0},{3,1},{4,6},{5,7},{6,4},{7,5},{8,10},{9,11},{10,... | collective-permute-start | bytes 36872 | tf_op jit(solution)/shard_map/ppermute | solution.py:33
  12.9 3.7 %collective-permute-start.4 = (f32[24,128]{1,0:T(8,128)S(1)}, f32[24,128]{1,0:T(8,128)S(1)}, u32[]{:S(2)}, u32[]{:S(2)}) collective-permute-start(f32[24,128]{1,0:T(8,128)S(1)} %add.5.refs_0_), channel_id=1, source_target_pairs={{0,4},{1,5},{2,6},{3,7},{4,0},{5,1},{6,2},{7,3},{8,12},{9,13},{10,... | collective-permute-start | bytes 36872 | tf_op jit(solution)/shard_map/ppermute | solution.py:33
  14.0 4.6 %collective-permute-start.5 = (f32[24,128]{1,0:T(8,128)S(1)}, f32[24,128]{1,0:T(8,128)S(1)}, u32[]{:S(2)}, u32[]{:S(2)}) collective-permute-start(f32[24,128]{1,0:T(8,128)S(1)} %add.5.refs_0_), channel_id=1, source_target_pairs={{0,6},{1,7},{2,4},{3,5},{4,2},{5,3},{6,0},{7,1},{8,14},{9,15},{10,... | collective-permute-start | bytes 36872 | tf_op jit(solution)/shard_map/ppermute | solution.py:33
  19.0 4.8 %collective-permute-start.6 = (f32[72,256]{1,0:T(8,128)S(1)}, f32[72,256]{1,0:T(8,128)S(1)}, u32[]{:S(2)}, u32[]{:S(2)}) collective-permute-start(f32[72,256]{1,0:T(8,128)S(1)} %get-tuple-element.47), channel_id=1, source_target_pairs={{0,8},{8,0},{16,24},{24,16},{1,9},{9,1},{17,25},{25,17},{2,10},{10... | collective-permute-start | bytes 221192 | tf_op jit(solution)/shard_map/ppermute | solution.py:33
  20.6 6.8 %collective-permute-start.7 = (f32[72,256]{1,0:T(8,128)S(1)}, f32[72,256]{1,0:T(8,128)S(1)}, u32[]{:S(2)}, u32[]{:S(2)}) collective-permute-start(f32[72,256]{1,0:T(8,128)S(1)} %get-tuple-element.48), channel_id=1, source_target_pairs={{0,16},{8,24},{16,0},{24,8},{1,17},{9,25},{17,1},{25,9},{2,18},{10... | collective-permute-start | bytes 221192 | tf_op jit(solution)/shard_map/ppermute | solution.py:33
  23.2 6.2 %collective-permute-start.8 = (f32[72,256]{1,0:T(8,128)S(1)}, f32[72,256]{1,0:T(8,128)S(1)}, u32[]{:S(2)}, u32[]{:S(2)}) collective-permute-start(f32[72,256]{1,0:T(8,128)S(1)} %get-tuple-element.49), channel_id=1, source_target_pairs={{0,24},{8,16},{16,8},{24,0},{1,25},{9,17},{17,9},{25,1},{2,26},{10... | collective-permute-start | bytes 221192 | tf_op jit(solution)/shard_map/ppermute | solution.py:33

commit v6 on v5

--- a/solution.py
+++ b/solution.py
@@ -48,6 +48,10 @@
         parts = [value] + [swap(value, axis, o, size) for o in offsets[1:]]
         bit = masks[-1] * 2
     return parts
+
+
+def issued(values, order):
+    return [values[i] for i in order], [order.index(i) for i in range(len(values))]
 
 
 def step_polynomial(moments):
@@ -397,9 +401,9 @@
         pay_ref[i : i + 1, :] += line
 
 
-def combine_kernel(n_pay, weight_ref, *refs):
-    n_parts = ITERS + 1
-    packed = tree_sum([r[...] for r in refs[:n_pay]])
+def combine_kernel(places, weight_ref, *refs):
+    n_parts, n_pay = ITERS + 1, len(places)
+    packed = tree_sum([refs[i][...] for i in places])
     part_refs = refs[n_pay : n_pay + n_parts]
     edge_refs = refs[n_pay + n_parts : n_pay + 2 * n_parts]
     out_refs = refs[n_pay + 2 * n_parts :]
@@ -436,8 +440,8 @@
             out_ref[sources * rows + s : sources * rows + s + 1, :LANES] = read[s]
 
 
-def sum_kernel(*refs):
-    part_refs, (field_ref, read_ref) = refs[:-2], refs[-2:]
+def sum_kernel(places, *refs):
+    part_refs, (field_ref, read_ref) = [refs[i] for i in places], refs[-2:]
     sources, rows, _ = field_ref.shape
     electrodes = read_ref.shape[1]
     for s in range(sources):
@@ -516,12 +520,13 @@
         [pltpu.VMEM((chunks, SUBLANES, LANES), f32)] + [pair] * 7,
     )
     packed = tile_parts(outside[-1], "tile")
+    packed, places = issued(packed, (0, *range(len(packed) - 1, 0, -1)))
     share = depth // waves
     split = share % LANES == 0
     width = share if split else depth
     block = jax.ShapeDtypeStruct((sources * rows + SUBLANES, width), f32)
     pieces = vmem_call(
-        functools.partial(combine_kernel, len(packed)),
+        functools.partial(combine_kernel, places),
         [block] * (waves if split else 1),
         [weights[None], *packed, *inside[: ITERS + 1], *outside[: ITERS + 1]],
     )
@@ -541,9 +546,10 @@
             final[: sources * rows].reshape(sources, rows, share),
             final[sources * rows :].reshape(sources, electrodes),
         )
+    pieces, places = issued(pieces, (0, waves - 1, *range(1, waves - 1)))
     return tuple(
         vmem_call(
-            sum_kernel,
+            functools.partial(sum_kernel, places),
             [
                 jax.ShapeDtypeStruct((sources, rows, share), f32),
                 jax.ShapeDtypeStruct((sources, electrodes), f32),

time: 30.2 us -> 28.1 us (0.930)
  waiting for transfers between devices: 10.6 us -> 8.61 us
    ppermute x8, waiting for transfers between devices: 10.6 us -> 8.61 us  [swap(): return lax.ppermute(value, axis, [(i, i ^ mask) for i in range(size)])]
  transfers between devices with their start and end apart: 9 -> 9, of which waited for: 6 -> 7; matrix products, arithmetic and copies ran while one was open for 0% -> 0% of each run, Pallas kernels for 4% -> 4%
where the time goes in v6:
time: 28.1 us; the launch traced here: 28 us
  starting transfers between devices  13.5 us (48%)
  waiting for transfers between devices  8.61 us (31%)
  Pallas kernels  3.8 us (14%)
  between operations  2.03 us (7%)
    ppermute x8, starting transfers between devices, swap(): return lax.ppermute(value, axis, [(i, i ^ mask) for i in range(size)])  12.8 us
    ppermute x8, waiting for transfers between devices, swap(): return lax.ppermute(value, axis, [(i, i ^ mask) for i in range(size)])  8.61 us
    pallas_call x4, Pallas kernels, vmem_call(): pl.pallas_call(kernel, out_shape=out_shape, in_specs=[VMEM] * len(inputs)...  2.74 us
    pallas_call x1, Pallas kernels, shards(): pl.pallas_call(edge_kernel, out_shape=[rim, rim, jax.ShapeDtypeStruct((n_...  1.06 us
    ppermute x1, starting transfers between devices, shards(): far = lax.ppermute(far, 'tile', far_pairs + [(j, i) for i, j in far_pairs])  0.66 us
  transfers between devices with their start and end apart: 9, of which 7 were waited for; matrix products, arithmetic and copies ran while one was open for 0% of the time, Pallas kernels for 4%

profile of v6, /device:TPU:0, one launch (start us, length us, event | category | flops | bytes accessed | tf_op | source)
XLA Modules:
  0.0 28.0 jit_solution(671112639052369096)
XLA Ops:
  0.6 0.0 copy-start
  0.6 0.0 copy-start.1
  0.7 1.1 %shard_map.95 = (f32[3,4,1024]{2,1,0:T(4,128)S(1)}, f32[3,4,1024]{2,1,0:T(4,128)S(1)}, f32[8,8,128]{2,1,0:T(8,128)S(1)}, s32[4,8,128]{2,1,0:T(8,128)S(1)}) custom-call(f32[2,32,1024]{2,1,0:T(8,128)} %bitcast.7, s32[32,1024]{1,0:T(8,128)} %class_ref.1, f32[8]{0:T(128)} %cond_hbm.1, s32[2]{0:T(128)} %row_hbm.1, s32[2]{0:T(128)} %col_hbm.1), custom_call_target="tpu_custom_call" | custom-call | tf_op jit(solution)/shard_map/pallas_call | solution.py:480
  1.7 0.0 copy-start.2
  1.7 0.7 %collective-permute-start = (f32[3,4,1024]{2,1,0:T(4,128)S(1)}, f32[3,4,1024]{2,1,0:T(4,128)S(1)}, u32[]{:S(2)}, u32[]{:S(2)}) collective-permute-start(f32[3,4,1024]{2,1,0:T(4,128)S(1)} %get-tuple-element.26), channel_id=1, source_target_pairs={{1,2},{3,4},{5,6},{2,1},{4,3},{6,5},{9,10},{11,12},{13,14},{10,9},... | collective-permute-start | bytes 147464 | tf_op jit(solution)/shard_map/ppermute | solution.py:499
  2.4 4.4 %collective-permute-start.1 = (f32[3,4,1024]{2,1,0:T(4,128)S(1)}, f32[3,4,1024]{2,1,0:T(4,128)S(1)}, u32[]{:S(2)}, u32[]{:S(2)}) collective-permute-start(f32[3,4,1024]{2,1,0:T(4,128)S(1)} %get-tuple-element.27), channel_id=1, source_target_pairs={{0,1},{1,0},{2,3},{3,2},{4,5},{5,4},{6,7},{7,6},{8,9},{9,8},{10,11... | collective-permute-start | bytes 147464 | tf_op jit(solution)/shard_map/ppermute | solution.py:33
  6.8 0.0 copy-done.2
  7.5 0.0 copy-done
  7.5 0.0 copy-done.1
  7.5 1.1 %shard_map.96 = (f32[2,8,40,128]{3,2,1,0:T(8,128)S(1)}, f32[2,8,40,128]{3,2,1,0:T(8,128)S(1)}, f32[2,8,40,128]{3,2,1,0:T(8,128)S(1)}, f32[2,8,40,128]{3,2,1,0:T(...) custom-call(f32[2,32,1024]{2,1,0:T(8,128)S(1)} %bitcast.8, ...), custom_call_target="tpu_custom_call" | custom-call | tf_op jit(solution)/shard_map/pallas_call | solution.py:91
  8.6 0.0 collective-permute-done.far_ref
  8.6 0.0 collective-permute-done.1.near_ref
  8.6 0.7 %shard_map.97 = (f32[2,2,8,8,128]{4,3,2,1,0:T(8,128)S(1)}, f32[2,2,8,8,128]{4,3,2,1,0:T(8,128)S(1)}, f32[2,2,8,8,128]{4,3,2,1,0:T(8,128)S(1)}, f32[2,2,8,8,128]{4,3,2,1,0:T(8,128)S(1)}, f32[24,128]{1,0:T(8,128)S(1)}) custom-call(f32[3,4,1024]{2,1,0:T(4,128)S(1)} %collective-permute-done.far_ref, f32[3,4,1024]{2,1,0:T(4,128)S(1)} %collective-permute-done.1.near_ref, ...), custom_call_target="tpu_custom_call" | custom-call | tf_op jit(solution)/shard_map/pallas_call | solution.py:91
  9.3 0.1 collective-permute-start.2
  9.3 1.2 %collective-permute-done.2 = f32[24,128]{1,0:T(8,128)S(1)} collective-permute-done((f32[24,128]{1,0:T(8,128)S(1)}, f32[24,128]{1,0:T(8,128)S(1)}, u32[]{:S(2)}, u32[]{:S(2)}) %collective-permute-start.2) | collective-permute-done | bytes 12320 | tf_op jit(solution)/shard_map/ppermute | solution.py:33
  10.5 2.9 %collective-permute-start.3 = (f32[24,128]{1,0:T(8,128)S(1)}, f32[24,128]{1,0:T(8,128)S(1)}, u32[]{:S(2)}, u32[]{:S(2)}) collective-permute-start(f32[24,128]{1,0:T(8,128)S(1)} %add.5.refs_0_), channel_id=1, source_target_pairs={{0,6},{1,7},{2,4},{3,5},{4,2},{5,3},{6,0},{7,1},{8,14},{9,15},{10,... | collective-permute-start | bytes 36872 | tf_op jit(solution)/shard_map/ppermute | solution.py:33
  13.4 0.9 %collective-permute-start.4 = (f32[24,128]{1,0:T(8,128)S(1)}, f32[24,128]{1,0:T(8,128)S(1)}, u32[]{:S(2)}, u32[]{:S(2)}) collective-permute-start(f32[24,128]{1,0:T(8,128)S(1)} %add.5.refs_0_), channel_id=1, source_target_pairs={{0,4},{1,5},{2,6},{3,7},{4,0},{5,1},{6,2},{7,3},{8,12},{9,13},{10,... | collective-permute-start | bytes 36872 | tf_op jit(solution)/shard_map/ppermute | solution.py:33
  14.3 0.1 collective-permute-start.5
  15.1 0.1 collective-permute-done.3.refs_1_
  15.1 2.0 %collective-permute-done.4.refs_2_ = f32[24,128]{1,0:T(8,128)S(1)} collective-permute-done((f32[24,128]{1,0:T(8,128)S(1)}, f32[24,128]{1,0:T(8,128)S(1)}, u32[]{:S(2)}, u32[]{:S(2)}) %collective-permute-start.4) | collective-permute-done | bytes 12320 | tf_op jit(solution)/shard_map/ppermute | solution.py:33
  17.1 0.9 %collective-permute-done.5.refs_3_ = f32[24,128]{1,0:T(8,128)S(1)} collective-permute-done((f32[24,128]{1,0:T(8,128)S(1)}, f32[24,128]{1,0:T(8,128)S(1)}, u32[]{:S(2)}, u32[]{:S(2)}) %collective-permute-start.5) | collective-permute-done | bytes 12320 | tf_op jit(solution)/shard_map/ppermute | solution.py:33
  18.0 0.3 %shard_map.98 = (f32[72,256]{1,0:T(8,128)S(1)}, f32[72,256]{1,0:T(8,128)S(1)}, f32[72,256]{1,0:T(8,128)S(1)}, f32[72,256]{1,0:T(8,128)S(1)}) custom-call(f32[1,1]{1,0:T(1,128)} %bitcast.6.weight_ref, f32[24,128]{1,0:T(8,128)S(1)} %add.5.refs_0_, f32[24,128]{1,0:T(8,128)S(1)} %collective-permute-done.3.refs_1_, f32[24,128]{1,0:T(8,128)S(1)} %collective-permute-done.4.refs_2_, ...), custom_call_target="tpu_custom_call" | custom-call | tf_op jit(solution)/shard_map/pallas_call | solution.py:91
  18.4 3.7 %collective-permute-start.6 = (f32[72,256]{1,0:T(8,128)S(1)}, f32[72,256]{1,0:T(8,128)S(1)}, u32[]{:S(2)}, u32[]{:S(2)}) collective-permute-start(f32[72,256]{1,0:T(8,128)S(1)} %get-tuple-element.47), channel_id=1, source_target_pairs={{0,24},{8,16},{16,8},{24,0},{1,25},{9,17},{17,9},{25,1},{2,26},{10... | collective-permute-start | bytes 221192 | tf_op jit(solution)/shard_map/ppermute | solution.py:33
  22.1 0.0 collective-permute-start.7
  22.1 0.8 %collective-permute-start.8 = (f32[72,256]{1,0:T(8,128)S(1)}, f32[72,256]{1,0:T(8,128)S(1)}, u32[]{:S(2)}, u32[]{:S(2)}) collective-permute-start(f32[72,256]{1,0:T(8,128)S(1)} %get-tuple-element.49), channel_id=1, source_target_pairs={{0,16},{8,24},{16,0},{24,8},{1,17},{9,25},{17,1},{25,9},{2,18},{10... | collective-permute-start | bytes 221192 | tf_op jit(solution)/shard_map/ppermute | solution.py:33
  22.8 1.8 %collective-permute-done.6.refs_1_ = f32[72,256]{1,0:T(8,128)S(1)} collective-permute-done((f32[72,256]{1,0:T(8,128)S(1)}, f32[72,256]{1,0:T(8,128)S(1)}, u32[]{:S(2)}, u32[]{:S(2)}) %collective-permute-start.6) | collective-permute-done | bytes 73760 | tf_op jit(solution)/shard_map/ppermute | solution.py:33
  24.7 1.8 %collective-permute-done.7.refs_2_ = f32[72,256]{1,0:T(8,128)S(1)} collective-permute-done((f32[72,256]{1,0:T(8,128)S(1)}, f32[72,256]{1,0:T(8,128)S(1)}, u32[]{:S(2)}, u32[]{:S(2)}) %collective-permute-start.7) | collective-permute-done | bytes 73760 | tf_op jit(solution)/shard_map/ppermute | solution.py:33
  26.4 0.9 %collective-permute-done.8.refs_3_ = f32[72,256]{1,0:T(8,128)S(1)} collective-permute-done((f32[72,256]{1,0:T(8,128)S(1)}, f32[72,256]{1,0:T(8,128)S(1)}, u32[]{:S(2)}, u32[]{:S(2)}) %collective-permute-start.8) | collective-permute-done | bytes 73760 | tf_op jit(solution)/shard_map/ppermute | solution.py:33
  27.3 0.6 %shard_map.99 = (f32[2,32,256]{2,1,0:T(8,128)}, f32[2,64]{1,0:T(2,128)}) custom-call(f32[72,256]{1,0:T(8,128)S(1)} %get-tuple-element.46.refs_0_, f32[72,256]{1,0:T(8,128)S(1)} %collective-permute-done.6.refs_1_, f32[72,256]{1,0:T(8,128)S(1)} %collective-permute-done.7.refs_2_, f32[72,256]{1,0:T(8,128)S(1)} %collective-permute-done.8.refs_3_), custom_call_target="tpu_custom_call" | custom-call | tf_op jit(solution)/shard_map/pallas_call | solution.py:91
  (2 shorter events, 0.0 us)
Async XLA Ops:
  0.6 6.8 %copy-start = (f32[1,2,32,1024]{3,2,1,0:T(8,128)S(1)}, f32[1,2,32,1024]{3,2,1,0:T(8,128)}, u32[]{:S(2)}) copy-start(f32[1,2,32,1024]{3,2,1,0:T(8,128)} %param.8) | copy-start | bytes 786436
  0.6 6.8 %copy-start.1 = (s32[32,1024]{1,0:T(8,128)S(1)}, s32[32,1024]{1,0:T(8,128)}, u32[]{:S(2)}) copy-start(s32[32,1024]{1,0:T(8,128)} %class_ref.1) | copy-start | bytes 393220
  1.7 5.1 %copy-start.2 = (s32[64]{0:T(128)S(1)}, s32[64]{0:T(128)}, u32[]{:S(2)}) copy-start(s32[64]{0:T(128)} %param.15) | copy-start | bytes 772
  1.7 6.8 %collective-permute-start = (f32[3,4,1024]{2,1,0:T(4,128)S(1)}, f32[3,4,1024]{2,1,0:T(4,128)S(1)}, u32[]{:S(2)}, u32[]{:S(2)}) collective-permute-start(f32[3,4,1024]{2,1,0:T(4,128)S(1)} %get-tuple-element.26), channel_id=1, source_target_pairs={{1,2},{3,4},{5,6},{2,1},{4,3},{6,5},{9,10},{11,12},{13,14},{10,9},... | collective-permute-start | bytes 147464 | tf_op jit(solution)/shard_map/ppermute | solution.py:499
  2.4 6.2 %collective-permute-start.1 = (f32[3,4,1024]{2,1,0:T(4,128)S(1)}, f32[3,4,1024]{2,1,0:T(4,128)S(1)}, u32[]{:S(2)}, u32[]{:S(2)}) collective-permute-start(f32[3,4,1024]{2,1,0:T(4,128)S(1)} %get-tuple-element.27), channel_id=1, source_target_pairs={{0,1},{1,0},{2,3},{3,2},{4,5},{5,4},{6,7},{7,6},{8,9},{9,8},{10,11... | collective-permute-start | bytes 147464 | tf_op jit(solution)/shard_map/ppermute | solution.py:33
  9.3 1.2 %collective-permute-start.2 = (f32[24,128]{1,0:T(8,128)S(1)}, f32[24,128]{1,0:T(8,128)S(1)}, u32[]{:S(2)}, u32[]{:S(2)}) collective-permute-start(f32[24,128]{1,0:T(8,128)S(1)} %get-tuple-element.41), channel_id=1, source_target_pairs={{0,1},{1,0},{2,3},{3,2},{4,5},{5,4},{6,7},{7,6},{8,9},{9,8},{10,11... | collective-permute-start | bytes 36872 | tf_op jit(solution)/shard_map/ppermute | solution.py:33
  10.5 4.6 %collective-permute-start.3 = (f32[24,128]{1,0:T(8,128)S(1)}, f32[24,128]{1,0:T(8,128)S(1)}, u32[]{:S(2)}, u32[]{:S(2)}) collective-permute-start(f32[24,128]{1,0:T(8,128)S(1)} %add.5.refs_0_), channel_id=1, source_target_pairs={{0,6},{1,7},{2,4},{3,5},{4,2},{5,3},{6,0},{7,1},{8,14},{9,15},{10,... | collective-permute-start | bytes 36872 | tf_op jit(solution)/shard_map/ppermute | solution.py:33
  13.4 3.7 %collective-permute-start.4 = (f32[24,128]{1,0:T(8,128)S(1)}, f32[24,128]{1,0:T(8,128)S(1)}, u32[]{:S(2)}, u32[]{:S(2)}) collective-permute-start(f32[24,128]{1,0:T(8,128)S(1)} %add.5.refs_0_), channel_id=1, source_target_pairs={{0,4},{1,5},{2,6},{3,7},{4,0},{5,1},{6,2},{7,3},{8,12},{9,13},{10,... | collective-permute-start | bytes 36872 | tf_op jit(solution)/shard_map/ppermute | solution.py:33
  14.3 3.7 %collective-permute-start.5 = (f32[24,128]{1,0:T(8,128)S(1)}, f32[24,128]{1,0:T(8,128)S(1)}, u32[]{:S(2)}, u32[]{:S(2)}) collective-permute-start(f32[24,128]{1,0:T(8,128)S(1)} %add.5.refs_0_), channel_id=1, source_target_pairs={{0,2},{1,3},{2,0},{3,1},{4,6},{5,7},{6,4},{7,5},{8,10},{9,11},{10,... | collective-permute-start | bytes 36872 | tf_op jit(solution)/shard_map/ppermute | solution.py:33
  18.4 6.3 %collective-permute-start.6 = (f32[72,256]{1,0:T(8,128)S(1)}, f32[72,256]{1,0:T(8,128)S(1)}, u32[]{:S(2)}, u32[]{:S(2)}) collective-permute-start(f32[72,256]{1,0:T(8,128)S(1)} %get-tuple-element.47), channel_id=1, source_target_pairs={{0,24},{8,16},{16,8},{24,0},{1,25},{9,17},{17,9},{25,1},{2,26},{10... | collective-permute-start | bytes 221192 | tf_op jit(solution)/shard_map/ppermute | solution.py:33
  22.1 4.4 %collective-permute-start.7 = (f32[72,256]{1,0:T(8,128)S(1)}, f32[72,256]{1,0:T(8,128)S(1)}, u32[]{:S(2)}, u32[]{:S(2)}) collective-permute-start(f32[72,256]{1,0:T(8,128)S(1)} %get-tuple-element.48), channel_id=1, source_target_pairs={{0,8},{8,0},{16,24},{24,16},{1,9},{9,1},{17,25},{25,17},{2,10},{10... | collective-permute-start | bytes 221192 | tf_op jit(solution)/shard_map/ppermute | solution.py:33
  22.1 5.3 %collective-permute-start.8 = (f32[72,256]{1,0:T(8,128)S(1)}, f32[72,256]{1,0:T(8,128)S(1)}, u32[]{:S(2)}, u32[]{:S(2)}) collective-permute-start(f32[72,256]{1,0:T(8,128)S(1)} %get-tuple-element.49), channel_id=1, source_target_pairs={{0,16},{8,24},{16,0},{24,8},{1,17},{9,25},{17,1},{25,9},{2,18},{10... | collective-permute-start | bytes 221192 | tf_op jit(solution)/shard_map/ppermute | solution.py:33

commit v7 on v6

--- a/solution.py
+++ b/solution.py
@@ -305,8 +305,11 @@
     last = total - SUBLANES
     own = (jnp.logical_not(upper), upper)
 
+    inside = (tile > 0) & (tile < lax.axis_size("tile") - 1)
+
     def came_in(index, c):
-        far, near = far_ref[index, :, cols(c)], near_ref[index, :, cols(c)]
+        far = jnp.where(inside, far_ref[index, :, cols(c)], 0.0)
+        near = near_ref[index, :, cols(c)]
         return jnp.concatenate(
             [jnp.where(even, far, near), jnp.where(even, near, far)], axis=0
         )
@@ -495,8 +498,8 @@
         ],
         compiler_params=PARAMS,
     )(*[pltpu.with_memory_space_constraint(a, pltpu.HBM) for a in raw])
-    far_pairs = [(i, i + 1) for i in range(1, tiles - 1, 2)]
-    far = lax.ppermute(far, "tile", far_pairs + [(j, i) for i, j in far_pairs])
+    ring = [(i, (i + 1) % tiles) for i in range(1, tiles, 2)]
+    far = lax.ppermute(far, "tile", ring + [(j, i) for i, j in ring])
     near = swap(near, "tile", 1, tiles)
     total, chunks = rows + 2 * halo, depth // LANES
     picks = jnp.pad(electrode_row, (0, LANES - electrodes), constant_values=-1)[None]

time: 28.1 us -> 26.3 us (0.936)
  starting transfers between devices: 13.5 us -> 12 us
  waiting for transfers between devices: 8.61 us -> 8.29 us
    ppermute x8, starting transfers between devices: 12.8 us -> 8.57 us  [swap(): return lax.ppermute(value, axis, [(i, i ^ mask) for i in range(size)])]
    ppermute x1, starting transfers between devices: 0.66 us -> 3.43 us  [shards(): far = lax.ppermute(far, 'tile', ring + [(j, i) for i, j in ring])]
    ppermute x8, waiting for transfers between devices: 8.61 us -> 8.29 us  [swap(): return lax.ppermute(value, axis, [(i, i ^ mask) for i in range(size)])]
where the time goes in v7:
time: 26.3 us; the launch traced here: 26.1 us
  starting transfers between devices  12 us (46%)
  waiting for transfers between devices  8.29 us (32%)
  Pallas kernels  3.8 us (14%)
  between operations  2.03 us (8%)
    ppermute x8, starting transfers between devices, swap(): return lax.ppermute(value, axis, [(i, i ^ mask) for i in range(size)])  8.57 us
    ppermute x8, waiting for transfers between devices, swap(): return lax.ppermute(value, axis, [(i, i ^ mask) for i in range(size)])  8.29 us
    ppermute x1, starting transfers between devices, shards(): far = lax.ppermute(far, 'tile', ring + [(j, i) for i, j in ring])  3.43 us
    pallas_call x4, Pallas kernels, vmem_call(): pl.pallas_call(kernel, out_shape=out_shape, in_specs=[VMEM] * len(inputs)...  2.74 us
    pallas_call x1, Pallas kernels, shards(): pl.pallas_call(edge_kernel, out_shape=[rim, rim, jax.ShapeDtypeStruct((n_...  1.06 us
  transfers between devices with their start and end apart: 9, of which 7 were waited for; matrix products, arithmetic and copies ran while one was open for 0% of the time, Pallas kernels for 4%

profile of v7, /device:TPU:0, one launch (start us, length us, event | category | flops | bytes accessed | tf_op | source)
XLA Modules:
  0.0 26.1 jit_solution(17032159393147612084)
XLA Ops:
  0.6 0.0 copy-start
  0.6 0.0 copy-start.1
  0.7 1.1 %shard_map.95 = (f32[3,4,1024]{2,1,0:T(4,128)S(1)}, f32[3,4,1024]{2,1,0:T(4,128)S(1)}, f32[8,8,128]{2,1,0:T(8,128)S(1)}, s32[4,8,128]{2,1,0:T(8,128)S(1)}) custom-call(f32[2,32,1024]{2,1,0:T(8,128)} %bitcast.7, s32[32,1024]{1,0:T(8,128)} %class_ref.1, f32[8]{0:T(128)} %cond_hbm.1, s32[2]{0:T(128)} %row_hbm.1, s32[2]{0:T(128)} %col_hbm.1), custom_call_target="tpu_custom_call" | custom-call | tf_op jit(solution)/shard_map/pallas_call | solution.py:483
  1.7 0.0 copy-start.2
  1.7 3.4 %collective-permute-start = (f32[3,4,1024]{2,1,0:T(4,128)S(1)}, f32[3,4,1024]{2,1,0:T(4,128)S(1)}, u32[]{:S(2)}, u32[]{:S(2)}) collective-permute-start(f32[3,4,1024]{2,1,0:T(4,128)S(1)} %get-tuple-element.26), channel_id=1, source_target_pairs={{1,2},{3,4},{5,6},{7,0},{2,1},{4,3},{6,5},{0,7},{9,10},{11,12},{13... | collective-permute-start | bytes 147464 | tf_op jit(solution)/shard_map/ppermute | solution.py:502
  5.2 0.0 collective-permute-start.1
  5.2 0.0 copy-done.2
  5.8 0.0 copy-done
  5.8 0.0 copy-done.1
  5.8 1.1 %shard_map.96 = (f32[2,8,40,128]{3,2,1,0:T(8,128)S(1)}, f32[2,8,40,128]{3,2,1,0:T(8,128)S(1)}, f32[2,8,40,128]{3,2,1,0:T(8,128)S(1)}, f32[2,8,40,128]{3,2,1,0:T(...) custom-call(f32[2,32,1024]{2,1,0:T(8,128)S(1)} %bitcast.8, ...), custom_call_target="tpu_custom_call" | custom-call | tf_op jit(solution)/shard_map/pallas_call | solution.py:91
  6.9 0.0 collective-permute-done.far_ref
  6.9 0.0 collective-permute-done.1.near_ref
  7.0 0.7 %shard_map.97 = (f32[2,2,8,8,128]{4,3,2,1,0:T(8,128)S(1)}, f32[2,2,8,8,128]{4,3,2,1,0:T(8,128)S(1)}, f32[2,2,8,8,128]{4,3,2,1,0:T(8,128)S(1)}, f32[2,2,8,8,128]{4,3,2,1,0:T(8,128)S(1)}, f32[24,128]{1,0:T(8,128)S(1)}) custom-call(f32[3,4,1024]{2,1,0:T(4,128)S(1)} %collective-permute-done.far_ref, f32[3,4,1024]{2,1,0:T(4,128)S(1)} %collective-permute-done.1.near_ref, ...), custom_call_target="tpu_custom_call" | custom-call | tf_op jit(solution)/shard_map/pallas_call | solution.py:91
  7.6 0.6 %collective-permute-start.2 = (f32[24,128]{1,0:T(8,128)S(1)}, f32[24,128]{1,0:T(8,128)S(1)}, u32[]{:S(2)}, u32[]{:S(2)}) collective-permute-start(f32[24,128]{1,0:T(8,128)S(1)} %get-tuple-element.41), channel_id=1, source_target_pairs={{0,1},{1,0},{2,3},{3,2},{4,5},{5,4},{6,7},{7,6},{8,9},{9,8},{10,11... | collective-permute-start | bytes 36872 | tf_op jit(solution)/shard_map/ppermute | solution.py:33
  8.2 0.8 %collective-permute-done.2 = f32[24,128]{1,0:T(8,128)S(1)} collective-permute-done((f32[24,128]{1,0:T(8,128)S(1)}, f32[24,128]{1,0:T(8,128)S(1)}, u32[]{:S(2)}, u32[]{:S(2)}) %collective-permute-start.2) | collective-permute-done | bytes 12320 | tf_op jit(solution)/shard_map/ppermute | solution.py:33
  9.0 2.6 %collective-permute-start.3 = (f32[24,128]{1,0:T(8,128)S(1)}, f32[24,128]{1,0:T(8,128)S(1)}, u32[]{:S(2)}, u32[]{:S(2)}) collective-permute-start(f32[24,128]{1,0:T(8,128)S(1)} %add.5.refs_0_), channel_id=1, source_target_pairs={{0,6},{1,7},{2,4},{3,5},{4,2},{5,3},{6,0},{7,1},{8,14},{9,15},{10,... | collective-permute-start | bytes 36872 | tf_op jit(solution)/shard_map/ppermute | solution.py:33
  11.6 0.9 %collective-permute-start.4 = (f32[24,128]{1,0:T(8,128)S(1)}, f32[24,128]{1,0:T(8,128)S(1)}, u32[]{:S(2)}, u32[]{:S(2)}) collective-permute-start(f32[24,128]{1,0:T(8,128)S(1)} %add.5.refs_0_), channel_id=1, source_target_pairs={{0,4},{1,5},{2,6},{3,7},{4,0},{5,1},{6,2},{7,3},{8,12},{9,13},{10,... | collective-permute-start | bytes 36872 | tf_op jit(solution)/shard_map/ppermute | solution.py:33
  12.5 0.1 collective-permute-start.5
  13.2 0.4 %collective-permute-done.3.refs_1_ = f32[24,128]{1,0:T(8,128)S(1)} collective-permute-done((f32[24,128]{1,0:T(8,128)S(1)}, f32[24,128]{1,0:T(8,128)S(1)}, u32[]{:S(2)}, u32[]{:S(2)}) %collective-permute-start.3) | collective-permute-done | bytes 12320 | tf_op jit(solution)/shard_map/ppermute | solution.py:33
  13.6 1.7 %collective-permute-done.4.refs_2_ = f32[24,128]{1,0:T(8,128)S(1)} collective-permute-done((f32[24,128]{1,0:T(8,128)S(1)}, f32[24,128]{1,0:T(8,128)S(1)}, u32[]{:S(2)}, u32[]{:S(2)}) %collective-permute-start.4) | collective-permute-done | bytes 12320 | tf_op jit(solution)/shard_map/ppermute | solution.py:33
  15.3 0.9 %collective-permute-done.5.refs_3_ = f32[24,128]{1,0:T(8,128)S(1)} collective-permute-done((f32[24,128]{1,0:T(8,128)S(1)}, f32[24,128]{1,0:T(8,128)S(1)}, u32[]{:S(2)}, u32[]{:S(2)}) %collective-permute-start.5) | collective-permute-done | bytes 12320 | tf_op jit(solution)/shard_map/ppermute | solution.py:33
  16.2 0.3 %shard_map.98 = (f32[72,256]{1,0:T(8,128)S(1)}, f32[72,256]{1,0:T(8,128)S(1)}, f32[72,256]{1,0:T(8,128)S(1)}, f32[72,256]{1,0:T(8,128)S(1)}) custom-call(f32[1,1]{1,0:T(1,128)} %bitcast.6.weight_ref, f32[24,128]{1,0:T(8,128)S(1)} %add.5.refs_0_, f32[24,128]{1,0:T(8,128)S(1)} %collective-permute-done.3.refs_1_, f32[24,128]{1,0:T(8,128)S(1)} %collective-permute-done.4.refs_2_, ...), custom_call_target="tpu_custom_call" | custom-call | tf_op jit(solution)/shard_map/pallas_call | solution.py:91
  16.6 3.7 %collective-permute-start.6 = (f32[72,256]{1,0:T(8,128)S(1)}, f32[72,256]{1,0:T(8,128)S(1)}, u32[]{:S(2)}, u32[]{:S(2)}) collective-permute-start(f32[72,256]{1,0:T(8,128)S(1)} %get-tuple-element.47), channel_id=1, source_target_pairs={{0,24},{8,16},{16,8},{24,0},{1,25},{9,17},{17,9},{25,1},{2,26},{10... | collective-permute-start | bytes 221192 | tf_op jit(solution)/shard_map/ppermute | solution.py:33
  20.2 0.0 collective-permute-start.7
  20.2 0.8 %collective-permute-start.8 = (f32[72,256]{1,0:T(8,128)S(1)}, f32[72,256]{1,0:T(8,128)S(1)}, u32[]{:S(2)}, u32[]{:S(2)}) collective-permute-start(f32[72,256]{1,0:T(8,128)S(1)} %get-tuple-element.49), channel_id=1, source_target_pairs={{0,16},{8,24},{16,0},{24,8},{1,17},{9,25},{17,1},{25,9},{2,18},{10... | collective-permute-start | bytes 221192 | tf_op jit(solution)/shard_map/ppermute | solution.py:33
  21.0 1.8 %collective-permute-done.6.refs_1_ = f32[72,256]{1,0:T(8,128)S(1)} collective-permute-done((f32[72,256]{1,0:T(8,128)S(1)}, f32[72,256]{1,0:T(8,128)S(1)}, u32[]{:S(2)}, u32[]{:S(2)}) %collective-permute-start.6) | collective-permute-done | bytes 73760 | tf_op jit(solution)/shard_map/ppermute | solution.py:33
  22.9 1.8 %collective-permute-done.7.refs_2_ = f32[72,256]{1,0:T(8,128)S(1)} collective-permute-done((f32[72,256]{1,0:T(8,128)S(1)}, f32[72,256]{1,0:T(8,128)S(1)}, u32[]{:S(2)}, u32[]{:S(2)}) %collective-permute-start.7) | collective-permute-done | bytes 73760 | tf_op jit(solution)/shard_map/ppermute | solution.py:33
  24.6 0.9 %collective-permute-done.8.refs_3_ = f32[72,256]{1,0:T(8,128)S(1)} collective-permute-done((f32[72,256]{1,0:T(8,128)S(1)}, f32[72,256]{1,0:T(8,128)S(1)}, u32[]{:S(2)}, u32[]{:S(2)}) %collective-permute-start.8) | collective-permute-done | bytes 73760 | tf_op jit(solution)/shard_map/ppermute | solution.py:33
  25.5 0.6 %shard_map.99 = (f32[2,32,256]{2,1,0:T(8,128)}, f32[2,64]{1,0:T(2,128)}) custom-call(f32[72,256]{1,0:T(8,128)S(1)} %get-tuple-element.46.refs_0_, f32[72,256]{1,0:T(8,128)S(1)} %collective-permute-done.6.refs_1_, f32[72,256]{1,0:T(8,128)S(1)} %collective-permute-done.7.refs_2_, f32[72,256]{1,0:T(8,128)S(1)} %collective-permute-done.8.refs_3_), custom_call_target="tpu_custom_call" | custom-call | tf_op jit(solution)/shard_map/pallas_call | solution.py:91
  (2 shorter events, 0.0 us)
Async XLA Ops:
  0.6 5.2 %copy-start = (f32[1,2,32,1024]{3,2,1,0:T(8,128)S(1)}, f32[1,2,32,1024]{3,2,1,0:T(8,128)}, u32[]{:S(2)}) copy-start(f32[1,2,32,1024]{3,2,1,0:T(8,128)} %param.8) | copy-start | bytes 786436
  0.6 5.2 %copy-start.1 = (s32[32,1024]{1,0:T(8,128)S(1)}, s32[32,1024]{1,0:T(8,128)}, u32[]{:S(2)}) copy-start(s32[32,1024]{1,0:T(8,128)} %class_ref.1) | copy-start | bytes 393220
  1.7 3.4 %copy-start.2 = (s32[64]{0:T(128)S(1)}, s32[64]{0:T(128)}, u32[]{:S(2)}) copy-start(s32[64]{0:T(128)} %param.15) | copy-start | bytes 772
  1.7 5.2 %collective-permute-start = (f32[3,4,1024]{2,1,0:T(4,128)S(1)}, f32[3,4,1024]{2,1,0:T(4,128)S(1)}, u32[]{:S(2)}, u32[]{:S(2)}) collective-permute-start(f32[3,4,1024]{2,1,0:T(4,128)S(1)} %get-tuple-element.26), channel_id=1, source_target_pairs={{1,2},{3,4},{5,6},{7,0},{2,1},{4,3},{6,5},{0,7},{9,10},{11,12},{13... | collective-permute-start | bytes 147464 | tf_op jit(solution)/shard_map/ppermute | solution.py:502
  5.2 1.8 %collective-permute-start.1 = (f32[3,4,1024]{2,1,0:T(4,128)S(1)}, f32[3,4,1024]{2,1,0:T(4,128)S(1)}, u32[]{:S(2)}, u32[]{:S(2)}) collective-permute-start(f32[3,4,1024]{2,1,0:T(4,128)S(1)} %get-tuple-element.27), channel_id=1, source_target_pairs={{0,1},{1,0},{2,3},{3,2},{4,5},{5,4},{6,7},{7,6},{8,9},{9,8},{10,11... | collective-permute-start | bytes 147464 | tf_op jit(solution)/shard_map/ppermute | solution.py:33
  7.6 1.4 %collective-permute-start.2 = (f32[24,128]{1,0:T(8,128)S(1)}, f32[24,128]{1,0:T(8,128)S(1)}, u32[]{:S(2)}, u32[]{:S(2)}) collective-permute-start(f32[24,128]{1,0:T(8,128)S(1)} %get-tuple-element.41), channel_id=1, source_target_pairs={{0,1},{1,0},{2,3},{3,2},{4,5},{5,4},{6,7},{7,6},{8,9},{9,8},{10,11... | collective-permute-start | bytes 36872 | tf_op jit(solution)/shard_map/ppermute | solution.py:33
  9.0 4.6 %collective-permute-start.3 = (f32[24,128]{1,0:T(8,128)S(1)}, f32[24,128]{1,0:T(8,128)S(1)}, u32[]{:S(2)}, u32[]{:S(2)}) collective-permute-start(f32[24,128]{1,0:T(8,128)S(1)} %add.5.refs_0_), channel_id=1, source_target_pairs={{0,6},{1,7},{2,4},{3,5},{4,2},{5,3},{6,0},{7,1},{8,14},{9,15},{10,... | collective-permute-start | bytes 36872 | tf_op jit(solution)/shard_map/ppermute | solution.py:33
  11.6 3.7 %collective-permute-start.4 = (f32[24,128]{1,0:T(8,128)S(1)}, f32[24,128]{1,0:T(8,128)S(1)}, u32[]{:S(2)}, u32[]{:S(2)}) collective-permute-start(f32[24,128]{1,0:T(8,128)S(1)} %add.5.refs_0_), channel_id=1, source_target_pairs={{0,4},{1,5},{2,6},{3,7},{4,0},{5,1},{6,2},{7,3},{8,12},{9,13},{10,... | collective-permute-start | bytes 36872 | tf_op jit(solution)/shard_map/ppermute | solution.py:33
  12.5 3.7 %collective-permute-start.5 = (f32[24,128]{1,0:T(8,128)S(1)}, f32[24,128]{1,0:T(8,128)S(1)}, u32[]{:S(2)}, u32[]{:S(2)}) collective-permute-start(f32[24,128]{1,0:T(8,128)S(1)} %add.5.refs_0_), channel_id=1, source_target_pairs={{0,2},{1,3},{2,0},{3,1},{4,6},{5,7},{6,4},{7,5},{8,10},{9,11},{10,... | collective-permute-start | bytes 36872 | tf_op jit(solution)/shard_map/ppermute | solution.py:33
  16.6 6.3 %collective-permute-start.6 = (f32[72,256]{1,0:T(8,128)S(1)}, f32[72,256]{1,0:T(8,128)S(1)}, u32[]{:S(2)}, u32[]{:S(2)}) collective-permute-start(f32[72,256]{1,0:T(8,128)S(1)} %get-tuple-element.47), channel_id=1, source_target_pairs={{0,24},{8,16},{16,8},{24,0},{1,25},{9,17},{17,9},{25,1},{2,26},{10... | collective-permute-start | bytes 221192 | tf_op jit(solution)/shard_map/ppermute | solution.py:33
  20.2 4.4 %collective-permute-start.7 = (f32[72,256]{1,0:T(8,128)S(1)}, f32[72,256]{1,0:T(8,128)S(1)}, u32[]{:S(2)}, u32[]{:S(2)}) collective-permute-start(f32[72,256]{1,0:T(8,128)S(1)} %get-tuple-element.48), channel_id=1, source_target_pairs={{0,8},{8,0},{16,24},{24,16},{1,9},{9,1},{17,25},{25,17},{2,10},{10... | collective-permute-start | bytes 221192 | tf_op jit(solution)/shard_map/ppermute | solution.py:33
  20.2 5.3 %collective-permute-start.8 = (f32[72,256]{1,0:T(8,128)S(1)}, f32[72,256]{1,0:T(8,128)S(1)}, u32[]{:S(2)}, u32[]{:S(2)}) collective-permute-start(f32[72,256]{1,0:T(8,128)S(1)} %get-tuple-element.49), channel_id=1, source_target_pairs={{0,16},{8,24},{16,0},{24,8},{1,17},{9,25},{17,1},{25,9},{2,18},{10... | collective-permute-start | bytes 221192 | tf_op jit(solution)/shard_map/ppermute | solution.py:33

commit v8 on v7

--- a/solution.py
+++ b/solution.py
@@ -6,6 +6,7 @@
 from jax.experimental import pallas as pl
 from jax.experimental.pallas import tpu as pltpu
 from jax.sharding import PartitionSpec as P
+
 
 ITERS = 3
 SOURCE_STRENGTH = 50.0
@@ -87,13 +88,14 @@
 PARAMS = pltpu.CompilerParams(vmem_limit_bytes=16 << 20)
 
 
-def vmem_call(kernel, out_shape, inputs, scratch=()):
+def vmem_call(kernel, out_shape, inputs, scratch=(), aliases=()):
     return pl.pallas_call(
         kernel,
         out_shape=out_shape,
         in_specs=[VMEM] * len(inputs),
         out_specs=jax.tree.map(lambda _: VMEM, out_shape),
         scratch_shapes=list(scratch),
+        input_output_aliases=dict(aliases),
         compiler_params=PARAMS,
     )(*inputs)
 
@@ -284,60 +286,57 @@
         pay_ref[i : i + 1, :] = line
 
 
-def outer_kernel(far_ref, near_ref, par_ref, pick_ref, *refs):
+def outer_kernel(even_end, wraps, came_ref, par_ref, pick_ref, *refs):
     x_in, *basis_in = refs[: 1 + ITERS]
     pay_in, sig_in, side_in, above_in, below_in, hit_in, square_in = refs[1 + ITERS : 8 + ITERS]
-    outs = refs[8 + ITERS :]
-    x_ref, *basis_refs = outs[: 1 + ITERS]
+    outs = refs[-(10 + ITERS) :]
+    x_out, *basis_outs = outs[: 1 + ITERS]
     pay_ref = outs[1 + ITERS]
     sigma_ref, west_raw, up_ref, down_ref, west_ref, east_ref, diag_ref, inv_ref = outs[2 + ITERS :]
     sources, chunks, total, _ = x_in.shape
-    n_class = par_ref.shape[0]
-    halo = far_ref.shape[1]
+    halo = came_ref.shape[1]
     rows = total - 2 * halo
     lane = lax.broadcasted_iota(jnp.int32, (SUBLANES, LANES), 1)
     row = lax.broadcasted_iota(jnp.int32, (SUBLANES, LANES), 0)
     tile = lax.axis_index("tile")
     even = tile % 2 == 0
     square = square_in[...]
-    values = [par_ref[i] for i in range(n_class)]
+    values = [par_ref[i] for i in range(par_ref.shape[0])]
     upper = row < halo
     last = total - SUBLANES
-    own = (jnp.logical_not(upper), upper)
-
     inside = (tile > 0) & (tile < lax.axis_size("tile") - 1)
 
     def came_in(index, c):
-        far = jnp.where(inside, far_ref[index, :, cols(c)], 0.0)
-        near = near_ref[index, :, cols(c)]
-        return jnp.concatenate(
-            [jnp.where(even, far, near), jnp.where(even, near, far)], axis=0
-        )
-
-    def set_in(new, kept):
-        return jnp.where(upper, new, kept[:SUBLANES]), jnp.where(upper, kept[last:], new)
-
-    for c in range(chunks):
-        sigma_ref[c] = conductivity(came_in(sources, c), values)
-        for s in range(sources):
-            x_ref[0, s, c], x_ref[1, s, c] = set_in(came_in(s, c), x_in.at[s, c])
-    for c, fresh, left, _ in neighbours(lambda c: sigma_ref[c], chunks, lane):
-        face = harmonic(left, fresh)
-        face = jnp.where(lane == 0, 0.0, face) if c == 0 else face
-        west_raw[0, c], west_raw[1, c] = set_in(face, side_in.at[c])
-    for e in (0, 1):
-        for c, west, _, east in neighbours(lambda c: west_raw[e, c], chunks, lane):
-            fresh = sigma_ref[c]
-            first, end = set_in(fresh, sig_in.at[c])
-            sigma = end if e else first
-            face = harmonic(
-                jnp.where(upper, pltpu.roll(first, SUBLANES - 1, 0), pltpu.roll(end, 1, 0)), fresh
-            )
+        value = came_ref[index, :, cols(c)]
+        if wraps:
+            value = jnp.where(inside, value, 0.0)
+        return jnp.concatenate([value, value], axis=0)
+
+    def one_end(e):
+        at = last if e else 0
+        tile_at = slice(at, at + SUBLANES)
+        own = upper if e else jnp.logical_not(upper)
+        x_ref, *basis_refs = [r.at[e] for r in (x_out, *basis_outs)]
+
+        def set_in(new, kept):
+            return jnp.where(own, kept[tile_at], new)
+
+        for c in range(chunks):
+            sigma_ref[c] = conductivity(came_in(sources, c), values)
+            for s in range(sources):
+                x_ref[s, c] = set_in(came_in(s, c), x_in.at[s, c])
+        for c, fresh, left, _ in neighbours(lambda c: sigma_ref[c], chunks, lane):
+            face = harmonic(left, fresh)
+            face = jnp.where(lane == 0, 0.0, face) if c == 0 else face
+            west_raw[c] = set_in(face, side_in.at[c])
+        for c, west, _, east in neighbours(lambda c: west_raw[c], chunks, lane):
+            sigma = set_in(sigma_ref[c], sig_in.at[c])
+            face = harmonic(pltpu.roll(sigma, 1 if e else SUBLANES - 1, 0), sigma)
             if e:
-                up = jnp.where(upper, above_in[c, last:], face)
+                up = set_in(face, above_in.at[c])
                 down = pltpu.roll(up, SUBLANES - 1, 0)
             else:
-                down = jnp.where(upper, face, below_in[c, :SUBLANES])
+                down = set_in(face, below_in.at[c])
                 up = pltpu.roll(down, 1, 0)
             diag = up + down + west + square * sigma
             if c == chunks - 1:
@@ -347,73 +346,75 @@
             else:
                 diag = diag + east
             inverse = 1.0 / jnp.maximum(diag, TINY)
-            diag_ref[e, c] = jnp.where(own[e], diag, 0.0)
-            inv_ref[e, c] = inverse
-            up_ref[e, c] = up * inverse
-            down_ref[e, c] = down * inverse
-            west_ref[e, c] = west * inverse
-            east_ref[e, c] = east * inverse
-
-    def spread(whole, e, s, c, here, left, right):
-        above = pltpu.roll(here, 1, 0)
-        below = pltpu.roll(here, SUBLANES - 1, 0)
-        if e:
-            above = jnp.where(row == 0, whole[s, c, last - 1 : last], above)
-        else:
-            below = jnp.where(row == SUBLANES - 1, whole[s, c, SUBLANES : SUBLANES + 1], below)
-        return (
-            up_ref[e, c] * above
-            + down_ref[e, c] * below
-            + west_ref[e, c] * left
-            + east_ref[e, c] * right
-        )
-
-    sums = {}
-    both = [(e, s) for e in (0, 1) for s in range(sources)]
-    for e, s in both:
-        for c, here, left, right in neighbours(lambda c: x_ref[e, s, c], chunks, lane):
-            new = hit_in[e, s, c] * inv_ref[e, c] - (
-                here - spread(x_in, e, s, c, here, left, right)
+            diag_ref[c] = jnp.where(own, diag, 0.0)
+            inv_ref[c] = inverse
+            up_ref[c] = up * inverse
+            down_ref[c] = down * inverse
+            west_ref[c] = west * inverse
+            east_ref[c] = east * inverse
+
+        def spread(whole, s, c, here, left, right):
+            above = pltpu.roll(here, 1, 0)
+            below = pltpu.roll(here, SUBLANES - 1, 0)
+            if e:
+                above = jnp.where(row == 0, whole[s, c, last - 1 : last], above)
+            else:
+                below = jnp.where(
+                    row == SUBLANES - 1, whole[s, c, SUBLANES : SUBLANES + 1], below
+                )
+            return (
+                up_ref[c] * above
+                + down_ref[c] * below
+                + west_ref[c] * left
+                + east_ref[c] * right
             )
-            basis_refs[0][e, s, c] = new
-            add(sums, (0, s), diag_ref[e, c] * new * new)
-    for i in range(ITERS):
-        for e, s in both:
-            for c, here, left, right in neighbours(
-                lambda c: basis_refs[i][e, s, c], chunks, lane
-            ):
-                new = spread(basis_in[i], e, s, c, here, left, right)
-                weighted = diag_ref[e, c] * new
-                add(sums, (2 * i + 1, s), weighted * here)
-                if i + 1 < ITERS:
-                    basis_refs[i + 1][e, s, c] = new
-                    add(sums, (2 * i + 2, s), weighted * new)
-    pickers = [
-        own[e] & (row + (tile * rows - halo + at) == pick_ref[...]) for e, at in ((0, 0), (1, last))
-    ]
-    tops = []
-    for ref in (x_ref, *basis_refs):
-        for s in range(sources):
-            line = 0.0
-            for e in (0, 1):
-                top = jnp.broadcast_to(ref[e, s, 0, :, 0:1], (SUBLANES, LANES))
-                line = line + jnp.where(pickers[e], top, 0.0)
-            tops.append(line_sum(line))
-    pay_ref[...] = pay_in[...]
-    for i, line in enumerate(lines_of(tops, sums, sources)):
-        pay_ref[i : i + 1, :] += line
-
-
-def combine_kernel(places, weight_ref, *refs):
+
+        sums = {}
+        for s in range(sources):
+            for c, here, left, right in neighbours(lambda c: x_ref[s, c], chunks, lane):
+                new = hit_in[e, s, c] * inv_ref[c] - (here - spread(x_in, s, c, here, left, right))
+                basis_refs[0][s, c] = new
+                add(sums, (0, s), diag_ref[c] * new * new)
+        for i in range(ITERS):
+            for s in range(sources):
+                for c, here, left, right in neighbours(
+                    lambda c: basis_refs[i][s, c], chunks, lane
+                ):
+                    new = spread(basis_in[i], s, c, here, left, right)
+                    weighted = diag_ref[c] * new
+                    add(sums, (2 * i + 1, s), weighted * here)
+                    if i + 1 < ITERS:
+                        basis_refs[i + 1][s, c] = new
+                        add(sums, (2 * i + 2, s), weighted * new)
+        picker = own & (row + (tile * rows - halo + at) == pick_ref[...])
+        tops = []
+        for ref in (x_ref, *basis_refs):
+            for s in range(sources):
+                top = jnp.broadcast_to(ref[s, 0, :, 0:1], (SUBLANES, LANES))
+                tops.append(line_sum(jnp.where(picker, top, 0.0)))
+        lines = lines_of(tops, sums, sources)
+        for i, line in enumerate(lines):
+            pay_ref[i : i + 1, :] = pay_in[i : i + 1, :] + line
+        pay_ref[len(lines) :, :] = pay_in[len(lines) :, :]
+
+    @pl.when(even)
+    def _():
+        one_end(even_end)
+
+    @pl.when(jnp.logical_not(even))
+    def _():
+        one_end(1 - even_end)
+
+
+def combine_kernel(places, halo, weight_ref, *refs):
     n_parts, n_pay = ITERS + 1, len(places)
     packed = tree_sum([refs[i][...] for i in places])
     part_refs = refs[n_pay : n_pay + n_parts]
     edge_refs = refs[n_pay + n_parts : n_pay + 2 * n_parts]
     out_refs = refs[n_pay + 2 * n_parts :]
     sources, _, total, _ = part_refs[0].shape
-    share = out_refs[0].shape[1]
-    rows = (out_refs[0].shape[0] - SUBLANES) // sources
-    halo = (total - rows) // 2
+    rows = total - 2 * halo
+    per = (out_refs[0].shape[0] - SUBLANES) // (rows * sources)
     first = n_parts * sources
     totals = jnp.sum(packed[first : first + 2 * ITERS * sources], axis=1, keepdims=True)
     poly = step_polynomial([totals[n * sources : (n + 1) * sources] for n in range(2 * ITERS)])
@@ -425,7 +426,6 @@
     ]
     split = len(out_refs) > 1
     wave = lax.axis_index("wave") if split else 0
-    per = share // LANES
     inner = slice(SUBLANES, total - SUBLANES)
     for mask, out_ref in enumerate(out_refs):
         block = wave ^ mask if split else 0
@@ -437,19 +437,23 @@
                     sum(scale[s][i] * edge_refs[i][e, s, c] for i in range(n_parts)) for e in (0, 1)
                 )
                 value = jnp.concatenate([top[halo:], middle, end[: SUBLANES - halo]], axis=0)
-                out_ref[s * rows : (s + 1) * rows, cols(k)] = value
-        out_ref[sources * rows :, :] = jnp.zeros((SUBLANES, share), jnp.float32)
-        for s in range(sources):
-            out_ref[sources * rows + s : sources * rows + s + 1, :LANES] = read[s]
+                out_ref[pl.ds((s * per + k) * rows, rows), :] = value
+        end_row = sources * per * rows
+        out_ref[end_row:, :] = jnp.zeros((SUBLANES, LANES), jnp.float32)
+        for s in range(sources):
+            out_ref[end_row + s : end_row + s + 1, :] = read[s]
 
 
 def sum_kernel(places, *refs):
     part_refs, (field_ref, read_ref) = [refs[i] for i in places], refs[-2:]
-    sources, rows, _ = field_ref.shape
+    sources, rows, share = field_ref.shape
     electrodes = read_ref.shape[1]
+    per = share // LANES
     for s in range(sources):
-        field_ref[s] = tree_sum([r[s * rows : (s + 1) * rows, :] for r in part_refs])
-    last = tree_sum([r[sources * rows :, :LANES] for r in part_refs])
+        for k in range(per):
+            at = pl.ds((s * per + k) * rows, rows)
+            field_ref[s, :, cols(k)] = tree_sum([r[at, :] for r in part_refs])
+    last = tree_sum([r[sources * per * rows :, :] for r in part_refs])
     read_ref[...] = last[:sources, :electrodes]
 
 
@@ -515,30 +519,43 @@
         [field, class_map, params, wavenumbers[None], spots, picks],
         [pltpu.VMEM((chunks, total, LANES), f32)] * 6,
     )
-    pair = pltpu.VMEM((2, chunks, SUBLANES, LANES), f32)
+    ready = list(inside)
+    scratch = [pltpu.VMEM((chunks, SUBLANES, LANES), f32)] * 8
     outside = vmem_call(
-        outer_kernel,
+        functools.partial(outer_kernel, 1, False),
         [ends] * (ITERS + 1) + [pay],
-        [far, near, params, picks, *inside],
-        [pltpu.VMEM((chunks, SUBLANES, LANES), f32)] + [pair] * 7,
+        [near, params, picks, *ready],
+        scratch,
+    )
+    ready[ITERS + 1] = outside[-1]
+    inputs = [far, params, picks, *ready, *outside[:-1]]
+    held = len(inputs) - (ITERS + 1)
+    outside = vmem_call(
+        functools.partial(outer_kernel, 0, True),
+        [ends] * (ITERS + 1) + [pay],
+        inputs,
+        scratch,
+        {held + i: i for i in range(ITERS + 1)},
     )
     packed = tile_parts(outside[-1], "tile")
     packed, places = issued(packed, (0, *range(len(packed) - 1, 0, -1)))
     share = depth // waves
     split = share % LANES == 0
     width = share if split else depth
-    block = jax.ShapeDtypeStruct((sources * rows + SUBLANES, width), f32)
+    n = sources * rows * width // LANES
+    block = jax.ShapeDtypeStruct((n + SUBLANES, LANES), f32)
     pieces = vmem_call(
-        functools.partial(combine_kernel, places),
+        functools.partial(combine_kernel, places, halo),
         [block] * (waves if split else 1),
         [weights[None], *packed, *inside[: ITERS + 1], *outside[: ITERS + 1]],
     )
     if not split:
-        n = sources * rows
         read = pieces[0][n : n + sources, :electrodes].reshape(-1, share)
+        whole = pieces[0][:n].reshape(sources, chunks, rows, LANES)
+        whole = whole.transpose(0, 2, 1, 3).reshape(sources * rows, depth)
         pieces = [
             jnp.concatenate(
-                [lax.dynamic_slice_in_dim(pieces[0][:n], (wave ^ mask) * share, share, 1), read]
+                [lax.dynamic_slice_in_dim(whole, (wave ^ mask) * share, share, 1), read]
             )
             for mask in range(waves)
         ]

time: 26.3 us -> 26.3 us (level)
  waiting for transfers between devices: 8.29 us -> 7.81 us
  Pallas kernels: 3.8 us -> 4.12 us
    ppermute x8, waiting for transfers between devices: 8.29 us -> 7.81 us  [swap(): return lax.ppermute(value, axis, [(i, i ^ mask) for i in range(size)])]
    pallas_call x4 -> x5, Pallas kernels: 2.74 us -> 3.06 us  [vmem_call(): pl.pallas_call(kernel, out_shape=out_shape, in_specs=[VMEM] * len(inputs)...]
  transfers between devices with their start and end apart: 9 -> 9, of which waited for: 7 -> 7; matrix products, arithmetic and copies ran while one was open for 0% -> 0% of each run, Pallas kernels for 4% -> 6%
where the time goes in v8:
time: 26.3 us; the launch traced here: 26.1 us
  starting transfers between devices  12.1 us (46%)
  waiting for transfers between devices  7.81 us (30%)
  Pallas kernels  4.12 us (16%)
  between operations  2.04 us (8%)
    ppermute x8, starting transfers between devices, swap(): return lax.ppermute(value, axis, [(i, i ^ mask) for i in range(size)])  8.57 us
    ppermute x8, waiting for transfers between devices, swap(): return lax.ppermute(value, axis, [(i, i ^ mask) for i in range(size)])  7.81 us
    ppermute x1, starting transfers between devices, shards(): far = lax.ppermute(far, 'tile', ring + [(j, i) for i, j in ring])  3.54 us
    pallas_call x5, Pallas kernels, vmem_call(): pl.pallas_call(kernel, out_shape=out_shape, in_specs=[VMEM] * len(inputs)...  3.06 us
    pallas_call x1, Pallas kernels, shards(): pl.pallas_call(edge_kernel, out_shape=[rim, rim, jax.ShapeDtypeStruct((n_...  1.06 us
  transfers between devices with their start and end apart: 9, of which 7 were waited for; matrix products, arithmetic and copies ran while one was open for 0% of the time, Pallas kernels for 6%

profile of v8, /device:TPU:0, one launch (start us, length us, event | category | flops | bytes accessed | tf_op | source)
XLA Modules:
  0.0 26.1 jit_solution(10375739613425324663)
XLA Ops:
  0.6 0.0 copy-start
  0.6 0.0 copy-start.1
  0.7 1.1 %shard_map.95 = (f32[3,4,1024]{2,1,0:T(4,128)S(1)}, f32[3,4,1024]{2,1,0:T(4,128)S(1)}, f32[8,8,128]{2,1,0:T(8,128)S(1)}, s32[4,8,128]{2,1,0:T(8,128)S(1)}) custom-call(f32[2,32,1024]{2,1,0:T(8,128)} %bitcast.7, s32[32,1024]{1,0:T(8,128)} %class_ref.1, f32[8]{0:T(128)} %cond_hbm.1, s32[2]{0:T(128)} %row_hbm.1, s32[2]{0:T(128)} %col_hbm.1), custom_call_target="tpu_custom_call" | custom-call | tf_op jit(solution)/shard_map/pallas_call | solution.py:487
  1.7 0.0 copy-start.2
  1.7 0.6 %collective-permute-start.1 = (f32[3,4,1024]{2,1,0:T(4,128)S(1)}, f32[3,4,1024]{2,1,0:T(4,128)S(1)}, u32[]{:S(2)}, u32[]{:S(2)}) collective-permute-start(f32[3,4,1024]{2,1,0:T(4,128)S(1)} %get-tuple-element.38), channel_id=1, source_target_pairs={{0,1},{1,0},{2,3},{3,2},{4,5},{5,4},{6,7},{7,6},{8,9},{9,8},{10,11... | collective-permute-start | bytes 147464 | tf_op jit(solution)/shard_map/ppermute | solution.py:34
  2.3 3.5 %collective-permute-start = (f32[3,4,1024]{2,1,0:T(4,128)S(1)}, f32[3,4,1024]{2,1,0:T(4,128)S(1)}, u32[]{:S(2)}, u32[]{:S(2)}) collective-permute-start(f32[3,4,1024]{2,1,0:T(4,128)S(1)} %get-tuple-element.31), channel_id=1, source_target_pairs={{1,2},{3,4},{5,6},{7,0},{2,1},{4,3},{6,5},{0,7},{9,10},{11,12},{13... | collective-permute-start | bytes 147464 | tf_op jit(solution)/shard_map/ppermute | solution.py:506
  5.8 0.0 copy-done.2
  6.5 0.0 copy-done
  6.5 0.0 copy-done.1
  6.5 1.1 %shard_map.96 = (f32[2,8,40,128]{3,2,1,0:T(8,128)S(1)}, f32[2,8,40,128]{3,2,1,0:T(8,128)S(1)}, f32[2,8,40,128]{3,2,1,0:T(8,128)S(1)}, f32[2,8,40,128]{3,2,1,0:T(...) custom-call(f32[2,32,1024]{2,1,0:T(8,128)S(1)} %bitcast.8, ...), custom_call_target="tpu_custom_call" | custom-call | tf_op jit(solution)/shard_map/pallas_call | solution.py:92
  7.6 0.0 collective-permute-done.1.came_ref
  7.6 0.5 %shard_map.97 = (f32[2,2,8,8,128]{4,3,2,1,0:T(8,128)S(1)}, f32[2,2,8,8,128]{4,3,2,1,0:T(8,128)S(1)}, f32[2,2,8,8,128]{4,3,2,1,0:T(8,128)S(1)}, f32[2,2,8,8,128]{4,3,2,1,0:T(8,128)S(1)}, f32[24,128]{1,0:T(8,128)S(1)}) custom-call(f32[3,4,1024]{2,1,0:T(4,128)S(1)} %collective-permute-done.1.came_ref, f32[8,8,128]{2,1,0:T(8,128)S(1)} %get-tuple-element.32.par_ref, ...), custom_call_target="tpu_custom_call" | custom-call | tf_op jit(solution)/shard_map/pallas_call | solution.py:92
  8.1 0.0 collective-permute-done.came_ref
  8.1 0.5 %shard_map.98 = (f32[2,2,8,8,128]{4,3,2,1,0:T(8,128)S(1)}, f32[2,2,8,8,128]{4,3,2,1,0:T(8,128)S(1)}, f32[2,2,8,8,128]{4,3,2,1,0:T(8,128)S(1)}, f32[2,2,8,8,128]{4,3,2,1,0:T(8,128)S(1)}, f32[24,128]{1,0:T(8,128)S(1)}) custom-call(f32[3,4,1024]{2,1,0:T(4,128)S(1)} %collective-permute-done.c, ...), custom_call_target="tpu_custom_call", output_to_operand_aliasing={{0}: (14, {}), {1}: (15, {}), {2}: (16, {}), {3}: (17, {})} | custom-call | tf_op jit(solution)/shard_map/pallas_call | solution.py:92
  8.6 0.1 collective-permute-start.2
  8.7 1.2 %collective-permute-done.2 = f32[24,128]{1,0:T(8,128)S(1)} collective-permute-done((f32[24,128]{1,0:T(8,128)S(1)}, f32[24,128]{1,0:T(8,128)S(1)}, u32[]{:S(2)}, u32[]{:S(2)}) %collective-permute-start.2) | collective-permute-done | bytes 12320 | tf_op jit(solution)/shard_map/ppermute | solution.py:34
  9.9 2.2 %collective-permute-start.3 = (f32[24,128]{1,0:T(8,128)S(1)}, f32[24,128]{1,0:T(8,128)S(1)}, u32[]{:S(2)}, u32[]{:S(2)}) collective-permute-start(f32[24,128]{1,0:T(8,128)S(1)} %add.5.refs_0_), channel_id=1, source_target_pairs={{0,6},{1,7},{2,4},{3,5},{4,2},{5,3},{6,0},{7,1},{8,14},{9,15},{10,... | collective-permute-start | bytes 36872 | tf_op jit(solution)/shard_map/ppermute | solution.py:34
  12.0 0.5 %collective-permute-start.4 = (f32[24,128]{1,0:T(8,128)S(1)}, f32[24,128]{1,0:T(8,128)S(1)}, u32[]{:S(2)}, u32[]{:S(2)}) collective-permute-start(f32[24,128]{1,0:T(8,128)S(1)} %add.5.refs_0_), channel_id=1, source_target_pairs={{0,4},{1,5},{2,6},{3,7},{4,0},{5,1},{6,2},{7,3},{8,12},{9,13},{10,... | collective-permute-start | bytes 36872 | tf_op jit(solution)/shard_map/ppermute | solution.py:34
  12.5 0.8 %collective-permute-start.5 = (f32[24,128]{1,0:T(8,128)S(1)}, f32[24,128]{1,0:T(8,128)S(1)}, u32[]{:S(2)}, u32[]{:S(2)}) collective-permute-start(f32[24,128]{1,0:T(8,128)S(1)} %add.5.refs_0_), channel_id=1, source_target_pairs={{0,2},{1,3},{2,0},{3,1},{4,6},{5,7},{6,4},{7,5},{8,10},{9,11},{10,... | collective-permute-start | bytes 36872 | tf_op jit(solution)/shard_map/ppermute | solution.py:34
  14.0 0.5 %collective-permute-done.3.refs_1_ = f32[24,128]{1,0:T(8,128)S(1)} collective-permute-done((f32[24,128]{1,0:T(8,128)S(1)}, f32[24,128]{1,0:T(8,128)S(1)}, u32[]{:S(2)}, u32[]{:S(2)}) %collective-permute-start.3) | collective-permute-done | bytes 12320 | tf_op jit(solution)/shard_map/ppermute | solution.py:34
  14.5 1.3 %collective-permute-done.4.refs_2_ = f32[24,128]{1,0:T(8,128)S(1)} collective-permute-done((f32[24,128]{1,0:T(8,128)S(1)}, f32[24,128]{1,0:T(8,128)S(1)}, u32[]{:S(2)}, u32[]{:S(2)}) %collective-permute-start.4) | collective-permute-done | bytes 12320 | tf_op jit(solution)/shard_map/ppermute | solution.py:34
  15.7 0.5 %collective-permute-done.5.refs_3_ = f32[24,128]{1,0:T(8,128)S(1)} collective-permute-done((f32[24,128]{1,0:T(8,128)S(1)}, f32[24,128]{1,0:T(8,128)S(1)}, u32[]{:S(2)}, u32[]{:S(2)}) %collective-permute-start.5) | collective-permute-done | bytes 12320 | tf_op jit(solution)/shard_map/ppermute | solution.py:34
  16.2 0.3 %shard_map.99 = (f32[136,128]{1,0:T(8,128)S(1)}, f32[136,128]{1,0:T(8,128)S(1)}, f32[136,128]{1,0:T(8,128)S(1)}, f32[136,128]{1,0:T(8,128)S(1)}) custom-call(f32[1,1]{1,0:T(1,128)} %bitcast.6.weight_ref, f32[24,128]{1,0:T(8,128)S(1)} %add.5.refs_0_, f32[24,128]{1,0:T(8,128)S(1)} %collective-permute-done.3.refs_1_, ...), custom_call_target="tpu_custom_call" | custom-call | tf_op jit(solution)/shard_map/pallas_call | solution.py:92
  16.6 3.7 %collective-permute-start.6 = (f32[136,128]{1,0:T(8,128)S(1)}, f32[136,128]{1,0:T(8,128)S(1)}, u32[]{:S(2)}, u32[]{:S(2)}) collective-permute-start(f32[136,128]{1,0:T(8,128)S(1)} %get-tuple-element.57), channel_id=1, source_target_pairs={{0,24},{8,16},{16,8},{24,0},{1,25},{9,17},{17,9},{25,1},{2,26},{10... | collective-permute-start | bytes 208904 | tf_op jit(solution)/shard_map/ppermute | solution.py:34
  20.2 0.0 collective-permute-start.7
  20.2 0.8 %collective-permute-start.8 = (f32[136,128]{1,0:T(8,128)S(1)}, f32[136,128]{1,0:T(8,128)S(1)}, u32[]{:S(2)}, u32[]{:S(2)}) collective-permute-start(f32[136,128]{1,0:T(8,128)S(1)} %get-tuple-element.59), channel_id=1, source_target_pairs={{0,16},{8,24},{16,0},{24,8},{1,17},{9,25},{17,1},{25,9},{2,18},{10... | collective-permute-start | bytes 208904 | tf_op jit(solution)/shard_map/ppermute | solution.py:34
  21.0 1.8 %collective-permute-done.6.refs_1_ = f32[136,128]{1,0:T(8,128)S(1)} collective-permute-done((f32[136,128]{1,0:T(8,128)S(1)}, f32[136,128]{1,0:T(8,128)S(1)}, u32[]{:S(2)}, u32[]{:S(2)}) %collective-permute-start.6) | collective-permute-done | bytes 69664 | tf_op jit(solution)/shard_map/ppermute | solution.py:34
  22.8 1.7 %collective-permute-done.7.refs_2_ = f32[136,128]{1,0:T(8,128)S(1)} collective-permute-done((f32[136,128]{1,0:T(8,128)S(1)}, f32[136,128]{1,0:T(8,128)S(1)}, u32[]{:S(2)}, u32[]{:S(2)}) %collective-permute-start.7) | collective-permute-done | bytes 69664 | tf_op jit(solution)/shard_map/ppermute | solution.py:34
  24.6 0.9 %collective-permute-done.8.refs_3_ = f32[136,128]{1,0:T(8,128)S(1)} collective-permute-done((f32[136,128]{1,0:T(8,128)S(1)}, f32[136,128]{1,0:T(8,128)S(1)}, u32[]{:S(2)}, u32[]{:S(2)}) %collective-permute-start.8) | collective-permute-done | bytes 69664 | tf_op jit(solution)/shard_map/ppermute | solution.py:34
  25.5 0.7 %shard_map.100 = (f32[2,32,256]{2,1,0:T(8,128)}, f32[2,64]{1,0:T(2,128)}) custom-call(f32[136,128]{1,0:T(8,128)S(1)} %get-tuple-element.56.refs_0_, f32[136,128]{1,0:T(8,128)S(1)} %collective-permute-done.6.refs_1_, f32[136,128]{1,0:T(8,128)S(1)} %collective-permute-done.7.refs_2_, f32[136,128]{1,0:T(8,128)S(1)} %collective-permute-done.8.refs_3_), custom_call_target="tpu_custom_call" | custom-call | tf_op jit(solution)/shard_map/pallas_call | solution.py:92
  (2 shorter events, 0.0 us)
Async XLA Ops:
  0.6 5.9 %copy-start = (f32[1,2,32,1024]{3,2,1,0:T(8,128)S(1)}, f32[1,2,32,1024]{3,2,1,0:T(8,128)}, u32[]{:S(2)}) copy-start(f32[1,2,32,1024]{3,2,1,0:T(8,128)} %param.8) | copy-start | bytes 786436
  0.6 5.9 %copy-start.1 = (s32[32,1024]{1,0:T(8,128)S(1)}, s32[32,1024]{1,0:T(8,128)}, u32[]{:S(2)}) copy-start(s32[32,1024]{1,0:T(8,128)} %class_ref.1) | copy-start | bytes 393220
  1.7 4.1 %copy-start.2 = (s32[64]{0:T(128)S(1)}, s32[64]{0:T(128)}, u32[]{:S(2)}) copy-start(s32[64]{0:T(128)} %param.15) | copy-start | bytes 772
  1.7 5.9 %collective-permute-start.1 = (f32[3,4,1024]{2,1,0:T(4,128)S(1)}, f32[3,4,1024]{2,1,0:T(4,128)S(1)}, u32[]{:S(2)}, u32[]{:S(2)}) collective-permute-start(f32[3,4,1024]{2,1,0:T(4,128)S(1)} %get-tuple-element.38), channel_id=1, source_target_pairs={{0,1},{1,0},{2,3},{3,2},{4,5},{5,4},{6,7},{7,6},{8,9},{9,8},{10,11... | collective-permute-start | bytes 147464 | tf_op jit(solution)/shard_map/ppermute | solution.py:34
  2.3 5.8 %collective-permute-start = (f32[3,4,1024]{2,1,0:T(4,128)S(1)}, f32[3,4,1024]{2,1,0:T(4,128)S(1)}, u32[]{:S(2)}, u32[]{:S(2)}) collective-permute-start(f32[3,4,1024]{2,1,0:T(4,128)S(1)} %get-tuple-element.31), channel_id=1, source_target_pairs={{1,2},{3,4},{5,6},{7,0},{2,1},{4,3},{6,5},{0,7},{9,10},{11,12},{13... | collective-permute-start | bytes 147464 | tf_op jit(solution)/shard_map/ppermute | solution.py:506
  8.6 1.2 %collective-permute-start.2 = (f32[24,128]{1,0:T(8,128)S(1)}, f32[24,128]{1,0:T(8,128)S(1)}, u32[]{:S(2)}, u32[]{:S(2)}) collective-permute-start(f32[24,128]{1,0:T(8,128)S(1)} %get-tuple-element.51), channel_id=1, source_target_pairs={{0,1},{1,0},{2,3},{3,2},{4,5},{5,4},{6,7},{7,6},{8,9},{9,8},{10,11... | collective-permute-start | bytes 36872 | tf_op jit(solution)/shard_map/ppermute | solution.py:34
  9.9 4.6 %collective-permute-start.3 = (f32[24,128]{1,0:T(8,128)S(1)}, f32[24,128]{1,0:T(8,128)S(1)}, u32[]{:S(2)}, u32[]{:S(2)}) collective-permute-start(f32[24,128]{1,0:T(8,128)S(1)} %add.5.refs_0_), channel_id=1, source_target_pairs={{0,6},{1,7},{2,4},{3,5},{4,2},{5,3},{6,0},{7,1},{8,14},{9,15},{10,... | collective-permute-start | bytes 36872 | tf_op jit(solution)/shard_map/ppermute | solution.py:34
  12.0 3.7 %collective-permute-start.4 = (f32[24,128]{1,0:T(8,128)S(1)}, f32[24,128]{1,0:T(8,128)S(1)}, u32[]{:S(2)}, u32[]{:S(2)}) collective-permute-start(f32[24,128]{1,0:T(8,128)S(1)} %add.5.refs_0_), channel_id=1, source_target_pairs={{0,4},{1,5},{2,6},{3,7},{4,0},{5,1},{6,2},{7,3},{8,12},{9,13},{10,... | collective-permute-start | bytes 36872 | tf_op jit(solution)/shard_map/ppermute | solution.py:34
  12.5 3.7 %collective-permute-start.5 = (f32[24,128]{1,0:T(8,128)S(1)}, f32[24,128]{1,0:T(8,128)S(1)}, u32[]{:S(2)}, u32[]{:S(2)}) collective-permute-start(f32[24,128]{1,0:T(8,128)S(1)} %add.5.refs_0_), channel_id=1, source_target_pairs={{0,2},{1,3},{2,0},{3,1},{4,6},{5,7},{6,4},{7,5},{8,10},{9,11},{10,... | collective-permute-start | bytes 36872 | tf_op jit(solution)/shard_map/ppermute | solution.py:34
  16.6 6.2 %collective-permute-start.6 = (f32[136,128]{1,0:T(8,128)S(1)}, f32[136,128]{1,0:T(8,128)S(1)}, u32[]{:S(2)}, u32[]{:S(2)}) collective-permute-start(f32[136,128]{1,0:T(8,128)S(1)} %get-tuple-element.57), channel_id=1, source_target_pairs={{0,24},{8,16},{16,8},{24,0},{1,25},{9,17},{17,9},{25,1},{2,26},{10... | collective-permute-start | bytes 208904 | tf_op jit(solution)/shard_map/ppermute | solution.py:34
  20.2 4.3 %collective-permute-start.7 = (f32[136,128]{1,0:T(8,128)S(1)}, f32[136,128]{1,0:T(8,128)S(1)}, u32[]{:S(2)}, u32[]{:S(2)}) collective-permute-start(f32[136,128]{1,0:T(8,128)S(1)} %get-tuple-element.58), channel_id=1, source_target_pairs={{0,8},{8,0},{16,24},{24,16},{1,9},{9,1},{17,25},{25,17},{2,10},{10... | collective-permute-start | bytes 208904 | tf_op jit(solution)/shard_map/ppermute | solution.py:34
  20.2 5.2 %collective-permute-start.8 = (f32[136,128]{1,0:T(8,128)S(1)}, f32[136,128]{1,0:T(8,128)S(1)}, u32[]{:S(2)}, u32[]{:S(2)}) collective-permute-start(f32[136,128]{1,0:T(8,128)S(1)} %get-tuple-element.59), channel_id=1, source_target_pairs={{0,16},{8,24},{16,0},{24,8},{1,17},{9,25},{17,1},{25,9},{2,18},{10... | collective-permute-start | bytes 208904 | tf_op jit(solution)/shard_map/ppermute | solution.py:34

commit v9 on v8

--- a/solution.py
+++ b/solution.py
@@ -11,6 +11,7 @@
 ITERS = 3
 SOURCE_STRENGTH = 50.0
 TINY = 1e-30
+LEAST_KEPT = 3e-4
 LANES = 128
 SUBLANES = 8
 
@@ -56,32 +57,43 @@
 
 
 def step_polynomial(moments):
-    def inner(poly):
-        return sum(a * b * moments[i + j] for i, a in enumerate(poly) for j, b in enumerate(poly))
-
-    def energy(poly):
-        return sum(
-            a * b * (moments[i + j] - moments[i + j + 1])
-            for i, a in enumerate(poly)
-            for j, b in enumerate(poly)
-        )
+    trusted = []
+
+    def product(poly, term):
+        value = size = 0.0
+        for i, a in enumerate(poly):
+            for j, b in enumerate(poly):
+                part, bound = term(i + j)
+                value = value + a * b * part
+                size = size + jnp.abs(a * b) * bound
+        trusted.append(value > LEAST_KEPT * size)
+        return value
+
+    def inner(n):
+        return moments[n], jnp.abs(moments[n])
+
+    def energy(n):
+        return moments[n] - moments[n + 1], jnp.abs(moments[n]) + jnp.abs(moments[n + 1])
 
     one = jnp.ones_like(moments[0])
     zero = jnp.zeros_like(moments[0])
     res, way, total = [one], [one], [zero] * ITERS
     gamma = moments[0]
     for iteration in range(ITERS):
-        alpha = safe_div(gamma, energy(way))
+        alpha = safe_div(gamma, product(way, energy))
         total = [t + alpha * (way[i] if i < len(way) else zero) for i, t in enumerate(total)]
         if iteration + 1 < ITERS:
             longer = way + [zero]
             shifted = [zero] + way
             res = [r - alpha * (a - b) for r, a, b in zip(res + [zero], longer, shifted)]
-            gamma_next = jnp.maximum(inner(res), 0.0)
+            gamma_next = jnp.maximum(product(res, inner), 0.0)
             ratio = safe_div(gamma_next, gamma)
             way = [r + ratio * a for r, a in zip(res, longer)]
             gamma = gamma_next
-    return total
+    kept = trusted[0]
+    for other in trusted[1:]:
+        kept = kept & other
+    return total, jnp.where(kept, 0.0, 1.0)
 
 
 VMEM = pl.BlockSpec(memory_space=pltpu.VMEM)
@@ -417,7 +429,10 @@
     per = (out_refs[0].shape[0] - SUBLANES) // (rows * sources)
     first = n_parts * sources
     totals = jnp.sum(packed[first : first + 2 * ITERS * sources], axis=1, keepdims=True)
-    poly = step_polynomial([totals[n * sources : (n + 1) * sources] for n in range(2 * ITERS)])
+    poly, lost = step_polynomial(
+        [totals[n * sources : (n + 1) * sources] for n in range(2 * ITERS)]
+    )
+    lost = jnp.broadcast_to(jnp.max(lost, axis=0, keepdims=True), (1, LANES))
     weight = weight_ref[...]
     scale = [[weight] + [weight * p[s : s + 1] for p in poly] for s in range(sources)]
     read = [
@@ -442,6 +457,7 @@
         out_ref[end_row:, :] = jnp.zeros((SUBLANES, LANES), jnp.float32)
         for s in range(sources):
             out_ref[end_row + s : end_row + s + 1, :] = read[s]
+        out_ref[end_row + sources : end_row + sources + 1, :] = lost
 
 
 def sum_kernel(places, *refs):
@@ -455,6 +471,91 @@
             field_ref[s, :, cols(k)] = tree_sum([r[at, :] for r in part_refs])
     last = tree_sum([r[sources * per * rows :, :] for r in part_refs])
     read_ref[...] = last[:sources, :electrodes]
+
+
+def careful(
+    warm_start,
+    class_map,
+    conductivities,
+    wavenumbers,
+    weights,
+    source_row,
+    source_col,
+    electrode_row,
+):
+    rows, depth = class_map.shape
+    tiles, waves = lax.axis_size("tile"), lax.axis_size("wave")
+    tile, wave = lax.axis_index("tile"), lax.axis_index("wave")
+
+    def extended(shard, dim):
+        up = [(i, i + 1) for i in range(tiles - 1)]
+        down = [(j, i) for i, j in up]
+        last = lax.slice_in_dim(shard, rows - 1, rows, axis=dim)
+        initial = lax.slice_in_dim(shard, 0, 1, axis=dim)
+        before = lax.ppermute(last, "tile", up)
+        after = lax.ppermute(initial, "tile", down)
+        return jnp.concatenate([before, shard, after], axis=dim)
+
+    class_ids = jnp.arange(conductivities.shape[0], dtype=jnp.int32)
+    sigma = jnp.sum(
+        jnp.where(class_map[None] == class_ids[:, None, None], conductivities[:, None, None], 0.0),
+        axis=0,
+    )
+    sigma_rim = extended(sigma, 0)
+    face_row = harmonic(sigma_rim[:-1], sigma_rim[1:])
+    face_up = face_row[:-1]
+    face_down = face_row[1:]
+    col_inner = harmonic(sigma[:, :-1], sigma[:, 1:])
+    face_left = jnp.concatenate([jnp.zeros((rows, 1), jnp.float32), col_inner], axis=1)
+    face_right = jnp.concatenate([col_inner, sigma[:, -1:]], axis=1)
+    wave_num = wavenumbers[0]
+    diag = face_up + face_down + face_left + face_right + wave_num * wave_num * sigma
+    global_row = tile * rows + jnp.arange(rows, dtype=jnp.int32)
+    col_ids = jnp.arange(depth, dtype=jnp.int32)
+    hits = (global_row[None, :, None] == source_row[:, None, None]) & (
+        col_ids[None, None, :] == source_col[:, None, None]
+    )
+
+    def operate(values):
+        row_padded = extended(values, 1)
+        col_padded = jnp.pad(values, ((0, 0), (0, 0), (1, 1)))
+        return (
+            diag * values
+            - face_up * row_padded[:, :-2]
+            - face_down * row_padded[:, 2:]
+            - face_left * col_padded[:, :, :-2]
+            - face_right * col_padded[:, :, 2:]
+        )
+
+    def inner(first, second):
+        return lax.psum(jnp.sum(first * second, axis=(1, 2)), "tile")[:, None, None]
+
+    field = warm_start[0]
+    residual = SOURCE_STRENGTH * hits.astype(jnp.float32) - operate(field)
+    scaled = residual / diag
+    direction = scaled
+    gamma = inner(residual, scaled)
+    for iteration in range(ITERS):
+        image = operate(direction)
+        step_size = gamma / inner(direction, image)
+        field = field + step_size * direction
+        if iteration + 1 < ITERS:
+            residual = residual - step_size * image
+            scaled = residual / diag
+            gamma_next = inner(residual, scaled)
+            direction = scaled + (gamma_next / gamma) * direction
+            gamma = gamma_next
+    weighted = weights[0] * field
+    picker = global_row[:, None] == electrode_row[None, :]
+    local_read = jnp.sum(jnp.where(picker, weighted[:, :, 0][:, :, None], 0.0), axis=1)
+    readings = lax.psum(local_read, ("wave", "tile"))
+    share = depth // waves
+    blocks = [
+        lax.dynamic_slice_in_dim(weighted, (wave ^ mask) * share, share, 2)
+        for mask in range(waves)
+    ]
+    blocks = [blocks[0]] + [swap(blocks[m], "wave", m, waves) for m in range(1, waves)]
+    return tree_sum(blocks), readings
 
 
 def shards(
@@ -551,6 +652,7 @@
     )
     if not split:
         read = pieces[0][n : n + sources, :electrodes].reshape(-1, share)
+        read = jnp.concatenate([read, pieces[0][n + sources :][:1, :share]])
         whole = pieces[0][:n].reshape(sources, chunks, rows, LANES)
         whole = whole.transpose(0, 2, 1, 3).reshape(sources * rows, depth)
         pieces = [
@@ -560,23 +662,38 @@
             for mask in range(waves)
         ]
     pieces = [pieces[0]] + [swap(pieces[m], "wave", m, waves) for m in range(1, waves)]
-    if not split:
-        final = tree_sum(pieces)
-        return (
-            final[: sources * rows].reshape(sources, rows, share),
-            final[sources * rows :].reshape(sources, electrodes),
+    lost = tree_sum([p[-1, 0] if not split else p[n + sources, 0] for p in pieces]) > 0.0
+    given = (
+        warm_start,
+        class_map,
+        conductivities,
+        wavenumbers,
+        weights,
+        source_row,
+        source_col,
+        electrode_row,
+    )
+
+    def usual():
+        if not split:
+            final = tree_sum(pieces)[:-1]
+            return (
+                final[: sources * rows].reshape(sources, rows, share),
+                final[sources * rows :].reshape(sources, electrodes),
+            )
+        parts, places = issued(pieces, (0, waves - 1, *range(1, waves - 1)))
+        return tuple(
+            vmem_call(
+                functools.partial(sum_kernel, places),
+                [
+                    jax.ShapeDtypeStruct((sources, rows, share), f32),
+                    jax.ShapeDtypeStruct((sources, electrodes), f32),
+                ],
+                parts,
+            )
         )
-    pieces, places = issued(pieces, (0, waves - 1, *range(1, waves - 1)))
-    return tuple(
-        vmem_call(
-            functools.partial(sum_kernel, places),
-            [
-                jax.ShapeDtypeStruct((sources, rows, share), f32),
-                jax.ShapeDtypeStruct((sources, electrodes), f32),
-            ],
-            pieces,
-        )
-    )
+
+    return lax.cond(lost, lambda: careful(*given), usual)
 
 
 def solution(mesh):

time: 26.3 us -> 30.7 us (1.17)
  local copies, waits for them, and re-layouts: 0.02 us -> 3.38 us
  between operations: 2.04 us -> 4.69 us
  waiting for transfers between devices: 7.81 us -> 6.98 us
  Pallas kernels: 4.12 us -> 3.52 us
    slice x0 -> x4, local copies, waits for them, and re-layouts: none -> 2.08 us  [shards(): p[n + sources, 0]]
    unnamed x6 -> x16, local copies, waits for them, and re-layouts: 0.01 us -> 1.3 us
    ppermute x8, waiting for transfers between devices: 7.81 us -> 6.98 us  [swap(): return lax.ppermute(value, axis, [(i, i ^ mask) for i in range(size)])]
    pallas_call x5, Pallas kernels: 3.06 us -> 2.46 us  [vmem_call(): pl.pallas_call(kernel, out_shape=out_shape, in_specs=[VMEM] * len(inputs)...]
  transfers between devices with their start and end apart: 9 -> 9, of which waited for: 7 -> 6; matrix products, arithmetic and copies ran while one was open for 0% -> 5% of each run, Pallas kernels for 6% -> 5%
where the time goes in v9:
time: 30.7 us; the launch traced here: 30.5 us
  starting transfers between devices  11.9 us (39%)
  waiting for transfers between devices  6.98 us (23%)
  between operations  4.69 us (15%)
  Pallas kernels  3.52 us (11%)
  local copies, waits for them, and re-layouts  3.38 us (11%)
    ppermute x8, starting transfers between devices, swap(): return lax.ppermute(value, axis, [(i, i ^ mask) for i in range(size)])  8.35 us
    ppermute x8, waiting for transfers between devices, swap(): return lax.ppermute(value, axis, [(i, i ^ mask) for i in range(size)])  6.98 us
    ppermute x1, starting transfers between devices, shards(): far = lax.ppermute(far, 'tile', ring + [(j, i) for i, j in ring])  3.54 us
    pallas_call x5, Pallas kernels, vmem_call(): pl.pallas_call(kernel, out_shape=out_shape, in_specs=[VMEM] * len(inputs)...  2.46 us
    slice x4, local copies, waits for them, and re-layouts, shards(): p[n + sources, 0]  2.08 us
    unnamed x16, local copies, waits for them, and re-layouts  1.3 us
    pallas_call x1, Pallas kernels, shards(): pl.pallas_call(edge_kernel, out_shape=[rim, rim, jax.ShapeDtypeStruct((n_...  1.06 us
  transfers between devices with their start and end apart: 9, of which 6 were waited for; matrix products, arithmetic and copies ran while one was open for 5% of the time, Pallas kernels for 5%

profile of v9, /device:TPU:0, one launch (start us, length us, event | category | flops | bytes accessed | tf_op | source)
XLA Modules:
  0.0 30.5 jit_solution(9536413892280293757)
XLA Ops:
  0.6 0.0 copy-start
  0.6 0.0 copy-start.1
  0.6 1.1 %shard_map.99 = (f32[3,4,1024]{2,1,0:T(4,128)S(1)}, f32[3,4,1024]{2,1,0:T(4,128)S(1)}, f32[8,8,128]{2,1,0:T(8,128)S(1)}, s32[4,8,128]{2,1,0:T(8,128)S(1)}) custom-call(f32[2,32,1024]{2,1,0:T(8,128)} %bitcast.16, s32[32,1024]{1,0:T(8,128)} %class_ref.1, f32[8]{0:T(128)} %cond_hbm.1, s32[2]{0:T(128)} %row_hbm.1, s32[2]{0:T(128)} %col_hbm.1), custom_call_target="tpu_custom_call" | custom-call | tf_op jit(solution)/shard_map/pallas_call | solution.py:588
  1.7 0.0 copy-start.5
  1.7 0.6 %collective-permute-start.14 = (f32[3,4,1024]{2,1,0:T(4,128)S(1)}, f32[3,4,1024]{2,1,0:T(4,128)S(1)}, u32[]{:S(2)}, u32[]{:S(2)}) collective-permute-start(f32[3,4,1024]{2,1,0:T(4,128)S(1)} %get-tuple-element.74), channel_id=1, source_target_pairs={{0,1},{1,0},{2,3},{3,2},{4,5},{5,4},{6,7},{7,6},{8,9},{9,8},{10,11... | collective-permute-start | bytes 147464 | tf_op jit(solution)/shard_map/ppermute | solution.py:35
  2.3 3.5 %collective-permute-start.13 = (f32[3,4,1024]{2,1,0:T(4,128)S(1)}, f32[3,4,1024]{2,1,0:T(4,128)S(1)}, u32[]{:S(2)}, u32[]{:S(2)}) collective-permute-start(f32[3,4,1024]{2,1,0:T(4,128)S(1)} %get-tuple-element.67), channel_id=1, source_target_pairs={{1,2},{3,4},{5,6},{7,0},{2,1},{4,3},{6,5},{0,7},{9,10},{11,12},{13... | collective-permute-start | bytes 147464 | tf_op jit(solution)/shard_map/ppermute | solution.py:607
  5.8 0.0 copy-done.5
  6.5 0.0 copy-done
  6.5 0.0 copy-done.1
  6.5 1.1 %shard_map.100 = (f32[2,8,40,128]{3,2,1,0:T(8,128)S(1)}, f32[2,8,40,128]{3,2,1,0:T(8,128)S(1)}, f32[2,8,40,128]{3,2,1,0:T(8,128)S(1)}, f32[2,8,40,128]{3,2,1,0:T...) custom-call(f32[2,32,1024]{2,1,0:T(8,128)S(1)} %bitcast.17, ...), custom_call_target="tpu_custom_call" | custom-call | tf_op jit(solution)/shard_map/pallas_call | solution.py:104
  7.6 0.0 collective-permute-done.14.came_ref
  7.6 0.5 %shard_map.101 = (f32[2,2,8,8,128]{4,3,2,1,0:T(8,128)S(1)}, f32[2,2,8,8,128]{4,3,2,1,0:T(8,128)S(1)}, f32[2,2,8,8,128]{4,3,2,1,0:T(8,128)S(1)}, f32[2,2,8,8,128]{4,3,2,1,0:T(8,128)S(1)}, f32[24,128]{1,0:T(8,128)S(1)}) custom-call(f32[3,4,1024]{2,1,0:T(4,128)S(1)} %collective-permute-done.14.came_ref, f32[8,8,128]{2,1,0:T(8,128)S(1)} %get-tuple-element.68.par_ref, ...), custom_call_target="tpu_custom_call" | custom-call | tf_op jit(solution)/shard_map/pallas_call | solution.py:104
  8.1 0.0 collective-permute-done.13.came_ref
  8.1 0.5 %shard_map.102 = (f32[2,2,8,8,128]{4,3,2,1,0:T(8,128)S(1)}, f32[2,2,8,8,128]{4,3,2,1,0:T(8,128)S(1)}, f32[2,2,8,8,128]{4,3,2,1,0:T(8,128)S(1)}, f32[2,2,8,8,128]{4,3,2,1,0:T(8,128)S(1)}, f32[24,128]{1,0:T(8,128)S(1)}) custom-call(f32[3,4,1024]{2,1,0:T(4,128)S(1)} %collective-permute-done., ...), custom_call_target="tpu_custom_call", output_to_operand_aliasing={{0}: (14, {}), {1}: (15, {}), {2}: (16, {}), {3}: (17, {})} | custom-call | tf_op jit(solution)/shard_map/pallas_call | solution.py:104
  8.6 0.1 collective-permute-start.15
  8.7 1.2 %collective-permute-done.15 = f32[24,128]{1,0:T(8,128)S(1)} collective-permute-done((f32[24,128]{1,0:T(8,128)S(1)}, f32[24,128]{1,0:T(8,128)S(1)}, u32[]{:S(2)}, u32[]{:S(2)}) %collective-permute-start.15) | collective-permute-done | bytes 12320 | tf_op jit(solution)/shard_map/ppermute | solution.py:35
  9.9 2.1 %collective-permute-start.16 = (f32[24,128]{1,0:T(8,128)S(1)}, f32[24,128]{1,0:T(8,128)S(1)}, u32[]{:S(2)}, u32[]{:S(2)}) collective-permute-start(f32[24,128]{1,0:T(8,128)S(1)} %add.109.refs_0_), channel_id=1, source_target_pairs={{0,6},{1,7},{2,4},{3,5},{4,2},{5,3},{6,0},{7,1},{8,14},{9,15},{10,... | collective-permute-start | bytes 36872 | tf_op jit(solution)/shard_map/ppermute | solution.py:35
  12.0 0.5 %collective-permute-start.17 = (f32[24,128]{1,0:T(8,128)S(1)}, f32[24,128]{1,0:T(8,128)S(1)}, u32[]{:S(2)}, u32[]{:S(2)}) collective-permute-start(f32[24,128]{1,0:T(8,128)S(1)} %add.109.refs_0_), channel_id=1, source_target_pairs={{0,4},{1,5},{2,6},{3,7},{4,0},{5,1},{6,2},{7,3},{8,12},{9,13},{10,... | collective-permute-start | bytes 36872 | tf_op jit(solution)/shard_map/ppermute | solution.py:35
  12.5 0.8 %collective-permute-start.18 = (f32[24,128]{1,0:T(8,128)S(1)}, f32[24,128]{1,0:T(8,128)S(1)}, u32[]{:S(2)}, u32[]{:S(2)}) collective-permute-start(f32[24,128]{1,0:T(8,128)S(1)} %add.109.refs_0_), channel_id=1, source_target_pairs={{0,2},{1,3},{2,0},{3,1},{4,6},{5,7},{6,4},{7,5},{8,10},{9,11},{10,... | collective-permute-start | bytes 36872 | tf_op jit(solution)/shard_map/ppermute | solution.py:35
  14.0 0.5 %collective-permute-done.16.refs_1_ = f32[24,128]{1,0:T(8,128)S(1)} collective-permute-done((f32[24,128]{1,0:T(8,128)S(1)}, f32[24,128]{1,0:T(8,128)S(1)}, u32[]{:S(2)}, u32[]{:S(2)}) %collective-permute-start.16) | collective-permute-done | bytes 12320 | tf_op jit(solution)/shard_map/ppermute | solution.py:35
  14.5 1.2 %collective-permute-done.17.refs_2_ = f32[24,128]{1,0:T(8,128)S(1)} collective-permute-done((f32[24,128]{1,0:T(8,128)S(1)}, f32[24,128]{1,0:T(8,128)S(1)}, u32[]{:S(2)}, u32[]{:S(2)}) %collective-permute-start.17) | collective-permute-done | bytes 12320 | tf_op jit(solution)/shard_map/ppermute | solution.py:35
  15.7 0.5 %collective-permute-done.18.refs_3_ = f32[24,128]{1,0:T(8,128)S(1)} collective-permute-done((f32[24,128]{1,0:T(8,128)S(1)}, f32[24,128]{1,0:T(8,128)S(1)}, u32[]{:S(2)}, u32[]{:S(2)}) %collective-permute-start.18) | collective-permute-done | bytes 12320 | tf_op jit(solution)/shard_map/ppermute | solution.py:35
  16.2 0.4 %shard_map.103 = (f32[136,128]{1,0:T(8,128)S(1)}, f32[136,128]{1,0:T(8,128)S(1)}, f32[136,128]{1,0:T(8,128)S(1)}, f32[136,128]{1,0:T(8,128)S(1)}) custom-call(f32[1,1]{1,0:T(1,128)} %bitcast.15.weight_ref, f32[24,128]{1,0:T(8,128)S(1)} %add.109.refs_0_, f32[24,128]{1,0:T(8,128)S(1)} %collective-permute-done.16.refs_1_, ...), custom_call_target="tpu_custom_call" | custom-call | tf_op jit(solution)/shard_map/pallas_call | solution.py:104
  16.6 2.7 %collective-permute-start.20 = (f32[136,128]{1,0:T(8,128)S(1)}, f32[136,128]{1,0:T(8,128)S(1)}, u32[]{:S(2)}, u32[]{:S(2)}) collective-permute-start(f32[136,128]{1,0:T(8,128)S(1)} %get-tuple-element.94), channel_id=1, source_target_pairs={{0,16},{8,24},{16,0},{24,8},{1,17},{9,25},{17,1},{25,9},{2,18},{10... | collective-permute-start | bytes 208904 | tf_op jit(solution)/shard_map/ppermute | solution.py:35
  19.3 1.3 %collective-permute-start.21 = (f32[136,128]{1,0:T(8,128)S(1)}, f32[136,128]{1,0:T(8,128)S(1)}, u32[]{:S(2)}, u32[]{:S(2)}) collective-permute-start(f32[136,128]{1,0:T(8,128)S(1)} %get-tuple-element.95), channel_id=1, source_target_pairs={{0,24},{8,16},{16,8},{24,0},{1,25},{9,17},{17,9},{25,1},{2,26},{10... | collective-permute-start | bytes 208904 | tf_op jit(solution)/shard_map/ppermute | solution.py:35
  20.6 0.2 collective-permute-start.19
  20.8 0.5 %slice.120 = f32[1,1]{1,0:T(1,128)} slice(f32[136,128]{1,0:T(8,128)S(1)} %get-tuple-element.92), slice={[130:131], [0:1]} | slice | bytes 8 | tf_op jit(solution)/shard_map/slice | solution.py:665
  21.3 2.7 %collective-permute-done.20 = f32[136,128]{1,0:T(8,128)S(1)} collective-permute-done((f32[136,128]{1,0:T(8,128)S(1)}, f32[136,128]{1,0:T(8,128)S(1)}, u32[]{:S(2)}, u32[]{:S(2)}) %collective-permute-start.20) | collective-permute-done | bytes 69664 | tf_op jit(solution)/shard_map/ppermute | solution.py:35
  24.0 0.5 %slice.141 = f32[1,1]{1,0:T(1,128)} slice(f32[136,128]{1,0:T(8,128)S(1)} %collective-permute-done.20), slice={[130:131], [0:1]} | slice | bytes 8 | tf_op jit(solution)/shard_map/slice | solution.py:665
  24.5 0.9 %collective-permute-done.21 = f32[136,128]{1,0:T(8,128)S(1)} collective-permute-done((f32[136,128]{1,0:T(8,128)S(1)}, f32[136,128]{1,0:T(8,128)S(1)}, u32[]{:S(2)}, u32[]{:S(2)}) %collective-permute-start.21) | collective-permute-done | bytes 69664 | tf_op jit(solution)/shard_map/ppermute | solution.py:35
  25.5 0.5 %slice.142 = f32[1,1]{1,0:T(1,128)} slice(f32[136,128]{1,0:T(8,128)S(1)} %collective-permute-done.21), slice={[130:131], [0:1]} | slice | bytes 8 | tf_op jit(solution)/shard_map/slice | solution.py:665
  27.3 0.0 collective-permute-done.19
  27.3 0.5 %slice.140 = f32[1,1]{1,0:T(1,128)} slice(f32[136,128]{1,0:T(8,128)S(1)} %collective-permute-done.19), slice={[130:131], [0:1]} | slice | bytes 8 | tf_op jit(solution)/shard_map/slice | solution.py:665
  29.1 0.0 copy-start.2
  29.1 0.0 copy-start.3
  29.1 0.0 copy-start.4
  29.1 0.6 %copy-done.2 = f32[8]{0:T(128)S(1)} copy-done((f32[8]{0:T(128)S(1)}, f32[8]{0:T(128)}, u32[]{:S(2)}) %copy-start.2) | copy-done | bytes 56
  29.8 0.0 copy-done.3
  29.8 0.0 copy-done.4
  29.8 0.0 copy-start.6
  29.8 0.0 copy-start.7
  29.9 0.6 %copy-done.6 = f32[2,32,256]{2,1,0:T(8,128)} copy-done((f32[2,32,256]{2,1,0:T(8,128)}, f32[2,32,256]{2,1,0:T(8,128)S(1)}, u32[]{:S(2)}) %copy-start.6) | copy-done | bytes 65560
  30.5 0.0 copy-done.7
  (4 shorter events, 0.0 us)
Async XLA Ops:
  0.6 5.9 %copy-start = (f32[1,2,32,1024]{3,2,1,0:T(8,128)S(1)}, f32[1,2,32,1024]{3,2,1,0:T(8,128)}, u32[]{:S(2)}) copy-start(f32[1,2,32,1024]{3,2,1,0:T(8,128)} %param.10) | copy-start | bytes 786436
  0.6 5.9 %copy-start.1 = (s32[32,1024]{1,0:T(8,128)S(1)}, s32[32,1024]{1,0:T(8,128)}, u32[]{:S(2)}) copy-start(s32[32,1024]{1,0:T(8,128)} %class_ref.1) | copy-start | bytes 393220
  1.7 4.1 %copy-start.5 = (s32[64]{0:T(128)S(1)}, s32[64]{0:T(128)}, u32[]{:S(2)}) copy-start(s32[64]{0:T(128)} %param.17) | copy-start | bytes 772
  1.7 5.9 %collective-permute-start.14 = (f32[3,4,1024]{2,1,0:T(4,128)S(1)}, f32[3,4,1024]{2,1,0:T(4,128)S(1)}, u32[]{:S(2)}, u32[]{:S(2)}) collective-permute-start(f32[3,4,1024]{2,1,0:T(4,128)S(1)} %get-tuple-element.74), channel_id=1, source_target_pairs={{0,1},{1,0},{2,3},{3,2},{4,5},{5,4},{6,7},{7,6},{8,9},{9,8},{10,11... | collective-permute-start | bytes 147464 | tf_op jit(solution)/shard_map/ppermute | solution.py:35
  2.3 5.8 %collective-permute-start.13 = (f32[3,4,1024]{2,1,0:T(4,128)S(1)}, f32[3,4,1024]{2,1,0:T(4,128)S(1)}, u32[]{:S(2)}, u32[]{:S(2)}) collective-permute-start(f32[3,4,1024]{2,1,0:T(4,128)S(1)} %get-tuple-element.67), channel_id=1, source_target_pairs={{1,2},{3,4},{5,6},{7,0},{2,1},{4,3},{6,5},{0,7},{9,10},{11,12},{13... | collective-permute-start | bytes 147464 | tf_op jit(solution)/shard_map/ppermute | solution.py:607
  8.6 1.2 %collective-permute-start.15 = (f32[24,128]{1,0:T(8,128)S(1)}, f32[24,128]{1,0:T(8,128)S(1)}, u32[]{:S(2)}, u32[]{:S(2)}) collective-permute-start(f32[24,128]{1,0:T(8,128)S(1)} %get-tuple-element.87), channel_id=1, source_target_pairs={{0,1},{1,0},{2,3},{3,2},{4,5},{5,4},{6,7},{7,6},{8,9},{9,8},{10,11... | collective-permute-start | bytes 36872 | tf_op jit(solution)/shard_map/ppermute | solution.py:35
  9.9 4.6 %collective-permute-start.16 = (f32[24,128]{1,0:T(8,128)S(1)}, f32[24,128]{1,0:T(8,128)S(1)}, u32[]{:S(2)}, u32[]{:S(2)}) collective-permute-start(f32[24,128]{1,0:T(8,128)S(1)} %add.109.refs_0_), channel_id=1, source_target_pairs={{0,6},{1,7},{2,4},{3,5},{4,2},{5,3},{6,0},{7,1},{8,14},{9,15},{10,... | collective-permute-start | bytes 36872 | tf_op jit(solution)/shard_map/ppermute | solution.py:35
  12.0 3.7 %collective-permute-start.17 = (f32[24,128]{1,0:T(8,128)S(1)}, f32[24,128]{1,0:T(8,128)S(1)}, u32[]{:S(2)}, u32[]{:S(2)}) collective-permute-start(f32[24,128]{1,0:T(8,128)S(1)} %add.109.refs_0_), channel_id=1, source_target_pairs={{0,4},{1,5},{2,6},{3,7},{4,0},{5,1},{6,2},{7,3},{8,12},{9,13},{10,... | collective-permute-start | bytes 36872 | tf_op jit(solution)/shard_map/ppermute | solution.py:35
  12.5 3.7 %collective-permute-start.18 = (f32[24,128]{1,0:T(8,128)S(1)}, f32[24,128]{1,0:T(8,128)S(1)}, u32[]{:S(2)}, u32[]{:S(2)}) collective-permute-start(f32[24,128]{1,0:T(8,128)S(1)} %add.109.refs_0_), channel_id=1, source_target_pairs={{0,2},{1,3},{2,0},{3,1},{4,6},{5,7},{6,4},{7,5},{8,10},{9,11},{10,... | collective-permute-start | bytes 36872 | tf_op jit(solution)/shard_map/ppermute | solution.py:35
  16.6 7.4 %collective-permute-start.20 = (f32[136,128]{1,0:T(8,128)S(1)}, f32[136,128]{1,0:T(8,128)S(1)}, u32[]{:S(2)}, u32[]{:S(2)}) collective-permute-start(f32[136,128]{1,0:T(8,128)S(1)} %get-tuple-element.94), channel_id=1, source_target_pairs={{0,16},{8,24},{16,0},{24,8},{1,17},{9,25},{17,1},{25,9},{2,18},{10... | collective-permute-start | bytes 208904 | tf_op jit(solution)/shard_map/ppermute | solution.py:35
  19.3 6.2 %collective-permute-start.21 = (f32[136,128]{1,0:T(8,128)S(1)}, f32[136,128]{1,0:T(8,128)S(1)}, u32[]{:S(2)}, u32[]{:S(2)}) collective-permute-start(f32[136,128]{1,0:T(8,128)S(1)} %get-tuple-element.95), channel_id=1, source_target_pairs={{0,24},{8,16},{16,8},{24,0},{1,25},{9,17},{17,9},{25,1},{2,26},{10... | collective-permute-start | bytes 208904 | tf_op jit(solution)/shard_map/ppermute | solution.py:35
  20.6 6.7 %collective-permute-start.19 = (f32[136,128]{1,0:T(8,128)S(1)}, f32[136,128]{1,0:T(8,128)S(1)}, u32[]{:S(2)}, u32[]{:S(2)}) collective-permute-start(f32[136,128]{1,0:T(8,128)S(1)} %get-tuple-element.93), channel_id=1, source_target_pairs={{0,8},{8,0},{16,24},{24,16},{1,9},{9,1},{17,25},{25,17},{2,10},{10... | collective-permute-start | bytes 208904 | tf_op jit(solution)/shard_map/ppermute | solution.py:35
  29.1 0.7 %copy-start.2 = (f32[8]{0:T(128)S(1)}, f32[8]{0:T(128)}, u32[]{:S(2)}) copy-start(f32[8]{0:T(128)} %cond_hbm.1) | copy-start | bytes 100
  29.1 0.7 %copy-start.3 = (s32[2]{0:T(128)S(1)}, s32[2]{0:T(128)}, u32[]{:S(2)}) copy-start(s32[2]{0:T(128)} %row_hbm.1) | copy-start | bytes 28
  29.1 0.7 %copy-start.4 = (s32[2]{0:T(128)S(1)}, s32[2]{0:T(128)}, u32[]{:S(2)}) copy-start(s32[2]{0:T(128)} %col_hbm.1) | copy-start | bytes 28
  29.8 0.6 %copy-start.6 = (f32[2,32,256]{2,1,0:T(8,128)}, f32[2,32,256]{2,1,0:T(8,128)S(1)}, u32[]{:S(2)}) copy-start(f32[2,32,256]{2,1,0:T(8,128)S(1)} %get-tuple-element.136) | copy-start | bytes 196612
  29.8 0.6 %copy-start.7 = (f32[2,64]{1,0:T(2,128)}, f32[2,64]{1,0:T(2,128)S(1)}, u32[]{:S(2)}) copy-start(f32[2,64]{1,0:T(2,128)S(1)} %get-tuple-element.135) | copy-start | bytes 1540

commit v10 on v9

--- a/solution.py
+++ b/solution.py
@@ -100,12 +100,12 @@
 PARAMS = pltpu.CompilerParams(vmem_limit_bytes=16 << 20)
 
 
-def vmem_call(kernel, out_shape, inputs, scratch=(), aliases=()):
+def vmem_call(kernel, out_shape, inputs, scratch=(), aliases=(), out_specs=None):
     return pl.pallas_call(
         kernel,
         out_shape=out_shape,
         in_specs=[VMEM] * len(inputs),
-        out_specs=jax.tree.map(lambda _: VMEM, out_shape),
+        out_specs=out_specs or jax.tree.map(lambda _: VMEM, out_shape),
         scratch_shapes=list(scratch),
         input_output_aliases=dict(aliases),
         compiler_params=PARAMS,
@@ -461,7 +461,7 @@
 
 
 def sum_kernel(places, *refs):
-    part_refs, (field_ref, read_ref) = [refs[i] for i in places], refs[-2:]
+    part_refs, (field_ref, read_ref, lost_ref) = [refs[i] for i in places], refs[-3:]
     sources, rows, share = field_ref.shape
     electrodes = read_ref.shape[1]
     per = share // LANES
@@ -471,18 +471,14 @@
             field_ref[s, :, cols(k)] = tree_sum([r[at, :] for r in part_refs])
     last = tree_sum([r[sources * per * rows :, :] for r in part_refs])
     read_ref[...] = last[:sources, :electrodes]
-
-
-def careful(
-    warm_start,
-    class_map,
-    conductivities,
-    wavenumbers,
-    weights,
-    source_row,
-    source_col,
-    electrode_row,
-):
+    lost_ref[0] = jnp.max(last[sources : sources + 1, :]).astype(jnp.int32)
+
+
+def careful(warm_start, class_map, params, wavenumbers, weights, spots, picks, electrodes):
+    sources = warm_start.shape[1]
+    conductivities = params[:, 0, 0]
+    source_row, source_col = spots[:sources, 0, 0], spots[sources:, 0, 0]
+    electrode_row = picks[0, :electrodes]
     rows, depth = class_map.shape
     tiles, waves = lax.axis_size("tile"), lax.axis_size("wave")
     tile, wave = lax.axis_index("tile"), lax.axis_index("wave")
@@ -662,38 +658,26 @@
             for mask in range(waves)
         ]
     pieces = [pieces[0]] + [swap(pieces[m], "wave", m, waves) for m in range(1, waves)]
-    lost = tree_sum([p[-1, 0] if not split else p[n + sources, 0] for p in pieces]) > 0.0
-    given = (
-        warm_start,
-        class_map,
-        conductivities,
-        wavenumbers,
-        weights,
-        source_row,
-        source_col,
-        electrode_row,
-    )
-
-    def usual():
-        if not split:
-            final = tree_sum(pieces)[:-1]
-            return (
-                final[: sources * rows].reshape(sources, rows, share),
-                final[sources * rows :].reshape(sources, electrodes),
-            )
-        parts, places = issued(pieces, (0, waves - 1, *range(1, waves - 1)))
-        return tuple(
-            vmem_call(
-                functools.partial(sum_kernel, places),
-                [
-                    jax.ShapeDtypeStruct((sources, rows, share), f32),
-                    jax.ShapeDtypeStruct((sources, electrodes), f32),
-                ],
-                parts,
-            )
+    if split:
+        pieces, places = issued(pieces, (0, waves - 1, *range(1, waves - 1)))
+        potentials, readings, lost = vmem_call(
+            functools.partial(sum_kernel, places),
+            [
+                jax.ShapeDtypeStruct((sources, rows, share), f32),
+                jax.ShapeDtypeStruct((sources, electrodes), f32),
+                jax.ShapeDtypeStruct((1,), jnp.int32),
+            ],
+            pieces,
+            out_specs=[VMEM, VMEM, pl.BlockSpec(memory_space=pltpu.SMEM)],
         )
-
-    return lax.cond(lost, lambda: careful(*given), usual)
+        lost = lost[0] > 0
+    else:
+        final = tree_sum(pieces)
+        lost = final[-1, 0] > 0.0
+        potentials = final[: sources * rows].reshape(sources, rows, share)
+        readings = final[sources * rows : -1].reshape(sources, electrodes)
+    given = (warm_start, class_map, params, wavenumbers, weights, spots, picks, electrodes)
+    return lax.cond(lost, lambda: careful(*given), lambda: (potentials, readings))
 
 
 def solution(mesh):

time: 30.7 us -> 27.6 us (0.90)
  local copies, waits for them, and re-layouts: 3.38 us -> 0.64 us
  between operations: 4.69 us -> 2.72 us
  waiting for transfers between devices: 6.98 us -> 7.82 us
  Pallas kernels: 3.52 us -> 4.12 us
    slice x4 -> x0, local copies, waits for them, and re-layouts: 2.08 us -> none  [shards(): p[n + sources, 0]]
    ppermute x8, waiting for transfers between devices: 6.98 us -> 7.82 us  [swap(): return lax.ppermute(value, axis, [(i, i ^ mask) for i in range(size)])]
    unnamed x16 -> x10, local copies, waits for them, and re-layouts: 1.3 us -> 0.63 us
    pallas_call x5, Pallas kernels: 2.46 us -> 3.07 us  [vmem_call(): pl.pallas_call(kernel, out_shape=out_shape, in_specs=[VMEM] * len(inputs)...]
  transfers between devices with their start and end apart: 9 -> 9, of which waited for: 6 -> 7; matrix products, arithmetic and copies ran while one was open for 5% -> 0% of each run, Pallas kernels for 5% -> 6%
where the time goes in v10:
time: 27.6 us; the launch traced here: 27.4 us
  starting transfers between devices  12.1 us (44%)
  waiting for transfers between devices  7.82 us (28%)
  Pallas kernels  4.12 us (15%)
  between operations  2.72 us (10%)
  local copies, waits for them, and re-layouts  0.64 us (2%)
    ppermute x8, starting transfers between devices, swap(): return lax.ppermute(value, axis, [(i, i ^ mask) for i in range(size)])  8.57 us
    ppermute x8, waiting for transfers between devices, swap(): return lax.ppermute(value, axis, [(i, i ^ mask) for i in range(size)])  7.82 us
    ppermute x1, starting transfers between devices, shards(): far = lax.ppermute(far, 'tile', ring + [(j, i) for i, j in ring])  3.54 us
    pallas_call x5, Pallas kernels, vmem_call(): pl.pallas_call(kernel, out_shape=out_shape, in_specs=[VMEM] * len(inputs)...  3.07 us
    pallas_call x1, Pallas kernels, shards(): pl.pallas_call(edge_kernel, out_shape=[rim, rim, jax.ShapeDtypeStruct((n_...  1.06 us
    unnamed x10, local copies, waits for them, and re-layouts  0.63 us
  transfers between devices with their start and end apart: 9, of which 7 were waited for; matrix products, arithmetic and copies ran while one was open for 0% of the time, Pallas kernels for 6%

profile of v10, /device:TPU:0, one launch (start us, length us, event | category | flops | bytes accessed | tf_op | source)
XLA Modules:
  0.0 27.4 jit_solution(4653850382663830949)
XLA Ops:
  0.6 0.0 copy-start
  0.6 0.0 copy-start.1
  0.7 1.1 %shard_map.99 = (f32[3,4,1024]{2,1,0:T(4,128)S(1)}, f32[3,4,1024]{2,1,0:T(4,128)S(1)}, f32[8,8,128]{2,1,0:T(8,128)S(1)}, s32[4,8,128]{2,1,0:T(8,128)S(1)}) custom-call(f32[2,32,1024]{2,1,0:T(8,128)} %bitcast.24, s32[32,1024]{1,0:T(8,128)} %class_ref.1, f32[8]{0:T(128)} %cond_hbm.1, s32[2]{0:T(128)} %row_hbm.1, s32[2]{0:T(128)} %col_hbm.1), custom_call_target="tpu_custom_call" | custom-call | tf_op jit(solution)/shard_map/pallas_call | solution.py:584
  1.7 0.0 copy-start.4
  1.7 0.6 %collective-permute-start.14 = (f32[3,4,1024]{2,1,0:T(4,128)S(1)}, f32[3,4,1024]{2,1,0:T(4,128)S(1)}, u32[]{:S(2)}, u32[]{:S(2)}) collective-permute-start(f32[3,4,1024]{2,1,0:T(4,128)S(1)} %get-tuple-element.66), channel_id=1, source_target_pairs={{0,1},{1,0},{2,3},{3,2},{4,5},{5,4},{6,7},{7,6},{8,9},{9,8},{10,11... | collective-permute-start | bytes 147464 | tf_op jit(solution)/shard_map/ppermute | solution.py:35
  2.3 3.5 %collective-permute-start.13 = (f32[3,4,1024]{2,1,0:T(4,128)S(1)}, f32[3,4,1024]{2,1,0:T(4,128)S(1)}, u32[]{:S(2)}, u32[]{:S(2)}) collective-permute-start(f32[3,4,1024]{2,1,0:T(4,128)S(1)} %get-tuple-element.59), channel_id=1, source_target_pairs={{1,2},{3,4},{5,6},{7,0},{2,1},{4,3},{6,5},{0,7},{9,10},{11,12},{13... | collective-permute-start | bytes 147464 | tf_op jit(solution)/shard_map/ppermute | solution.py:603
  5.8 0.0 copy-done.4
  6.5 0.0 copy-done
  6.5 0.0 copy-done.1
  6.5 1.1 %shard_map.100 = (f32[2,8,40,128]{3,2,1,0:T(8,128)S(1)}, f32[2,8,40,128]{3,2,1,0:T(8,128)S(1)}, f32[2,8,40,128]{3,2,1,0:T(8,128)S(1)}, f32[2,8,40,128]{3,2,1,0:T...) custom-call(f32[2,32,1024]{2,1,0:T(8,128)S(1)} %bitcast.25, ...), custom_call_target="tpu_custom_call" | custom-call | tf_op jit(solution)/shard_map/pallas_call | solution.py:104
  7.6 0.0 collective-permute-done.14.came_ref
  7.6 0.5 %shard_map.101 = (f32[2,2,8,8,128]{4,3,2,1,0:T(8,128)S(1)}, f32[2,2,8,8,128]{4,3,2,1,0:T(8,128)S(1)}, f32[2,2,8,8,128]{4,3,2,1,0:T(8,128)S(1)}, f32[2,2,8,8,128]{4,3,2,1,0:T(8,128)S(1)}, f32[24,128]{1,0:T(8,128)S(1)}) custom-call(f32[3,4,1024]{2,1,0:T(4,128)S(1)} %collective-permute-done.14.came_ref, f32[8,8,128]{2,1,0:T(8,128)S(1)} %get-tuple-element.60.par_ref, ...), custom_call_target="tpu_custom_call" | custom-call | tf_op jit(solution)/shard_map/pallas_call | solution.py:104
  8.1 0.0 collective-permute-done.13.came_ref
  8.1 0.5 %shard_map.102 = (f32[2,2,8,8,128]{4,3,2,1,0:T(8,128)S(1)}, f32[2,2,8,8,128]{4,3,2,1,0:T(8,128)S(1)}, f32[2,2,8,8,128]{4,3,2,1,0:T(8,128)S(1)}, f32[2,2,8,8,128]{4,3,2,1,0:T(8,128)S(1)}, f32[24,128]{1,0:T(8,128)S(1)}) custom-call(f32[3,4,1024]{2,1,0:T(4,128)S(1)} %collective-permute-done., ...), custom_call_target="tpu_custom_call", output_to_operand_aliasing={{0}: (14, {}), {1}: (15, {}), {2}: (16, {}), {3}: (17, {})} | custom-call | tf_op jit(solution)/shard_map/pallas_call | solution.py:104
  8.6 0.1 collective-permute-start.15
  8.7 1.2 %collective-permute-done.15 = f32[24,128]{1,0:T(8,128)S(1)} collective-permute-done((f32[24,128]{1,0:T(8,128)S(1)}, f32[24,128]{1,0:T(8,128)S(1)}, u32[]{:S(2)}, u32[]{:S(2)}) %collective-permute-start.15) | collective-permute-done | bytes 12320 | tf_op jit(solution)/shard_map/ppermute | solution.py:35
  9.9 2.2 %collective-permute-start.16 = (f32[24,128]{1,0:T(8,128)S(1)}, f32[24,128]{1,0:T(8,128)S(1)}, u32[]{:S(2)}, u32[]{:S(2)}) collective-permute-start(f32[24,128]{1,0:T(8,128)S(1)} %add.97.refs_0_), channel_id=1, source_target_pairs={{0,6},{1,7},{2,4},{3,5},{4,2},{5,3},{6,0},{7,1},{8,14},{9,15},{10,... | collective-permute-start | bytes 36872 | tf_op jit(solution)/shard_map/ppermute | solution.py:35
  12.0 0.5 %collective-permute-start.17 = (f32[24,128]{1,0:T(8,128)S(1)}, f32[24,128]{1,0:T(8,128)S(1)}, u32[]{:S(2)}, u32[]{:S(2)}) collective-permute-start(f32[24,128]{1,0:T(8,128)S(1)} %add.97.refs_0_), channel_id=1, source_target_pairs={{0,4},{1,5},{2,6},{3,7},{4,0},{5,1},{6,2},{7,3},{8,12},{9,13},{10,... | collective-permute-start | bytes 36872 | tf_op jit(solution)/shard_map/ppermute | solution.py:35
  12.5 0.8 %collective-permute-start.18 = (f32[24,128]{1,0:T(8,128)S(1)}, f32[24,128]{1,0:T(8,128)S(1)}, u32[]{:S(2)}, u32[]{:S(2)}) collective-permute-start(f32[24,128]{1,0:T(8,128)S(1)} %add.97.refs_0_), channel_id=1, source_target_pairs={{0,2},{1,3},{2,0},{3,1},{4,6},{5,7},{6,4},{7,5},{8,10},{9,11},{10,... | collective-permute-start | bytes 36872 | tf_op jit(solution)/shard_map/ppermute | solution.py:35
  14.0 0.5 %collective-permute-done.16.refs_1_ = f32[24,128]{1,0:T(8,128)S(1)} collective-permute-done((f32[24,128]{1,0:T(8,128)S(1)}, f32[24,128]{1,0:T(8,128)S(1)}, u32[]{:S(2)}, u32[]{:S(2)}) %collective-permute-start.16) | collective-permute-done | bytes 12320 | tf_op jit(solution)/shard_map/ppermute | solution.py:35
  14.5 1.3 %collective-permute-done.17.refs_2_ = f32[24,128]{1,0:T(8,128)S(1)} collective-permute-done((f32[24,128]{1,0:T(8,128)S(1)}, f32[24,128]{1,0:T(8,128)S(1)}, u32[]{:S(2)}, u32[]{:S(2)}) %collective-permute-start.17) | collective-permute-done | bytes 12320 | tf_op jit(solution)/shard_map/ppermute | solution.py:35
  15.7 0.5 %collective-permute-done.18.refs_3_ = f32[24,128]{1,0:T(8,128)S(1)} collective-permute-done((f32[24,128]{1,0:T(8,128)S(1)}, f32[24,128]{1,0:T(8,128)S(1)}, u32[]{:S(2)}, u32[]{:S(2)}) %collective-permute-start.18) | collective-permute-done | bytes 12320 | tf_op jit(solution)/shard_map/ppermute | solution.py:35
  16.2 0.4 %shard_map.103 = (f32[136,128]{1,0:T(8,128)S(1)}, f32[136,128]{1,0:T(8,128)S(1)}, f32[136,128]{1,0:T(8,128)S(1)}, f32[136,128]{1,0:T(8,128)S(1)}) custom-call(f32[1,1]{1,0:T(1,128)} %bitcast.23.weight_ref, f32[24,128]{1,0:T(8,128)S(1)} %add.97.refs_0_, f32[24,128]{1,0:T(8,128)S(1)} %collective-permute-done.16.refs_1_, ...), custom_call_target="tpu_custom_call" | custom-call | tf_op jit(solution)/shard_map/pallas_call | solution.py:104
  16.6 3.7 %collective-permute-start.19 = (f32[136,128]{1,0:T(8,128)S(1)}, f32[136,128]{1,0:T(8,128)S(1)}, u32[]{:S(2)}, u32[]{:S(2)}) collective-permute-start(f32[136,128]{1,0:T(8,128)S(1)} %get-tuple-element.85), channel_id=1, source_target_pairs={{0,24},{8,16},{16,8},{24,0},{1,25},{9,17},{17,9},{25,1},{2,26},{10... | collective-permute-start | bytes 208904 | tf_op jit(solution)/shard_map/ppermute | solution.py:35
  20.3 0.0 collective-permute-start.20
  20.3 0.8 %collective-permute-start.21 = (f32[136,128]{1,0:T(8,128)S(1)}, f32[136,128]{1,0:T(8,128)S(1)}, u32[]{:S(2)}, u32[]{:S(2)}) collective-permute-start(f32[136,128]{1,0:T(8,128)S(1)} %get-tuple-element.87), channel_id=1, source_target_pairs={{0,16},{8,24},{16,0},{24,8},{1,17},{9,25},{17,1},{25,9},{2,18},{10... | collective-permute-start | bytes 208904 | tf_op jit(solution)/shard_map/ppermute | solution.py:35
  21.0 1.8 %collective-permute-done.19.refs_1_ = f32[136,128]{1,0:T(8,128)S(1)} collective-permute-done((f32[136,128]{1,0:T(8,128)S(1)}, f32[136,128]{1,0:T(8,128)S(1)}, u32[]{:S(2)}, u32[]{:S(2)}) %collective-permute-start.19) | collective-permute-done | bytes 69664 | tf_op jit(solution)/shard_map/ppermute | solution.py:35
  22.8 1.7 %collective-permute-done.20.refs_2_ = f32[136,128]{1,0:T(8,128)S(1)} collective-permute-done((f32[136,128]{1,0:T(8,128)S(1)}, f32[136,128]{1,0:T(8,128)S(1)}, u32[]{:S(2)}, u32[]{:S(2)}) %collective-permute-start.20) | collective-permute-done | bytes 69664 | tf_op jit(solution)/shard_map/ppermute | solution.py:35
  24.6 0.9 %collective-permute-done.21.refs_3_ = f32[136,128]{1,0:T(8,128)S(1)} collective-permute-done((f32[136,128]{1,0:T(8,128)S(1)}, f32[136,128]{1,0:T(8,128)S(1)}, u32[]{:S(2)}, u32[]{:S(2)}) %collective-permute-start.21) | collective-permute-done | bytes 69664 | tf_op jit(solution)/shard_map/ppermute | solution.py:35
  25.5 0.7 %shard_map.104 = (f32[2,32,256]{2,1,0:T(8,128)S(1)}, f32[2,64]{1,0:T(2,128)S(1)}, s32[1]{0:T(128)}) custom-call(f32[136,128]{1,0:T(8,128)S(1)} %get-tuple-element.84.refs_0_, f32[136,128]{1,0:T(8,128)S(1)} %collective-permute-done.19.refs_1_, f32[136,128]{1,0:T(8,128)S(1)} %collective-permute-done.20.refs_2_, f32[136,128]{1,0:T(8,128)S(1)} %collective-permute-done.21.refs_3_), custom_call_target="tpu_custom_call" | custom-call | tf_op jit(solution)/shard_map/pallas_call | solution.py:104
  26.8 0.0 copy-start.2
  26.8 0.0 copy-start.3
  26.8 0.6 %copy-done.2 = f32[2,32,256]{2,1,0:T(8,128)} copy-done((f32[2,32,256]{2,1,0:T(8,128)}, f32[2,32,256]{2,1,0:T(8,128)S(1)}, u32[]{:S(2)}) %copy-start.2) | copy-done | bytes 65560
  27.4 0.0 copy-done.3
  (3 shorter events, 0.0 us)
Async XLA Ops:
  0.6 5.9 %copy-start = (f32[1,2,32,1024]{3,2,1,0:T(8,128)S(1)}, f32[1,2,32,1024]{3,2,1,0:T(8,128)}, u32[]{:S(2)}) copy-start(f32[1,2,32,1024]{3,2,1,0:T(8,128)} %param.10) | copy-start | bytes 786436
  0.6 5.9 %copy-start.1 = (s32[32,1024]{1,0:T(8,128)S(1)}, s32[32,1024]{1,0:T(8,128)}, u32[]{:S(2)}) copy-start(s32[32,1024]{1,0:T(8,128)} %class_ref.1) | copy-start | bytes 393220
  1.7 4.1 %copy-start.4 = (s32[64]{0:T(128)S(1)}, s32[64]{0:T(128)}, u32[]{:S(2)}) copy-start(s32[64]{0:T(128)} %param.17) | copy-start | bytes 772
  1.7 5.9 %collective-permute-start.14 = (f32[3,4,1024]{2,1,0:T(4,128)S(1)}, f32[3,4,1024]{2,1,0:T(4,128)S(1)}, u32[]{:S(2)}, u32[]{:S(2)}) collective-permute-start(f32[3,4,1024]{2,1,0:T(4,128)S(1)} %get-tuple-element.66), channel_id=1, source_target_pairs={{0,1},{1,0},{2,3},{3,2},{4,5},{5,4},{6,7},{7,6},{8,9},{9,8},{10,11... | collective-permute-start | bytes 147464 | tf_op jit(solution)/shard_map/ppermute | solution.py:35
  2.3 5.8 %collective-permute-start.13 = (f32[3,4,1024]{2,1,0:T(4,128)S(1)}, f32[3,4,1024]{2,1,0:T(4,128)S(1)}, u32[]{:S(2)}, u32[]{:S(2)}) collective-permute-start(f32[3,4,1024]{2,1,0:T(4,128)S(1)} %get-tuple-element.59), channel_id=1, source_target_pairs={{1,2},{3,4},{5,6},{7,0},{2,1},{4,3},{6,5},{0,7},{9,10},{11,12},{13... | collective-permute-start | bytes 147464 | tf_op jit(solution)/shard_map/ppermute | solution.py:603
  8.6 1.2 %collective-permute-start.15 = (f32[24,128]{1,0:T(8,128)S(1)}, f32[24,128]{1,0:T(8,128)S(1)}, u32[]{:S(2)}, u32[]{:S(2)}) collective-permute-start(f32[24,128]{1,0:T(8,128)S(1)} %get-tuple-element.79), channel_id=1, source_target_pairs={{0,1},{1,0},{2,3},{3,2},{4,5},{5,4},{6,7},{7,6},{8,9},{9,8},{10,11... | collective-permute-start | bytes 36872 | tf_op jit(solution)/shard_map/ppermute | solution.py:35
  9.9 4.6 %collective-permute-start.16 = (f32[24,128]{1,0:T(8,128)S(1)}, f32[24,128]{1,0:T(8,128)S(1)}, u32[]{:S(2)}, u32[]{:S(2)}) collective-permute-start(f32[24,128]{1,0:T(8,128)S(1)} %add.97.refs_0_), channel_id=1, source_target_pairs={{0,6},{1,7},{2,4},{3,5},{4,2},{5,3},{6,0},{7,1},{8,14},{9,15},{10,... | collective-permute-start | bytes 36872 | tf_op jit(solution)/shard_map/ppermute | solution.py:35
  12.0 3.7 %collective-permute-start.17 = (f32[24,128]{1,0:T(8,128)S(1)}, f32[24,128]{1,0:T(8,128)S(1)}, u32[]{:S(2)}, u32[]{:S(2)}) collective-permute-start(f32[24,128]{1,0:T(8,128)S(1)} %add.97.refs_0_), channel_id=1, source_target_pairs={{0,4},{1,5},{2,6},{3,7},{4,0},{5,1},{6,2},{7,3},{8,12},{9,13},{10,... | collective-permute-start | bytes 36872 | tf_op jit(solution)/shard_map/ppermute | solution.py:35
  12.5 3.7 %collective-permute-start.18 = (f32[24,128]{1,0:T(8,128)S(1)}, f32[24,128]{1,0:T(8,128)S(1)}, u32[]{:S(2)}, u32[]{:S(2)}) collective-permute-start(f32[24,128]{1,0:T(8,128)S(1)} %add.97.refs_0_), channel_id=1, source_target_pairs={{0,2},{1,3},{2,0},{3,1},{4,6},{5,7},{6,4},{7,5},{8,10},{9,11},{10,... | collective-permute-start | bytes 36872 | tf_op jit(solution)/shard_map/ppermute | solution.py:35
  16.6 6.2 %collective-permute-start.19 = (f32[136,128]{1,0:T(8,128)S(1)}, f32[136,128]{1,0:T(8,128)S(1)}, u32[]{:S(2)}, u32[]{:S(2)}) collective-permute-start(f32[136,128]{1,0:T(8,128)S(1)} %get-tuple-element.85), channel_id=1, source_target_pairs={{0,24},{8,16},{16,8},{24,0},{1,25},{9,17},{17,9},{25,1},{2,26},{10... | collective-permute-start | bytes 208904 | tf_op jit(solution)/shard_map/ppermute | solution.py:35
  20.3 4.3 %collective-permute-start.20 = (f32[136,128]{1,0:T(8,128)S(1)}, f32[136,128]{1,0:T(8,128)S(1)}, u32[]{:S(2)}, u32[]{:S(2)}) collective-permute-start(f32[136,128]{1,0:T(8,128)S(1)} %get-tuple-element.86), channel_id=1, source_target_pairs={{0,8},{8,0},{16,24},{24,16},{1,9},{9,1},{17,25},{25,17},{2,10},{10... | collective-permute-start | bytes 208904 | tf_op jit(solution)/shard_map/ppermute | solution.py:35
  20.3 5.2 %collective-permute-start.21 = (f32[136,128]{1,0:T(8,128)S(1)}, f32[136,128]{1,0:T(8,128)S(1)}, u32[]{:S(2)}, u32[]{:S(2)}) collective-permute-start(f32[136,128]{1,0:T(8,128)S(1)} %get-tuple-element.87), channel_id=1, source_target_pairs={{0,16},{8,24},{16,0},{24,8},{1,17},{9,25},{17,1},{25,9},{2,18},{10... | collective-permute-start | bytes 208904 | tf_op jit(solution)/shard_map/ppermute | solution.py:35
  26.8 0.6 %copy-start.2 = (f32[2,32,256]{2,1,0:T(8,128)}, f32[2,32,256]{2,1,0:T(8,128)S(1)}, u32[]{:S(2)}) copy-start(f32[2,32,256]{2,1,0:T(8,128)S(1)} %get-tuple-element.128) | copy-start | bytes 196612
  26.8 0.6 %copy-start.3 = (f32[2,64]{1,0:T(2,128)}, f32[2,64]{1,0:T(2,128)S(1)}, u32[]{:S(2)}) copy-start(f32[2,64]{1,0:T(2,128)S(1)} %get-tuple-element.127) | copy-start | bytes 1540

commit v11 on v10

--- a/solution.py
+++ b/solution.py
@@ -461,7 +461,8 @@
 
 
 def sum_kernel(places, *refs):
-    part_refs, (field_ref, read_ref, lost_ref) = [refs[i] for i in places], refs[-3:]
+    part_refs = [refs[i] for i in places]
+    field_hbm, read_hbm, lost_ref, field_ref, read_ref, sems = refs[len(places) :]
     sources, rows, share = field_ref.shape
     electrodes = read_ref.shape[1]
     per = share // LANES
@@ -471,7 +472,15 @@
             field_ref[s, :, cols(k)] = tree_sum([r[at, :] for r in part_refs])
     last = tree_sum([r[sources * per * rows :, :] for r in part_refs])
     read_ref[...] = last[:sources, :electrodes]
+    copies = [
+        pltpu.make_async_copy(field_ref, field_hbm, sems.at[0]),
+        pltpu.make_async_copy(read_ref, read_hbm, sems.at[1]),
+    ]
+    for copy in copies:
+        copy.start()
     lost_ref[0] = jnp.max(last[sources : sources + 1, :]).astype(jnp.int32)
+    for copy in copies:
+        copy.wait()
 
 
 def careful(warm_start, class_map, params, wavenumbers, weights, spots, picks, electrodes):
@@ -663,12 +672,18 @@
         potentials, readings, lost = vmem_call(
             functools.partial(sum_kernel, places),
             [
-                jax.ShapeDtypeStruct((sources, rows, share), f32),
-                jax.ShapeDtypeStruct((sources, electrodes), f32),
+                pltpu.HBM((sources, rows, share), f32),
+                pltpu.HBM((sources, electrodes), f32),
                 jax.ShapeDtypeStruct((1,), jnp.int32),
             ],
             pieces,
-            out_specs=[VMEM, VMEM, pl.BlockSpec(memory_space=pltpu.SMEM)],
+            [
+                pltpu.VMEM((sources, rows, share), f32),
+                pltpu.VMEM((sources, electrodes), f32),
+                pltpu.SemaphoreType.DMA((2,)),
+            ],
+            out_specs=[pl.BlockSpec(memory_space=pltpu.HBM)] * 2
+            + [pl.BlockSpec(memory_space=pltpu.SMEM)],
         )
         lost = lost[0] > 0
     else:

time: 27.6 us -> 27.5 us (level)
  local copies, waits for them, and re-layouts: 0.64 us -> 0.02 us
  Pallas kernels: 4.12 us -> 4.66 us
    unnamed x10 -> x6, local copies, waits for them, and re-layouts: 0.63 us -> 0.01 us
    pallas_call x5, Pallas kernels: 3.07 us -> 3.6 us  [vmem_call(): pl.pallas_call(kernel, out_shape=out_shape, in_specs=[VMEM] * len(inputs)...]
where the time goes in v11:
time: 27.5 us; the launch traced here: 27.4 us
  starting transfers between devices  12.1 us (44%)
  waiting for transfers between devices  7.82 us (28%)
  Pallas kernels  4.66 us (17%)
  between operations  2.74 us (10%)
    ppermute x8, starting transfers between devices, swap(): return lax.ppermute(value, axis, [(i, i ^ mask) for i in range(size)])  8.57 us
    ppermute x8, waiting for transfers between devices, swap(): return lax.ppermute(value, axis, [(i, i ^ mask) for i in range(size)])  7.82 us
    pallas_call x5, Pallas kernels, vmem_call(): pl.pallas_call(kernel, out_shape=out_shape, in_specs=[VMEM] * len(inputs)...  3.6 us
    ppermute x1, starting transfers between devices, shards(): far = lax.ppermute(far, 'tile', ring + [(j, i) for i, j in ring])  3.54 us
    pallas_call x1, Pallas kernels, shards(): pl.pallas_call(edge_kernel, out_shape=[rim, rim, jax.ShapeDtypeStruct((n_...  1.06 us
  transfers between devices with their start and end apart: 9, of which 7 were waited for; matrix products, arithmetic and copies ran while one was open for 0% of the time, Pallas kernels for 6%

profile of v11, /device:TPU:0, one launch (start us, length us, event | category | flops | bytes accessed | tf_op | source)
XLA Modules:
  0.0 27.4 jit_solution(14108533045047620280)
XLA Ops:
  0.6 0.0 copy-start
  0.6 0.0 copy-start.1
  0.7 1.1 %shard_map.99 = (f32[3,4,1024]{2,1,0:T(4,128)S(1)}, f32[3,4,1024]{2,1,0:T(4,128)S(1)}, f32[8,8,128]{2,1,0:T(8,128)S(1)}, s32[4,8,128]{2,1,0:T(8,128)S(1)}) custom-call(f32[2,32,1024]{2,1,0:T(8,128)} %bitcast.24, s32[32,1024]{1,0:T(8,128)} %class_ref.1, f32[8]{0:T(128)} %cond_hbm.1, s32[2]{0:T(128)} %row_hbm.1, s32[2]{0:T(128)} %col_hbm.1), custom_call_target="tpu_custom_call" | custom-call | tf_op jit(solution)/shard_map/pallas_call | solution.py:593
  1.7 0.0 copy-start.2
  1.7 0.6 %collective-permute-start.14 = (f32[3,4,1024]{2,1,0:T(4,128)S(1)}, f32[3,4,1024]{2,1,0:T(4,128)S(1)}, u32[]{:S(2)}, u32[]{:S(2)}) collective-permute-start(f32[3,4,1024]{2,1,0:T(4,128)S(1)} %get-tuple-element.66), channel_id=1, source_target_pairs={{0,1},{1,0},{2,3},{3,2},{4,5},{5,4},{6,7},{7,6},{8,9},{9,8},{10,11... | collective-permute-start | bytes 147464 | tf_op jit(solution)/shard_map/ppermute | solution.py:35
  2.3 3.5 %collective-permute-start.13 = (f32[3,4,1024]{2,1,0:T(4,128)S(1)}, f32[3,4,1024]{2,1,0:T(4,128)S(1)}, u32[]{:S(2)}, u32[]{:S(2)}) collective-permute-start(f32[3,4,1024]{2,1,0:T(4,128)S(1)} %get-tuple-element.59), channel_id=1, source_target_pairs={{1,2},{3,4},{5,6},{7,0},{2,1},{4,3},{6,5},{0,7},{9,10},{11,12},{13... | collective-permute-start | bytes 147464 | tf_op jit(solution)/shard_map/ppermute | solution.py:612
  5.8 0.0 copy-done.2
  6.5 0.0 copy-done
  6.5 0.0 copy-done.1
  6.5 1.1 %shard_map.100 = (f32[2,8,40,128]{3,2,1,0:T(8,128)S(1)}, f32[2,8,40,128]{3,2,1,0:T(8,128)S(1)}, f32[2,8,40,128]{3,2,1,0:T(8,128)S(1)}, f32[2,8,40,128]{3,2,1,0:T...) custom-call(f32[2,32,1024]{2,1,0:T(8,128)S(1)} %bitcast.25, ...), custom_call_target="tpu_custom_call" | custom-call | tf_op jit(solution)/shard_map/pallas_call | solution.py:104
  7.6 0.0 collective-permute-done.14.came_ref
  7.6 0.5 %shard_map.101 = (f32[2,2,8,8,128]{4,3,2,1,0:T(8,128)S(1)}, f32[2,2,8,8,128]{4,3,2,1,0:T(8,128)S(1)}, f32[2,2,8,8,128]{4,3,2,1,0:T(8,128)S(1)}, f32[2,2,8,8,128]{4,3,2,1,0:T(8,128)S(1)}, f32[24,128]{1,0:T(8,128)S(1)}) custom-call(f32[3,4,1024]{2,1,0:T(4,128)S(1)} %collective-permute-done.14.came_ref, f32[8,8,128]{2,1,0:T(8,128)S(1)} %get-tuple-element.60.par_ref, ...), custom_call_target="tpu_custom_call" | custom-call | tf_op jit(solution)/shard_map/pallas_call | solution.py:104
  8.1 0.0 collective-permute-done.13.came_ref
  8.1 0.5 %shard_map.102 = (f32[2,2,8,8,128]{4,3,2,1,0:T(8,128)S(1)}, f32[2,2,8,8,128]{4,3,2,1,0:T(8,128)S(1)}, f32[2,2,8,8,128]{4,3,2,1,0:T(8,128)S(1)}, f32[2,2,8,8,128]{4,3,2,1,0:T(8,128)S(1)}, f32[24,128]{1,0:T(8,128)S(1)}) custom-call(f32[3,4,1024]{2,1,0:T(4,128)S(1)} %collective-permute-done., ...), custom_call_target="tpu_custom_call", output_to_operand_aliasing={{0}: (14, {}), {1}: (15, {}), {2}: (16, {}), {3}: (17, {})} | custom-call | tf_op jit(solution)/shard_map/pallas_call | solution.py:104
  8.6 0.1 collective-permute-start.15
  8.7 1.2 %collective-permute-done.15 = f32[24,128]{1,0:T(8,128)S(1)} collective-permute-done((f32[24,128]{1,0:T(8,128)S(1)}, f32[24,128]{1,0:T(8,128)S(1)}, u32[]{:S(2)}, u32[]{:S(2)}) %collective-permute-start.15) | collective-permute-done | bytes 12320 | tf_op jit(solution)/shard_map/ppermute | solution.py:35
  9.9 2.2 %collective-permute-start.16 = (f32[24,128]{1,0:T(8,128)S(1)}, f32[24,128]{1,0:T(8,128)S(1)}, u32[]{:S(2)}, u32[]{:S(2)}) collective-permute-start(f32[24,128]{1,0:T(8,128)S(1)} %add.97.refs_0_), channel_id=1, source_target_pairs={{0,6},{1,7},{2,4},{3,5},{4,2},{5,3},{6,0},{7,1},{8,14},{9,15},{10,... | collective-permute-start | bytes 36872 | tf_op jit(solution)/shard_map/ppermute | solution.py:35
  12.0 0.5 %collective-permute-start.17 = (f32[24,128]{1,0:T(8,128)S(1)}, f32[24,128]{1,0:T(8,128)S(1)}, u32[]{:S(2)}, u32[]{:S(2)}) collective-permute-start(f32[24,128]{1,0:T(8,128)S(1)} %add.97.refs_0_), channel_id=1, source_target_pairs={{0,4},{1,5},{2,6},{3,7},{4,0},{5,1},{6,2},{7,3},{8,12},{9,13},{10,... | collective-permute-start | bytes 36872 | tf_op jit(solution)/shard_map/ppermute | solution.py:35
  12.5 0.8 %collective-permute-start.18 = (f32[24,128]{1,0:T(8,128)S(1)}, f32[24,128]{1,0:T(8,128)S(1)}, u32[]{:S(2)}, u32[]{:S(2)}) collective-permute-start(f32[24,128]{1,0:T(8,128)S(1)} %add.97.refs_0_), channel_id=1, source_target_pairs={{0,2},{1,3},{2,0},{3,1},{4,6},{5,7},{6,4},{7,5},{8,10},{9,11},{10,... | collective-permute-start | bytes 36872 | tf_op jit(solution)/shard_map/ppermute | solution.py:35
  14.0 0.5 %collective-permute-done.16.refs_1_ = f32[24,128]{1,0:T(8,128)S(1)} collective-permute-done((f32[24,128]{1,0:T(8,128)S(1)}, f32[24,128]{1,0:T(8,128)S(1)}, u32[]{:S(2)}, u32[]{:S(2)}) %collective-permute-start.16) | collective-permute-done | bytes 12320 | tf_op jit(solution)/shard_map/ppermute | solution.py:35
  14.5 1.3 %collective-permute-done.17.refs_2_ = f32[24,128]{1,0:T(8,128)S(1)} collective-permute-done((f32[24,128]{1,0:T(8,128)S(1)}, f32[24,128]{1,0:T(8,128)S(1)}, u32[]{:S(2)}, u32[]{:S(2)}) %collective-permute-start.17) | collective-permute-done | bytes 12320 | tf_op jit(solution)/shard_map/ppermute | solution.py:35
  15.7 0.5 %collective-permute-done.18.refs_3_ = f32[24,128]{1,0:T(8,128)S(1)} collective-permute-done((f32[24,128]{1,0:T(8,128)S(1)}, f32[24,128]{1,0:T(8,128)S(1)}, u32[]{:S(2)}, u32[]{:S(2)}) %collective-permute-start.18) | collective-permute-done | bytes 12320 | tf_op jit(solution)/shard_map/ppermute | solution.py:35
  16.2 0.4 %shard_map.103 = (f32[136,128]{1,0:T(8,128)S(1)}, f32[136,128]{1,0:T(8,128)S(1)}, f32[136,128]{1,0:T(8,128)S(1)}, f32[136,128]{1,0:T(8,128)S(1)}) custom-call(f32[1,1]{1,0:T(1,128)} %bitcast.23.weight_ref, f32[24,128]{1,0:T(8,128)S(1)} %add.97.refs_0_, f32[24,128]{1,0:T(8,128)S(1)} %collective-permute-done.16.refs_1_, ...), custom_call_target="tpu_custom_call" | custom-call | tf_op jit(solution)/shard_map/pallas_call | solution.py:104
  16.6 3.7 %collective-permute-start.19 = (f32[136,128]{1,0:T(8,128)S(1)}, f32[136,128]{1,0:T(8,128)S(1)}, u32[]{:S(2)}, u32[]{:S(2)}) collective-permute-start(f32[136,128]{1,0:T(8,128)S(1)} %get-tuple-element.85), channel_id=1, source_target_pairs={{0,24},{8,16},{16,8},{24,0},{1,25},{9,17},{17,9},{25,1},{2,26},{10... | collective-permute-start | bytes 208904 | tf_op jit(solution)/shard_map/ppermute | solution.py:35
  20.3 0.0 collective-permute-start.20
  20.3 0.8 %collective-permute-start.21 = (f32[136,128]{1,0:T(8,128)S(1)}, f32[136,128]{1,0:T(8,128)S(1)}, u32[]{:S(2)}, u32[]{:S(2)}) collective-permute-start(f32[136,128]{1,0:T(8,128)S(1)} %get-tuple-element.87), channel_id=1, source_target_pairs={{0,16},{8,24},{16,0},{24,8},{1,17},{9,25},{17,1},{25,9},{2,18},{10... | collective-permute-start | bytes 208904 | tf_op jit(solution)/shard_map/ppermute | solution.py:35
  21.0 1.8 %collective-permute-done.19.refs_1_ = f32[136,128]{1,0:T(8,128)S(1)} collective-permute-done((f32[136,128]{1,0:T(8,128)S(1)}, f32[136,128]{1,0:T(8,128)S(1)}, u32[]{:S(2)}, u32[]{:S(2)}) %collective-permute-start.19) | collective-permute-done | bytes 69664 | tf_op jit(solution)/shard_map/ppermute | solution.py:35
  22.8 1.7 %collective-permute-done.20.refs_2_ = f32[136,128]{1,0:T(8,128)S(1)} collective-permute-done((f32[136,128]{1,0:T(8,128)S(1)}, f32[136,128]{1,0:T(8,128)S(1)}, u32[]{:S(2)}, u32[]{:S(2)}) %collective-permute-start.20) | collective-permute-done | bytes 69664 | tf_op jit(solution)/shard_map/ppermute | solution.py:35
  24.6 0.9 %collective-permute-done.21.refs_3_ = f32[136,128]{1,0:T(8,128)S(1)} collective-permute-done((f32[136,128]{1,0:T(8,128)S(1)}, f32[136,128]{1,0:T(8,128)S(1)}, u32[]{:S(2)}, u32[]{:S(2)}) %collective-permute-start.21) | collective-permute-done | bytes 69664 | tf_op jit(solution)/shard_map/ppermute | solution.py:35
  25.5 1.2 %shard_map.104 = (f32[2,32,256]{2,1,0:T(8,128)}, f32[2,64]{1,0:T(2,128)}, s32[1]{0:T(128)}) custom-call(f32[136,128]{1,0:T(8,128)S(1)} %get-tuple-element.84.refs_0_, f32[136,128]{1,0:T(8,128)S(1)} %collective-permute-done.19.refs_1_, f32[136,128]{1,0:T(8,128)S(1)} %collective-permute-done.20.refs_2_, f32[136,128]{1,0:T(8,128)S(1)} %collective-permute-done.21.refs_3_), custom_call_target="tpu_custom_call" | custom-call | tf_op jit(solution)/shard_map/pallas_call | solution.py:104
  (3 shorter events, 0.0 us)
Async XLA Ops:
  0.6 5.9 %copy-start = (f32[1,2,32,1024]{3,2,1,0:T(8,128)S(1)}, f32[1,2,32,1024]{3,2,1,0:T(8,128)}, u32[]{:S(2)}) copy-start(f32[1,2,32,1024]{3,2,1,0:T(8,128)} %param.10) | copy-start | bytes 786436
  0.6 5.9 %copy-start.1 = (s32[32,1024]{1,0:T(8,128)S(1)}, s32[32,1024]{1,0:T(8,128)}, u32[]{:S(2)}) copy-start(s32[32,1024]{1,0:T(8,128)} %class_ref.1) | copy-start | bytes 393220
  1.7 4.1 %copy-start.2 = (s32[64]{0:T(128)S(1)}, s32[64]{0:T(128)}, u32[]{:S(2)}) copy-start(s32[64]{0:T(128)} %param.17) | copy-start | bytes 772
  1.7 5.9 %collective-permute-start.14 = (f32[3,4,1024]{2,1,0:T(4,128)S(1)}, f32[3,4,1024]{2,1,0:T(4,128)S(1)}, u32[]{:S(2)}, u32[]{:S(2)}) collective-permute-start(f32[3,4,1024]{2,1,0:T(4,128)S(1)} %get-tuple-element.66), channel_id=1, source_target_pairs={{0,1},{1,0},{2,3},{3,2},{4,5},{5,4},{6,7},{7,6},{8,9},{9,8},{10,11... | collective-permute-start | bytes 147464 | tf_op jit(solution)/shard_map/ppermute | solution.py:35
  2.3 5.8 %collective-permute-start.13 = (f32[3,4,1024]{2,1,0:T(4,128)S(1)}, f32[3,4,1024]{2,1,0:T(4,128)S(1)}, u32[]{:S(2)}, u32[]{:S(2)}) collective-permute-start(f32[3,4,1024]{2,1,0:T(4,128)S(1)} %get-tuple-element.59), channel_id=1, source_target_pairs={{1,2},{3,4},{5,6},{7,0},{2,1},{4,3},{6,5},{0,7},{9,10},{11,12},{13... | collective-permute-start | bytes 147464 | tf_op jit(solution)/shard_map/ppermute | solution.py:612
  8.6 1.2 %collective-permute-start.15 = (f32[24,128]{1,0:T(8,128)S(1)}, f32[24,128]{1,0:T(8,128)S(1)}, u32[]{:S(2)}, u32[]{:S(2)}) collective-permute-start(f32[24,128]{1,0:T(8,128)S(1)} %get-tuple-element.79), channel_id=1, source_target_pairs={{0,1},{1,0},{2,3},{3,2},{4,5},{5,4},{6,7},{7,6},{8,9},{9,8},{10,11... | collective-permute-start | bytes 36872 | tf_op jit(solution)/shard_map/ppermute | solution.py:35
  9.9 4.6 %collective-permute-start.16 = (f32[24,128]{1,0:T(8,128)S(1)}, f32[24,128]{1,0:T(8,128)S(1)}, u32[]{:S(2)}, u32[]{:S(2)}) collective-permute-start(f32[24,128]{1,0:T(8,128)S(1)} %add.97.refs_0_), channel_id=1, source_target_pairs={{0,6},{1,7},{2,4},{3,5},{4,2},{5,3},{6,0},{7,1},{8,14},{9,15},{10,... | collective-permute-start | bytes 36872 | tf_op jit(solution)/shard_map/ppermute | solution.py:35
  12.0 3.7 %collective-permute-start.17 = (f32[24,128]{1,0:T(8,128)S(1)}, f32[24,128]{1,0:T(8,128)S(1)}, u32[]{:S(2)}, u32[]{:S(2)}) collective-permute-start(f32[24,128]{1,0:T(8,128)S(1)} %add.97.refs_0_), channel_id=1, source_target_pairs={{0,4},{1,5},{2,6},{3,7},{4,0},{5,1},{6,2},{7,3},{8,12},{9,13},{10,... | collective-permute-start | bytes 36872 | tf_op jit(solution)/shard_map/ppermute | solution.py:35
  12.5 3.7 %collective-permute-start.18 = (f32[24,128]{1,0:T(8,128)S(1)}, f32[24,128]{1,0:T(8,128)S(1)}, u32[]{:S(2)}, u32[]{:S(2)}) collective-permute-start(f32[24,128]{1,0:T(8,128)S(1)} %add.97.refs_0_), channel_id=1, source_target_pairs={{0,2},{1,3},{2,0},{3,1},{4,6},{5,7},{6,4},{7,5},{8,10},{9,11},{10,... | collective-permute-start | bytes 36872 | tf_op jit(solution)/shard_map/ppermute | solution.py:35
  16.6 6.2 %collective-permute-start.19 = (f32[136,128]{1,0:T(8,128)S(1)}, f32[136,128]{1,0:T(8,128)S(1)}, u32[]{:S(2)}, u32[]{:S(2)}) collective-permute-start(f32[136,128]{1,0:T(8,128)S(1)} %get-tuple-element.85), channel_id=1, source_target_pairs={{0,24},{8,16},{16,8},{24,0},{1,25},{9,17},{17,9},{25,1},{2,26},{10... | collective-permute-start | bytes 208904 | tf_op jit(solution)/shard_map/ppermute | solution.py:35
  20.3 4.3 %collective-permute-start.20 = (f32[136,128]{1,0:T(8,128)S(1)}, f32[136,128]{1,0:T(8,128)S(1)}, u32[]{:S(2)}, u32[]{:S(2)}) collective-permute-start(f32[136,128]{1,0:T(8,128)S(1)} %get-tuple-element.86), channel_id=1, source_target_pairs={{0,8},{8,0},{16,24},{24,16},{1,9},{9,1},{17,25},{25,17},{2,10},{10... | collective-permute-start | bytes 208904 | tf_op jit(solution)/shard_map/ppermute | solution.py:35
  20.3 5.2 %collective-permute-start.21 = (f32[136,128]{1,0:T(8,128)S(1)}, f32[136,128]{1,0:T(8,128)S(1)}, u32[]{:S(2)}, u32[]{:S(2)}) collective-permute-start(f32[136,128]{1,0:T(8,128)S(1)} %get-tuple-element.87), channel_id=1, source_target_pairs={{0,16},{8,24},{16,0},{24,8},{1,17},{9,25},{17,1},{25,9},{2,18},{10... | collective-permute-start | bytes 208904 | tf_op jit(solution)/shard_map/ppermute | solution.py:35
